TPU v7x, 256 devices: a whole 4x4x8 slice. The times are simulated.
256 devices in a mesh: row: 16 (over x_hi, y, core), col: 16 (over z, x_lo).
Axes of the slice: x: 4 (x_hi: 2, x_lo: 2; x = x_hi * 2 + x_lo), y: 4, z: 8, core: 2. Of those that a mesh axis runs over, the one named last changes fastest.
Arguments:
- vectors: float32 [96, 65536], P(None, ('col', 'row')), may hold values from -6 to 6
- blocks: float32 [16, 16, 176, 128, 128], P('row', 'col'), may hold values from -0.0546875 to 0.0546875
- block_row: int32 [16, 16, 176], P('row', 'col'), may hold values from 0 to 31
- block_col: int32 [16, 16, 176], P('row', 'col'), may hold values from 0 to 31
- block_count: int32 [16, 16], P('row', 'col'), may hold values from 22 to 176, as said below
- lower_bound: float32 [1], replicated, may hold values from -2.5 to -1.5
- upper_bound: float32 [1], replicated, may hold values from 1.5 to 2.5
Outputs:
- filtered: float32 [96, 65536], P(None, ('col', 'row'))
Inputs may be any that keep to these rules, and one draw needn't show every extreme that they name: `block_row`: local block row index within the device's band. `block_col`: local block column index within the device's band. `block_count`: in every row of the device grid one device has all 176 slots stored.
All inputs are finite; a program needn't handle non-finite values.
Results may differ from a plain program's by a relative error of at most 0.0003.
Values sent between devices are 32-bit elements; how exact they have to be, the bound alone decides.
No kernel may reach another device: no remote copies, remote signals or barrier semaphores. Data moves between devices by JAX's collectives and lax.ppermute only.
A program may use at most 128 MiB of HBM per device.

v0:
```python
import functools

import jax
import jax.numpy as jnp
from jax import lax
from jax.experimental import pallas as pl
from jax.experimental.pallas import tpu as pltpu
from jax.sharding import PartitionSpec as P


f32, bf16 = jnp.float32, jnp.bfloat16

NX, NY, NC, NZ, NL = 2, 4, 2, 8, 2


def row_perm(f):
    def at(x, y, c):
        return ((x % NX) * NY + y % NY) * NC + c % NC

    return [(at(x, y, c), at(*f(x, y, c))) for x in range(NX) for y in range(NY) for c in range(NC)]


def col_perm(f):
    def at(z, l):
        return (z % NZ) * NL + l % NL

    return [(at(z, l), at(*f(z, l))) for z in range(NZ) for l in range(NL)]


CORE = row_perm(lambda x, y, c: (x, y, c + 1))
Y_UP = row_perm(lambda x, y, c: (x, y + 1, c))
Y_DOWN = row_perm(lambda x, y, c: (x, y - 1, c))
Y_FAR = row_perm(lambda x, y, c: (x, y + 2, c))
X_HI = row_perm(lambda x, y, c: (x + 1, y, c))
Z_UP = col_perm(lambda z, l: (z + 1, l))
Z_DOWN = col_perm(lambda z, l: (z - 1, l))
X_LO = col_perm(lambda z, l: (z, l + 1))
FLIP = [(i * 16 + j, j * 16 + i) for i in range(16) for j in range(16)]


def send(x, axis, perm):
    return lax.ppermute(x, axis, perm)


def flip(x):
    return lax.ppermute(x, ("row", "col"), FLIP)


def cat(*xs):
    return jnp.concatenate(xs, axis=0)


def bar(*xs):
    return lax.optimization_barrier(xs)


FORWARD_OUT = (4, 4, 4, 4, 2, 2, 4, 4, 4)
BACKWARD_OUT = (4, 4, 4, 4, 16)
FORWARD_IN = ((0, 0, 16), (1, 0, 16))
BACKWARD_IN = (
    (0, 0, 4), (1, 0, 4), (2, 0, 4), (3, 0, 4), (4, 0, 2), (5, 0, 2), (6, 0, 4), (7, 0, 4), (8, 0, 4)
)


def split(x):
    high = x.astype(bf16)
    return high, (x - high.astype(f32)).astype(bf16)


def col_slot(cb, row):
    i = cb >> 1
    core = (i ^ row) & 1
    y = ((i >> 1) - (row >> 1)) & 3
    x = ((i >> 3) ^ (row >> 3)) & 1
    return (((core * 4 + y) * 2 + x) << 1) + (cb & 1)


def row_slot(rb, col):
    i = rb >> 1
    z = ((i >> 1) - (col >> 1)) & 7
    l = (i ^ col) & 1
    return ((z * 2 + l) << 1) + (rb & 1)


def product_kernel(backward, first, last, n_in, runs, out_sizes, *refs):
    rows, cols, count, here, blocks = refs[:5]
    parts, refs = refs[5 : 5 + n_in], refs[5 + n_in :]
    if not first:
        halves, total_in, refs = refs[0], refs[1], refs[2:]
    outs, refs = refs[: len(out_sizes)], refs[len(out_sizes) :]
    if first:
        halves, total, held, sems = refs
    else:
        total, held, sems = refs
    live = count[0, 0]
    bs = blocks.shape[-1]
    full = lax.div(live, UNROLL)
    middle = lax.div(full, 2)
    begin = 0 if first else middle
    end = full if last else middle

    def copy(c):
        where = pl.ds(c * UNROLL, UNROLL)
        return pltpu.make_async_copy(blocks.at[0, 0, where], held.at[where], sems.at[c])

    @pl.loop(begin, end)
    def _(c):
        copy(c).start()

    if last:

        @pl.when(full * UNROLL < live)
        def _():
            copy(full).start()

    if first:
        offset = 0
        for array, at, size in runs:

            @pl.loop(0, size)
            def _(k, part=parts[array], at=at, offset=offset):
                high, low = split(part[at + k])
                halves[offset + k, :, :bs] = high
                halves[offset + k, :, bs:] = low

            offset += size
        total[...] = jnp.zeros_like(total)
    else:
        total[...] = total_in[...]
    row, col = here[0], here[1]

    def one(s):
        rb, cb = row_slot(rows[0, 0, s], col), col_slot(cols[0, 0, s], row)
        high, low = split(held[s])
        zero = jnp.zeros_like(low)
        if backward:
            weights = jnp.concatenate(
                [jnp.concatenate([high, low], 1), jnp.concatenate([high, zero], 1)], 0
            )
            out = jnp.dot(halves[rb], weights, preferred_element_type=f32)
            total[cb] += out[:, :bs] + out[:, bs:]
        else:
            weights = jnp.concatenate(
                [jnp.concatenate([high, high], 1), jnp.concatenate([low, zero], 1)], 0
            )
            out = lax.dot_general(
                halves[cb], weights, (((1,), (1,)), ((), ())), preferred_element_type=f32
            )
            total[rb] += out[:, :bs] + out[:, bs:]

    @pl.loop(begin, end)
    def _(c):
        copy(c).wait()
        for k in range(UNROLL):
            one(c * UNROLL + k)

    if last:

        @pl.when(full * UNROLL < live)
        def _():
            copy(full).wait()

            @pl.loop(full * UNROLL, live)
            def _(s):
                one(s)

        offset = 0
        for out, size in zip(outs, out_sizes):
            out[...] = total[offset : offset + size]
            offset += size


UNROLL = 16


def products(backward, first, last, state, index):
    blocks = index[4]
    slots, bs = blocks.shape[2], blocks.shape[-1]
    vecs = state[0].shape[1]
    n_in = len(state) if first else 0
    runs = BACKWARD_IN if backward else FORWARD_IN
    out_sizes = () if not last else BACKWARD_OUT if backward else FORWARD_OUT
    smem = pl.BlockSpec(memory_space=pltpu.SMEM)
    vmem = pl.BlockSpec(memory_space=pltpu.VMEM)
    halves, total = (32, vecs, 2 * bs), (32, vecs, bs)
    out_shape = [jax.ShapeDtypeStruct((n, vecs, bs), f32) for n in out_sizes]
    scratch = []
    if first and not last:
        out_shape += [jax.ShapeDtypeStruct(halves, bf16), jax.ShapeDtypeStruct(total, f32)]
    elif first:
        scratch = [pltpu.VMEM(halves, bf16), pltpu.VMEM(total, f32)]
    else:
        scratch = [pltpu.VMEM(total, f32)]
    scratch += [
        pltpu.VMEM((slots, bs, bs), f32),
        pltpu.SemaphoreType.DMA((slots // UNROLL,)),
    ]
    share = 1 if first and last else 2
    return pl.pallas_call(
        functools.partial(product_kernel, backward, first, last, n_in, runs, out_sizes),
        in_specs=[smem] * 4 + [pl.BlockSpec(memory_space=pltpu.HBM)] + [vmem] * len(state),
        out_specs=[vmem] * len(out_shape),
        out_shape=out_shape,
        scratch_shapes=scratch,
        compiler_params=pltpu.CompilerParams(vmem_limit_bytes=48 << 20),
        cost_estimate=pl.CostEstimate(
            flops=24 * slots * vecs * bs * bs // share,
            bytes_accessed=4 * slots * bs * bs // share,
            transcendentals=0,
        ),
    )(*index, *state)


def body(vectors, blocks, block_row, block_col, block_count, lower_bound, upper_bound):
    vecs, bs = vectors.shape[0], blocks.shape[-1]
    here = jnp.stack([lax.axis_index("row"), lax.axis_index("col")]).astype(jnp.int32)
    center = (upper_bound[0] + lower_bound[0]) / 2.0
    half_width = (upper_bound[0] - lower_bound[0]) / 2.0
    index = (block_row, block_col, block_count, here, blocks)

    def apply_hamiltonian(a0, flipping, finish):
        a1 = send(a0, "row", X_HI)
        _, flipping = bar(a1, flipping)
        p0 = cat(a0, a1)
        p1 = send(p0, "row", Y_DOWN)
        p2 = send(p0, "row", Y_FAR)
        p3 = send(p0, "row", Y_UP)
        t0 = finish(flipping)
        t1 = send(t0, "col", X_LO)
        p1, p2, p3, t0, t1 = bar(p1, p2, p3, t0, t1)
        z0 = cat(t0, t1)
        up1 = send(z0, "col", Z_DOWN)
        down1 = send(z0, "col", Z_UP)
        p = cat(p0, p1, p2, p3)
        state = products(False, True, False, (p, send(p, "row", CORE)), index)
        up1, down1, *state = bar(up1, down1, *state)
        up2 = send(up1, "col", Z_DOWN)
        down2 = send(down1, "col", Z_UP)
        forward = products(False, False, True, state, index)
        up2, down2, *forward = bar(up2, down2, *forward)
        f0, f1, f2, f3, f4a, f4b, f5, f6, f7 = forward
        up3 = send(cat(up2, f4b), "col", Z_DOWN)
        down3 = send(cat(down2, f4a), "col", Z_UP)
        up3, down3 = bar(up3, down3)
        up4 = send(cat(up3[2:4], f5[:2], f5[2:] + up3[4:]), "col", Z_DOWN)
        down4 = send(cat(down3[:2], f3[:2] + down3[4:], f3[2:]), "col", Z_UP)
        up4, down4 = bar(up4, down4)
        u = send(f2 + down4[2:], "col", Z_UP)
        d = send(f6 + up4[2:], "col", Z_DOWN)
        state = (z0, up1, up2, up3, down4, up4, down3, down2, down1)
        backward = products(True, True, True, state, index)
        u, d, *backward = bar(u, d, *backward)
        g0, g1, g2, g3, other = backward
        u = send(f1 + u, "col", Z_UP)
        d = send(f7 + d, "col", Z_DOWN)
        o = send(other, "row", CORE)
        u, d, o = bar(u, d, o)
        h = send(f0[2:] + u[2:] + d[2:], "col", X_LO)
        q1 = send(g1 + o[4:8], "row", Y_UP)
        q2 = send(g2 + o[8:12], "row", Y_FAR)
        q3 = send(g3 + o[12:], "row", Y_DOWN)
        (flipped,) = bar(f0[:2] + u[:2] + d[:2] + h)
        flipped_back = flip(flipped)
        last = send(g0[2:] + o[2:4] + q1[2:] + q2[2:] + q3[2:], "row", X_HI)
        (own,) = bar(g0[:2] + o[:2] + q1[:2] + q2[:2] + q3[:2] + last)
        return own, flipped, flipped_back, t0

    y0 = vectors.reshape(vecs, -1, bs).transpose(1, 0, 2)

    def step(k, carry):
        before, now, flipping, scale, base = carry
        own, flipped, back, now_flipped = apply_hamiltonian(
            now, flip(flipping), lambda x: x * scale + base
        )
        later = (own + back - center * now) / half_width
        later = jnp.where(k == 0, later, 2.0 * later - before)
        base = (flipped - center * now_flipped) / half_width
        return now, later, own, 1.0 / half_width, base

    start = (y0, y0, y0, jnp.ones((), f32), jnp.zeros_like(y0))
    y2 = lax.fori_loop(0, 2, step, start)[1]
    return y2.transpose(1, 0, 2).reshape(vectors.shape)


def solution(mesh):
    placed = (
        P(None, ("col", "row")),
        P("row", "col", None, None, None),
        P("row", "col", None),
        P("row", "col", None),
        P("row", "col"),
        P(),
        P(),
    )
    return jax.shard_map(
        body, mesh=mesh, in_specs=placed, out_specs=P(None, ("col", "row")), check_vma=False
    )
```

profile of v0, /device:TPU:5, one launch (start us, length us, event | category | flops | bytes accessed | tf_op | source)
XLA Modules:
  0.0 226.6 jit_solution(11677328562684259490)
XLA Ops:
  1.3 0.9 reshape.12
  2.4 223.5 %while.23 = (s32[]{:T(128)}, f32[2,96,128]{2,1,0:T(8,128)S(1)}, f32[2,96,128]{2,1,0:T(8,128)S(1)}, f32[2,96,128]{2,1,0:T(8,128)S(1)}, f32[]{:T(128)}, /*index=5*...) while((s32[]{:T(128)}, f32[2,96,128]{2,1,0:T(8,128)S(1)}, ...), condition=%wide.region_1.2_spmd.clone, body=%wide.region_0.1_spmd.clone.sunk | while | flops 13289054208 | bytes 61119232 | solution.py:281
  2.5 11.4 %collective-permute-start.4 = (f32[2,96,128]{2,1,0:T(8,128)S(1)}, f32[2,96,128]{2,1,0:T(8,128)S(1)}, u32[]{:S(2)}, u32[]{:S(2)}) collective-permute-start(f32[2,96,128]{2,1,0:T(8,128)S(1)} %get-tuple-element.704), channel_id=1, source_target_pairs={{0,0},{1,16},{2,32},{3,48},{4,64},{5,80},{6,96},{7,112},{8,128},{9... | collective-permute-start | bytes 294920 | tf_op jit(solution)/shard_map/while/body/eval_jaxpr/ppermute | solution.py:46
  14.1 1.1 collective-permute-start.1
  15.2 1.5 collective-permute-start.2
  16.8 2.2 collective-permute-start.5
  19.0 2.3 %collective-permute-done.5 = f32[2,96,128]{2,1,0:T(8,128)S(1)} collective-permute-done((f32[2,96,128]{2,1,0:T(8,128)S(1)}, f32[2,96,128]{2,1,0:T(8,128)S(1)}, u32[]{:S(2)}, u32[]{:S(2)}) %collective-permute-start.5) | collective-permute-done | bytes 98336 | tf_op jit(solution)/shard_map/while/body/eval_jaxpr/ppermute | solution.py:42
  21.3 3.1 %collective-permute-done.2 = f32[4,96,128]{2,1,0:T(8,128)S(1)} collective-permute-done((f32[4,96,128]{2,1,0:T(8,128)S(1)}, f32[4,96,128]{2,1,0:T(8,128)S(1)}, u32[]{:S(2)}, u32[]{:S(2)}) %collective-permute-start.2) | collective-permute-done | bytes 196640 | tf_op jit(solution)/shard_map/while/body/eval_jaxpr/ppermute | solution.py:42
  24.5 4.2 %collective-permute-done.3 = f32[4,96,128]{2,1,0:T(8,128)S(1)} collective-permute-done((f32[4,96,128]{2,1,0:T(8,128)S(1)}, f32[4,96,128]{2,1,0:T(8,128)S(1)}, u32[]{:S(2)}, u32[]{:S(2)}) %collective-permute-start.3) | collective-permute-done | bytes 196640 | tf_op jit(solution)/shard_map/while/body/eval_jaxpr/ppermute | solution.py:42
  30.2 1.0 collective-permute-start.7
  31.5 3.3 %eval_jaxpr.18 = (bf16[32,96,256]{2,1,0:T(8,128)(2,1)S(1)}, f32[32,96,128]{2,1,0:T(8,128)S(1)}) custom-call(s32[1,1,176]{2,1,0:T(1,128)S(1)} %copy-done, s32[1,1,176]{2,1,0:T(1,128)S(1)} %copy-done.1, s32[1,1]{1,0:T(1,128)} %get-tuple-element.725.refs_2_, s32[2]{0:T(128)S(1)} %get-tuple-element.726.refs_3_, ...), custom_call_target="tpu_custom_call" | custom-call | flops 3321888768 | bytes 5767168 | tf_op jit(solution)/shard_map/while/body/eval_jaxpr/pallas_call | solution.py:199
  34.9 1.3 collective-permute-done.6.refs_6_
  36.1 1.4 collective-permute-done.7.refs_13_
  38.2 1.9 collective-permute-start.9
  40.2 6.2 %eval_jaxpr.19 = (f32[4,96,128]{2,1,0:T(8,128)S(1)}, f32[4,96,128]{2,1,0:T(8,128)S(1)}, f32[4,96,128]{2,1,0:T(8,128)S(1)}, f32[4,96,128]{2,1,0:T(8,128)S(1)}, f3...) custom-call(s32[1,1,176]{2,1,0:T(1,128)S(1)} %copy-done, ...), custom_call_target="tpu_custom_call" | custom-call | flops 3321888768 | bytes 5767168 | tf_op jit(solution)/shard_map/while/body/eval_jaxpr/pallas_call | solution.py:199
  46.4 1.5 collective-permute-start.12
  47.9 1.3 collective-permute-start.11
  49.3 5.6 %collective-permute-done.12.refs_11_ = f32[6,96,128]{2,1,0:T(8,128)S(1)} collective-permute-done((f32[6,96,128]{2,1,0:T(8,128)S(1)}, f32[6,96,128]{2,1,0:T(8,128)S(1)}, u32[]{:S(2)}, u32[]{:S(2)}) %collective-permute-start.12) | collective-permute-done | bytes 294944 | tf_op jit(solution)/shard_map/while/body/eval_jaxpr/ppermute | solution.py:42
  54.9 2.9 %collective-permute-done.11.refs_8_ = f32[6,96,128]{2,1,0:T(8,128)S(1)} collective-permute-done((f32[6,96,128]{2,1,0:T(8,128)S(1)}, f32[6,96,128]{2,1,0:T(8,128)S(1)}, u32[]{:S(2)}, u32[]{:S(2)}) %collective-permute-start.11) | collective-permute-done | bytes 294944 | tf_op jit(solution)/shard_map/while/body/eval_jaxpr/ppermute | solution.py:42
  57.9 1.0 collective-permute-start.14
  58.9 1.8 collective-permute-start.13
  60.8 6.4 %collective-permute-done.14.refs_9_ = f32[6,96,128]{2,1,0:T(8,128)S(1)} collective-permute-done((f32[6,96,128]{2,1,0:T(8,128)S(1)}, f32[6,96,128]{2,1,0:T(8,128)S(1)}, u32[]{:S(2)}, u32[]{:S(2)}) %collective-permute-start.14) | collective-permute-done | bytes 294944 | tf_op jit(solution)/shard_map/while/body/eval_jaxpr/ppermute | solution.py:42
  67.2 2.6 %collective-permute-start.16 = (f32[4,96,128]{2,1,0:T(8,128)S(1)}, f32[4,96,128]{2,1,0:T(8,128)S(1)}, u32[]{:S(2)}, u32[]{:S(2)}) collective-permute-start(f32[4,96,128]{2,1,0:T(8,128)S(1)} %slice_add_fusion.20), channel_id=1, source_target_pairs={{0,14},{1,15},{2,0},{3,1},{4,2},{5,3},{6,4},{7,5},{8,6},{9,7},{10,... | collective-permute-start | bytes 589832 | tf_op jit(solution)/shard_map/while/body/eval_jaxpr/ppermute | solution.py:42
  69.9 5.7 %eval_jaxpr.20 = (f32[4,96,128]{2,1,0:T(8,128)S(1)}, f32[4,96,128]{2,1,0:T(8,128)S(1)}, f32[4,96,128]{2,1,0:T(8,128)S(1)}, f32[4,96,128]{2,1,0:T(8,128)S(1)}, f32[16,96,128]{2,1,0:T(8,128)S(1)}) custom-call(s32[1,1,176]{2,1,0:T(1,128)S(1)} %copy-done, s32[1,1,176]{2,1,0:T(1,128)S(1)} %copy-done.1, s32[1,1]{1,0:T(1,128)} %get-tuple-element.725.refs_2_, ...), custom_call_target="tpu_custom_call" | custom-call | flops 6643777536 | bytes 11534336 | tf_op jit(solution)/shard_map/while/body/eval_jaxpr/pallas_call | solution.py:199
  75.7 3.1 %collective-permute-start.19 = (f32[16,96,128]{2,1,0:T(8,128)S(1)}, f32[16,96,128]{2,1,0:T(8,128)S(1)}, u32[]{:S(2)}, u32[]{:S(2)}) collective-permute-start(f32[16,96,128]{2,1,0:T(8,128)S(1)} %get-tuple-element.674), channel_id=1, source_target_pairs={{0,16},{16,0},{32,48},{48,32},{64,80},{80,64},{96,112},{112,96},{1... | collective-permute-start | bytes 2359304 | tf_op jit(solution)/shard_map/while/body/eval_jaxpr/ppermute | solution.py:42
  78.8 1.8 collective-permute-start.18
  80.7 4.6 %collective-permute-done.18 = f32[4,96,128]{2,1,0:T(8,128)S(1)} collective-permute-done((f32[4,96,128]{2,1,0:T(8,128)S(1)}, f32[4,96,128]{2,1,0:T(8,128)S(1)}, u32[]{:S(2)}, u32[]{:S(2)}) %collective-permute-start.18) | collective-permute-done | bytes 196640 | tf_op jit(solution)/shard_map/while/body/eval_jaxpr/ppermute | solution.py:42
  85.3 2.9 %collective-permute-done.17 = f32[4,96,128]{2,1,0:T(8,128)} collective-permute-done((f32[4,96,128]{2,1,0:T(8,128)S(1)}, f32[4,96,128]{2,1,0:T(8,128)}, u32[]{:S(2)}, u32[]{:S(2)}) %collective-permute-start.17) | collective-permute-done | bytes 196640 | tf_op jit(solution)/shard_map/while/body/eval_jaxpr/ppermute | solution.py:42
  88.2 0.9 slice_add_fusion.23
  89.1 1.6 collective-permute-start.24
  90.8 2.7 %collective-permute-start.20 = (f32[4,96,128]{2,1,0:T(8,128)S(1)}, f32[4,96,128]{2,1,0:T(8,128)S(1)}, u32[]{:S(2)}, u32[]{:S(2)}) collective-permute-start(f32[4,96,128]{2,1,0:T(8,128)S(1)} %get-tuple-element.678), channel_id=1, source_target_pairs={{0,96},{16,112},{32,0},{48,16},{64,32},{80,48},{96,64},{112,80},{1... | collective-permute-start | bytes 589832 | tf_op jit(solution)/shard_map/while/body/eval_jaxpr/ppermute | solution.py:42
  94.2 0.9 add_add_fusion.2
  95.1 7.6 %collective-permute-start.25 = (f32[2,96,128]{2,1,0:T(8,128)S(1)}, f32[2,96,128]{2,1,0:T(8,128)S(1)}, u32[]{:S(2)}, u32[]{:S(2)}) collective-permute-start(f32[2,96,128]{2,1,0:T(8,128)S(1)} %add_add_fusion.2), channel_id=1, source_target_pairs={{0,0},{1,16},{2,32},{3,48},{4,64},{5,80},{6,96},{7,112},{8,128},{9... | collective-permute-start | bytes 294920 | tf_op jit(solution)/shard_map/while/body/eval_jaxpr/ppermute | solution.py:46
  102.7 2.7 %collective-permute-done.22 = f32[4,96,128]{2,1,0:T(8,128)S(1)} collective-permute-done((f32[4,96,128]{2,1,0:T(8,128)S(1)}, f32[4,96,128]{2,1,0:T(8,128)S(1)}, u32[]{:S(2)}, u32[]{:S(2)}) %collective-permute-start.22) | collective-permute-done | bytes 196640 | tf_op jit(solution)/shard_map/while/body/eval_jaxpr/ppermute | solution.py:42
  105.5 3.0 %collective-permute-start.23 = (f32[2,96,128]{2,1,0:T(8,128)S(1)}, f32[2,96,128]{2,1,0:T(8,128)S(1)}, u32[]{:S(2)}, u32[]{:S(2)}) collective-permute-start(f32[2,96,128]{2,1,0:T(8,128)S(1)} %slice_add_fusion.22), channel_id=1, source_target_pairs={{0,128},{16,144},{32,160},{48,176},{64,192},{80,208},{96,224},{112... | collective-permute-start | bytes 294920 | tf_op jit(solution)/shard_map/while/body/eval_jaxpr/ppermute | solution.py:42
  109.1 8.5 %collective-permute-done.23 = f32[2,96,128]{2,1,0:T(8,128)S(1)} collective-permute-done((f32[2,96,128]{2,1,0:T(8,128)S(1)}, f32[2,96,128]{2,1,0:T(8,128)S(1)}, u32[]{:S(2)}, u32[]{:S(2)}) %collective-permute-start.23) | collective-permute-done | bytes 98336 | tf_op jit(solution)/shard_map/while/body/eval_jaxpr/ppermute | solution.py:42
  117.9 3.6 %collective-permute-start.4 = (f32[2,96,128]{2,1,0:T(8,128)S(1)}, f32[2,96,128]{2,1,0:T(8,128)S(1)}, u32[]{:S(2)}, u32[]{:S(2)}) collective-permute-start(f32[2,96,128]{2,1,0:T(8,128)S(1)} %get-tuple-element.704), channel_id=1, source_target_pairs={{0,0},{1,16},{2,32},{3,48},{4,64},{5,80},{6,96},{7,112},{8,128},{9... | collective-permute-start | bytes 294920 | tf_op jit(solution)/shard_map/while/body/eval_jaxpr/ppermute | solution.py:46
  121.6 1.9 collective-permute-done
  123.7 1.4 collective-permute-start.3
  125.0 4.0 %collective-permute-done.4 = f32[2,96,128]{2,1,0:T(8,128)S(1)} collective-permute-done((f32[2,96,128]{2,1,0:T(8,128)S(1)}, f32[2,96,128]{2,1,0:T(8,128)S(1)}, u32[]{:S(2)}, u32[]{:S(2)}) %collective-permute-start.4) | collective-permute-done | bytes 98336 | tf_op jit(solution)/shard_map/while/body/eval_jaxpr/ppermute | solution.py:46
  130.6 3.1 %collective-permute-done.5 = f32[2,96,128]{2,1,0:T(8,128)S(1)} collective-permute-done((f32[2,96,128]{2,1,0:T(8,128)S(1)}, f32[2,96,128]{2,1,0:T(8,128)S(1)}, u32[]{:S(2)}, u32[]{:S(2)}) %collective-permute-start.5) | collective-permute-done | bytes 98336 | tf_op jit(solution)/shard_map/while/body/eval_jaxpr/ppermute | solution.py:42
  133.8 4.4 %collective-permute-start.8 = (f32[16,96,128]{2,1,0:T(8,128)S(1)}, f32[16,96,128]{2,1,0:T(8,128)S(1)}, u32[]{:S(2)}, u32[]{:S(2)}) collective-permute-start(f32[16,96,128]{2,1,0:T(8,128)S(1)} %constant_dynamic-update-slice_fusion.22.refs_5_), channel_id=1, source_target_pairs={{0,16},{16,0},{32,48},{48,32},{64,80},{80,64},{96,112},{112,96},{1... | collective-permute-start | bytes 2359304 | tf_op jit(solution)/shard_map/while/body/eval_jaxpr/ppermute | solution.py:42
  138.3 2.1 collective-permute-start.6
  140.4 3.3 %eval_jaxpr.18 = (bf16[32,96,256]{2,1,0:T(8,128)(2,1)S(1)}, f32[32,96,128]{2,1,0:T(8,128)S(1)}) custom-call(s32[1,1,176]{2,1,0:T(1,128)S(1)} %copy-done, s32[1,1,176]{2,1,0:T(1,128)S(1)} %copy-done.1, s32[1,1]{1,0:T(1,128)} %get-tuple-element.725.refs_2_, s32[2]{0:T(128)S(1)} %get-tuple-element.726.refs_3_, ...), custom_call_target="tpu_custom_call" | custom-call | flops 3321888768 | bytes 5767168 | tf_op jit(solution)/shard_map/while/body/eval_jaxpr/pallas_call | solution.py:199
  143.8 1.0 collective-permute-done.6.refs_6_
  144.8 3.0 %collective-permute-done.7.refs_13_ = f32[4,96,128]{2,1,0:T(8,128)S(1)} collective-permute-done((f32[4,96,128]{2,1,0:T(8,128)S(1)}, f32[4,96,128]{2,1,0:T(8,128)S(1)}, u32[]{:S(2)}, u32[]{:S(2)}) %collective-permute-start.7) | collective-permute-done | bytes 196640 | tf_op jit(solution)/shard_map/while/body/eval_jaxpr/ppermute | solution.py:42
  147.8 2.7 %collective-permute-start.9 = (f32[4,96,128]{2,1,0:T(8,128)S(1)}, f32[4,96,128]{2,1,0:T(8,128)S(1)}, u32[]{:S(2)}, u32[]{:S(2)}) collective-permute-start(f32[4,96,128]{2,1,0:T(8,128)S(1)} %collective-permute-done.6.refs_6_), channel_id=1, source_target_pairs={{0,14},{1,15},{2,0},{3,1},{4,2},{5,3},{6,4},{7,5},{8,6},{9,7},{10,... | collective-permute-start | bytes 589832 | tf_op jit(solution)/shard_map/while/body/eval_jaxpr/ppermute | solution.py:42
  150.4 6.2 %eval_jaxpr.19 = (f32[4,96,128]{2,1,0:T(8,128)S(1)}, f32[4,96,128]{2,1,0:T(8,128)S(1)}, f32[4,96,128]{2,1,0:T(8,128)S(1)}, f32[4,96,128]{2,1,0:T(8,128)S(1)}, f3...) custom-call(s32[1,1,176]{2,1,0:T(1,128)S(1)} %copy-done, ...), custom_call_target="tpu_custom_call" | custom-call | flops 3321888768 | bytes 5767168 | tf_op jit(solution)/shard_map/while/body/eval_jaxpr/pallas_call | solution.py:199
  156.8 2.7 %collective-permute-start.11 = (f32[6,96,128]{2,1,0:T(8,128)S(1)}, f32[6,96,128]{2,1,0:T(8,128)S(1)}, u32[]{:S(2)}, u32[]{:S(2)}) collective-permute-start(f32[6,96,128]{2,1,0:T(8,128)S(1)} %pad_maximum_fusion.8), channel_id=1, source_target_pairs={{0,14},{1,15},{2,0},{3,1},{4,2},{5,3},{6,4},{7,5},{8,6},{9,7},{10,... | collective-permute-start | bytes 884744 | tf_op jit(solution)/shard_map/while/body/eval_jaxpr/ppermute | solution.py:42
  159.5 5.7 %collective-permute-done.12.refs_11_ = f32[6,96,128]{2,1,0:T(8,128)S(1)} collective-permute-done((f32[6,96,128]{2,1,0:T(8,128)S(1)}, f32[6,96,128]{2,1,0:T(8,128)S(1)}, u32[]{:S(2)}, u32[]{:S(2)}) %collective-permute-start.12) | collective-permute-done | bytes 294944 | tf_op jit(solution)/shard_map/while/body/eval_jaxpr/ppermute | solution.py:42
  165.4 2.7 %collective-permute-start.13 = (f32[6,96,128]{2,1,0:T(8,128)S(1)}, f32[6,96,128]{2,1,0:T(8,128)S(1)}, u32[]{:S(2)}, u32[]{:S(2)}) collective-permute-start(f32[6,96,128]{2,1,0:T(8,128)S(1)} %pad_maximum_fusion.10), channel_id=1, source_target_pairs={{0,14},{1,15},{2,0},{3,1},{4,2},{5,3},{6,4},{7,5},{8,6},{9,7},{10,... | collective-permute-start | bytes 884744 | tf_op jit(solution)/shard_map/while/body/eval_jaxpr/ppermute | solution.py:42
  168.1 4.8 %collective-permute-done.14.refs_9_ = f32[6,96,128]{2,1,0:T(8,128)S(1)} collective-permute-done((f32[6,96,128]{2,1,0:T(8,128)S(1)}, f32[6,96,128]{2,1,0:T(8,128)S(1)}, u32[]{:S(2)}, u32[]{:S(2)}) %collective-permute-start.14) | collective-permute-done | bytes 294944 | tf_op jit(solution)/shard_map/while/body/eval_jaxpr/ppermute | solution.py:42
  173.0 2.6 %collective-permute-start.16 = (f32[4,96,128]{2,1,0:T(8,128)S(1)}, f32[4,96,128]{2,1,0:T(8,128)S(1)}, u32[]{:S(2)}, u32[]{:S(2)}) collective-permute-start(f32[4,96,128]{2,1,0:T(8,128)S(1)} %slice_add_fusion.20), channel_id=1, source_target_pairs={{0,14},{1,15},{2,0},{3,1},{4,2},{5,3},{6,4},{7,5},{8,6},{9,7},{10,... | collective-permute-start | bytes 589832 | tf_op jit(solution)/shard_map/while/body/eval_jaxpr/ppermute | solution.py:42
  175.7 5.8 %eval_jaxpr.20 = (f32[4,96,128]{2,1,0:T(8,128)S(1)}, f32[4,96,128]{2,1,0:T(8,128)S(1)}, f32[4,96,128]{2,1,0:T(8,128)S(1)}, f32[4,96,128]{2,1,0:T(8,128)S(1)}, f32[16,96,128]{2,1,0:T(8,128)S(1)}) custom-call(s32[1,1,176]{2,1,0:T(1,128)S(1)} %copy-done, s32[1,1,176]{2,1,0:T(1,128)S(1)} %copy-done.1, s32[1,1]{1,0:T(1,128)} %get-tuple-element.725.refs_2_, ...), custom_call_target="tpu_custom_call" | custom-call | flops 6643777536 | bytes 11534336 | tf_op jit(solution)/shard_map/while/body/eval_jaxpr/pallas_call | solution.py:199
  181.4 4.7 %collective-permute-start.19 = (f32[16,96,128]{2,1,0:T(8,128)S(1)}, f32[16,96,128]{2,1,0:T(8,128)S(1)}, u32[]{:S(2)}, u32[]{:S(2)}) collective-permute-start(f32[16,96,128]{2,1,0:T(8,128)S(1)} %get-tuple-element.674), channel_id=1, source_target_pairs={{0,16},{16,0},{32,48},{48,32},{64,80},{80,64},{96,112},{112,96},{1... | collective-permute-start | bytes 2359304 | tf_op jit(solution)/shard_map/while/body/eval_jaxpr/ppermute | solution.py:42
  186.2 1.8 collective-permute-start.18
  188.1 4.6 %collective-permute-done.18 = f32[4,96,128]{2,1,0:T(8,128)S(1)} collective-permute-done((f32[4,96,128]{2,1,0:T(8,128)S(1)}, f32[4,96,128]{2,1,0:T(8,128)S(1)}, u32[]{:S(2)}, u32[]{:S(2)}) %collective-permute-start.18) | collective-permute-done | bytes 196640 | tf_op jit(solution)/shard_map/while/body/eval_jaxpr/ppermute | solution.py:42
  192.7 2.9 %collective-permute-done.17 = f32[4,96,128]{2,1,0:T(8,128)} collective-permute-done((f32[4,96,128]{2,1,0:T(8,128)S(1)}, f32[4,96,128]{2,1,0:T(8,128)}, u32[]{:S(2)}, u32[]{:S(2)}) %collective-permute-start.17) | collective-permute-done | bytes 196640 | tf_op jit(solution)/shard_map/while/body/eval_jaxpr/ppermute | solution.py:42
  196.5 3.0 %collective-permute-start.24 = (f32[2,96,128]{2,1,0:T(8,128)S(1)}, f32[2,96,128]{2,1,0:T(8,128)S(1)}, u32[]{:S(2)}, u32[]{:S(2)}) collective-permute-start(f32[2,96,128]{2,1,0:T(8,128)S(1)} %slice_add_fusion.23), channel_id=1, source_target_pairs={{0,1},{1,0},{2,3},{3,2},{4,5},{5,4},{6,7},{7,6},{8,9},{9,8},{10,11... | collective-permute-start | bytes 294920 | tf_op jit(solution)/shard_map/while/body/eval_jaxpr/ppermute | solution.py:42
  199.6 3.0 %collective-permute-start.20 = (f32[4,96,128]{2,1,0:T(8,128)S(1)}, f32[4,96,128]{2,1,0:T(8,128)S(1)}, u32[]{:S(2)}, u32[]{:S(2)}) collective-permute-start(f32[4,96,128]{2,1,0:T(8,128)S(1)} %get-tuple-element.678), channel_id=1, source_target_pairs={{0,96},{16,112},{32,0},{48,16},{64,32},{80,48},{96,64},{112,80},{1... | collective-permute-start | bytes 589832 | tf_op jit(solution)/shard_map/while/body/eval_jaxpr/ppermute | solution.py:42
  203.3 0.9 add_add_fusion.2
  204.2 6.0 %collective-permute-start.25 = (f32[2,96,128]{2,1,0:T(8,128)S(1)}, f32[2,96,128]{2,1,0:T(8,128)S(1)}, u32[]{:S(2)}, u32[]{:S(2)}) collective-permute-start(f32[2,96,128]{2,1,0:T(8,128)S(1)} %add_add_fusion.2), channel_id=1, source_target_pairs={{0,0},{1,16},{2,32},{3,48},{4,64},{5,80},{6,96},{7,112},{8,128},{9... | collective-permute-start | bytes 294920 | tf_op jit(solution)/shard_map/while/body/eval_jaxpr/ppermute | solution.py:46
  210.2 4.4 %collective-permute-done.22 = f32[4,96,128]{2,1,0:T(8,128)S(1)} collective-permute-done((f32[4,96,128]{2,1,0:T(8,128)S(1)}, f32[4,96,128]{2,1,0:T(8,128)S(1)}, u32[]{:S(2)}, u32[]{:S(2)}) %collective-permute-start.22) | collective-permute-done | bytes 196640 | tf_op jit(solution)/shard_map/while/body/eval_jaxpr/ppermute | solution.py:42
  215.3 10.5 %collective-permute-done.23 = f32[2,96,128]{2,1,0:T(8,128)S(1)} collective-permute-done((f32[2,96,128]{2,1,0:T(8,128)S(1)}, f32[2,96,128]{2,1,0:T(8,128)S(1)}, u32[]{:S(2)}, u32[]{:S(2)}) %collective-permute-start.23) | collective-permute-done | bytes 98336 | tf_op jit(solution)/shard_map/while/body/eval_jaxpr/ppermute | solution.py:42
  (114 shorter events, 10.6 us)
Async XLA Ops:
  2.4 29.1 %copy-start = (s32[1,1,176]{2,1,0:T(1,128)S(1)}, s32[1,1,176]{2,1,0:T(1,128)}, u32[]{:S(2)}) copy-start(s32[1,1,176]{2,1,0:T(1,128)} %get-tuple-element.723.refs_0_) | copy-start | bytes 2116 | tf_op jit(solution)/shard_map/while
  2.4 29.1 %copy-start.1 = (s32[1,1,176]{2,1,0:T(1,128)S(1)}, s32[1,1,176]{2,1,0:T(1,128)}, u32[]{:S(2)}) copy-start(s32[1,1,176]{2,1,0:T(1,128)} %get-tuple-element.724.refs_1_) | copy-start | bytes 2116 | tf_op jit(solution)/shard_map/while
  2.4 11.6 %collective-permute-start = (f32[2,96,128]{2,1,0:T(8,128)S(1)}, f32[2,96,128]{2,1,0:T(8,128)S(1)}, u32[]{:S(2)}, u32[]{:S(2)}) collective-permute-start(f32[2,96,128]{2,1,0:T(8,128)S(1)} %copy.29), channel_id=1, source_target_pairs={{0,128},{16,144},{32,160},{48,176},{64,192},{80,208},{96,224},{112... | collective-permute-start | bytes 294920 | tf_op jit(solution)/shard_map/while/body/eval_jaxpr/ppermute | solution.py:42
  2.5 14.3 %collective-permute-start.4 = (f32[2,96,128]{2,1,0:T(8,128)S(1)}, f32[2,96,128]{2,1,0:T(8,128)S(1)}, u32[]{:S(2)}, u32[]{:S(2)}) collective-permute-start(f32[2,96,128]{2,1,0:T(8,128)S(1)} %get-tuple-element.704), channel_id=1, source_target_pairs={{0,0},{1,16},{2,32},{3,48},{4,64},{5,80},{6,96},{7,112},{8,128},{9... | collective-permute-start | bytes 294920 | tf_op jit(solution)/shard_map/while/body/eval_jaxpr/ppermute | solution.py:46
  14.1 7.3 %collective-permute-start.1 = (f32[4,96,128]{2,1,0:T(8,128)S(1)}, f32[4,96,128]{2,1,0:T(8,128)S(1)}, u32[]{:S(2)}, u32[]{:S(2)}) collective-permute-start(f32[4,96,128]{2,1,0:T(8,128)S(1)} %get-tuple-element.623), channel_id=1, source_target_pairs={{0,96},{16,112},{32,0},{48,16},{64,32},{80,48},{96,64},{112,80},{1... | collective-permute-start | bytes 589832 | tf_op jit(solution)/shard_map/while/body/eval_jaxpr/ppermute | solution.py:42
  15.2 9.3 %collective-permute-start.2 = (f32[4,96,128]{2,1,0:T(8,128)S(1)}, f32[4,96,128]{2,1,0:T(8,128)S(1)}, u32[]{:S(2)}, u32[]{:S(2)}) collective-permute-start(f32[4,96,128]{2,1,0:T(8,128)S(1)} %get-tuple-element.623), channel_id=1, source_target_pairs={{0,64},{16,80},{32,96},{48,112},{64,0},{80,16},{96,32},{112,48},{1... | collective-permute-start | bytes 589832 | tf_op jit(solution)/shard_map/while/body/eval_jaxpr/ppermute | solution.py:42
  16.7 12.0 %collective-permute-start.3 = (f32[4,96,128]{2,1,0:T(8,128)S(1)}, f32[4,96,128]{2,1,0:T(8,128)S(1)}, u32[]{:S(2)}, u32[]{:S(2)}) collective-permute-start(f32[4,96,128]{2,1,0:T(8,128)S(1)} %get-tuple-element.623), channel_id=1, source_target_pairs={{0,32},{16,48},{32,64},{48,80},{64,96},{80,112},{96,0},{112,16},{1... | collective-permute-start | bytes 589832 | tf_op jit(solution)/shard_map/while/body/eval_jaxpr/ppermute | solution.py:42
  16.8 4.5 %collective-permute-start.5 = (f32[2,96,128]{2,1,0:T(8,128)S(1)}, f32[2,96,128]{2,1,0:T(8,128)S(1)}, u32[]{:S(2)}, u32[]{:S(2)}) collective-permute-start(f32[2,96,128]{2,1,0:T(8,128)S(1)} %select_add_fusion.2), channel_id=1, source_target_pairs={{0,1},{1,0},{2,3},{3,2},{4,5},{5,4},{6,7},{7,6},{8,9},{9,8},{10,11... | collective-permute-start | bytes 294920 | tf_op jit(solution)/shard_map/while/body/eval_jaxpr/ppermute | solution.py:42
  28.7 2.8 %collective-permute-start.8 = (f32[16,96,128]{2,1,0:T(8,128)S(1)}, f32[16,96,128]{2,1,0:T(8,128)S(1)}, u32[]{:S(2)}, u32[]{:S(2)}) collective-permute-start(f32[16,96,128]{2,1,0:T(8,128)S(1)} %constant_dynamic-update-slice_fusion.22.refs_5_), channel_id=1, source_target_pairs={{0,16},{16,0},{32,48},{48,32},{64,80},{80,64},{96,112},{112,96},{1... | collective-permute-start | bytes 2359304 | tf_op jit(solution)/shard_map/while/body/eval_jaxpr/ppermute | solution.py:42
  29.6 6.5 %collective-permute-start.6 = (f32[4,96,128]{2,1,0:T(8,128)S(1)}, f32[4,96,128]{2,1,0:T(8,128)S(1)}, u32[]{:S(2)}, u32[]{:S(2)}) collective-permute-start(f32[4,96,128]{2,1,0:T(8,128)S(1)} %constant_dynamic-update-slice_fusion.19.refs_5_), channel_id=1, source_target_pairs={{0,14},{1,15},{2,0},{3,1},{4,2},{5,3},{6,4},{7,5},{8,6},{9,7},{10,... | collective-permute-start | bytes 589832 | tf_op jit(solution)/shard_map/while/body/eval_jaxpr/ppermute | solution.py:42
  30.2 7.3 %collective-permute-start.7 = (f32[4,96,128]{2,1,0:T(8,128)S(1)}, f32[4,96,128]{2,1,0:T(8,128)S(1)}, u32[]{:S(2)}, u32[]{:S(2)}) collective-permute-start(f32[4,96,128]{2,1,0:T(8,128)S(1)} %constant_dynamic-update-slice_fusion.19.refs_5_), channel_id=1, source_target_pairs={{0,2},{1,3},{2,4},{3,5},{4,6},{5,7},{6,8},{7,9},{8,10},{9,11},{10,... | collective-permute-start | bytes 589832 | tf_op jit(solution)/shard_map/while/body/eval_jaxpr/ppermute | solution.py:42
  37.5 8.9 %collective-permute-start.10 = (f32[4,96,128]{2,1,0:T(8,128)S(1)}, f32[4,96,128]{2,1,0:T(8,128)S(1)}, u32[]{:S(2)}, u32[]{:S(2)}) collective-permute-start(f32[4,96,128]{2,1,0:T(8,128)S(1)} %collective-permute-done.7.refs_13_), channel_id=1, source_target_pairs={{0,2},{1,3},{2,4},{3,5},{4,6},{5,7},{6,8},{7,9},{8,10},{9,11},{10,... | collective-permute-start | bytes 589832 | tf_op jit(solution)/shard_map/while/body/eval_jaxpr/ppermute | solution.py:42
  38.2 8.1 %collective-permute-start.9 = (f32[4,96,128]{2,1,0:T(8,128)S(1)}, f32[4,96,128]{2,1,0:T(8,128)S(1)}, u32[]{:S(2)}, u32[]{:S(2)}) collective-permute-start(f32[4,96,128]{2,1,0:T(8,128)S(1)} %collective-permute-done.6.refs_6_), channel_id=1, source_target_pairs={{0,14},{1,15},{2,0},{3,1},{4,2},{5,3},{6,4},{7,5},{8,6},{9,7},{10,... | collective-permute-start | bytes 589832 | tf_op jit(solution)/shard_map/while/body/eval_jaxpr/ppermute | solution.py:42
  46.4 8.5 %collective-permute-start.12 = (f32[6,96,128]{2,1,0:T(8,128)S(1)}, f32[6,96,128]{2,1,0:T(8,128)S(1)}, u32[]{:S(2)}, u32[]{:S(2)}) collective-permute-start(f32[6,96,128]{2,1,0:T(8,128)S(1)} %pad_maximum_fusion.9), channel_id=1, source_target_pairs={{0,2},{1,3},{2,4},{3,5},{4,6},{5,7},{6,8},{7,9},{8,10},{9,11},{10,... | collective-permute-start | bytes 884744 | tf_op jit(solution)/shard_map/while/body/eval_jaxpr/ppermute | solution.py:42
  47.9 9.9 %collective-permute-start.11 = (f32[6,96,128]{2,1,0:T(8,128)S(1)}, f32[6,96,128]{2,1,0:T(8,128)S(1)}, u32[]{:S(2)}, u32[]{:S(2)}) collective-permute-start(f32[6,96,128]{2,1,0:T(8,128)S(1)} %pad_maximum_fusion.8), channel_id=1, source_target_pairs={{0,14},{1,15},{2,0},{3,1},{4,2},{5,3},{6,4},{7,5},{8,6},{9,7},{10,... | collective-permute-start | bytes 884744 | tf_op jit(solution)/shard_map/while/body/eval_jaxpr/ppermute | solution.py:42
  57.9 9.3 %collective-permute-start.14 = (f32[6,96,128]{2,1,0:T(8,128)S(1)}, f32[6,96,128]{2,1,0:T(8,128)S(1)}, u32[]{:S(2)}, u32[]{:S(2)}) collective-permute-start(f32[6,96,128]{2,1,0:T(8,128)S(1)} %pad_maximum_fusion.11), channel_id=1, source_target_pairs={{0,2},{1,3},{2,4},{3,5},{4,6},{5,7},{6,8},{7,9},{8,10},{9,11},{10,... | collective-permute-start | bytes 884744 | tf_op jit(solution)/shard_map/while/body/eval_jaxpr/ppermute | solution.py:42
  58.9 8.2 %collective-permute-start.13 = (f32[6,96,128]{2,1,0:T(8,128)S(1)}, f32[6,96,128]{2,1,0:T(8,128)S(1)}, u32[]{:S(2)}, u32[]{:S(2)}) collective-permute-start(f32[6,96,128]{2,1,0:T(8,128)S(1)} %pad_maximum_fusion.10), channel_id=1, source_target_pairs={{0,14},{1,15},{2,0},{3,1},{4,2},{5,3},{6,4},{7,5},{8,6},{9,7},{10,... | collective-permute-start | bytes 884744 | tf_op jit(solution)/shard_map/while/body/eval_jaxpr/ppermute | solution.py:42
  67.2 8.4 %collective-permute-start.16 = (f32[4,96,128]{2,1,0:T(8,128)S(1)}, f32[4,96,128]{2,1,0:T(8,128)S(1)}, u32[]{:S(2)}, u32[]{:S(2)}) collective-permute-start(f32[4,96,128]{2,1,0:T(8,128)S(1)} %slice_add_fusion.20), channel_id=1, source_target_pairs={{0,14},{1,15},{2,0},{3,1},{4,2},{5,3},{6,4},{7,5},{8,6},{9,7},{10,... | collective-permute-start | bytes 589832 | tf_op jit(solution)/shard_map/while/body/eval_jaxpr/ppermute | solution.py:42
  69.8 5.9 %collective-permute-start.15 = (f32[4,96,128]{2,1,0:T(8,128)S(1)}, f32[4,96,128]{2,1,0:T(8,128)S(1)}, u32[]{:S(2)}, u32[]{:S(2)}) collective-permute-start(f32[4,96,128]{2,1,0:T(8,128)S(1)} %slice_add_fusion.19), channel_id=1, source_target_pairs={{0,2},{1,3},{2,4},{3,5},{4,6},{5,7},{6,8},{7,9},{8,10},{9,11},{10,... | collective-permute-start | bytes 589832 | tf_op jit(solution)/shard_map/while/body/eval_jaxpr/ppermute | solution.py:42
  75.7 12.5 %collective-permute-start.19 = (f32[16,96,128]{2,1,0:T(8,128)S(1)}, f32[16,96,128]{2,1,0:T(8,128)S(1)}, u32[]{:S(2)}, u32[]{:S(2)}) collective-permute-start(f32[16,96,128]{2,1,0:T(8,128)S(1)} %get-tuple-element.674), channel_id=1, source_target_pairs={{0,16},{16,0},{32,48},{48,32},{64,80},{80,64},{96,112},{112,96},{1... | collective-permute-start | bytes 2359304 | tf_op jit(solution)/shard_map/while/body/eval_jaxpr/ppermute | solution.py:42
  78.8 6.5 %collective-permute-start.18 = (f32[4,96,128]{2,1,0:T(8,128)S(1)}, f32[4,96,128]{2,1,0:T(8,128)S(1)}, u32[]{:S(2)}, u32[]{:S(2)}) collective-permute-start(f32[4,96,128]{2,1,0:T(8,128)S(1)} %add.327), channel_id=1, source_target_pairs={{0,14},{1,15},{2,0},{3,1},{4,2},{5,3},{6,4},{7,5},{8,6},{9,7},{10,... | collective-permute-start | bytes 589832 | tf_op jit(solution)/shard_map/while/body/eval_jaxpr/ppermute | solution.py:42
  80.6 7.6 %collective-permute-start.17 = (f32[4,96,128]{2,1,0:T(8,128)S(1)}, f32[4,96,128]{2,1,0:T(8,128)}, u32[]{:S(2)}, u32[]{:S(2)}) collective-permute-start(f32[4,96,128]{2,1,0:T(8,128)S(1)} %add.326), channel_id=1, source_target_pairs={{0,2},{1,3},{2,4},{3,5},{4,6},{5,7},{6,8},{7,9},{8,10},{9,11},{10,... | collective-permute-start | bytes 589832 | tf_op jit(solution)/shard_map/while/body/eval_jaxpr/ppermute | solution.py:42
  89.1 5.0 %collective-permute-start.24 = (f32[2,96,128]{2,1,0:T(8,128)S(1)}, f32[2,96,128]{2,1,0:T(8,128)S(1)}, u32[]{:S(2)}, u32[]{:S(2)}) collective-permute-start(f32[2,96,128]{2,1,0:T(8,128)S(1)} %slice_add_fusion.23), channel_id=1, source_target_pairs={{0,1},{1,0},{2,3},{3,2},{4,5},{5,4},{6,7},{7,6},{8,9},{9,8},{10,11... | collective-permute-start | bytes 294920 | tf_op jit(solution)/shard_map/while/body/eval_jaxpr/ppermute | solution.py:42
  90.8 11.9 %collective-permute-start.20 = (f32[4,96,128]{2,1,0:T(8,128)S(1)}, f32[4,96,128]{2,1,0:T(8,128)S(1)}, u32[]{:S(2)}, u32[]{:S(2)}) collective-permute-start(f32[4,96,128]{2,1,0:T(8,128)S(1)} %get-tuple-element.678), channel_id=1, source_target_pairs={{0,96},{16,112},{32,0},{48,16},{64,32},{80,48},{96,64},{112,80},{1... | collective-permute-start | bytes 589832 | tf_op jit(solution)/shard_map/while/body/eval_jaxpr/ppermute | solution.py:42
  93.5 9.2 %collective-permute-start.21 = (f32[4,96,128]{2,1,0:T(8,128)S(1)}, f32[4,96,128]{2,1,0:T(8,128)S(1)}, u32[]{:S(2)}, u32[]{:S(2)}) collective-permute-start(f32[4,96,128]{2,1,0:T(8,128)S(1)} %get-tuple-element.679), channel_id=1, source_target_pairs={{0,64},{16,80},{32,96},{48,112},{64,0},{80,16},{96,32},{112,48},{1... | collective-permute-start | bytes 589832 | tf_op jit(solution)/shard_map/while/body/eval_jaxpr/ppermute | solution.py:42
  93.5 12.0 %collective-permute-start.22 = (f32[4,96,128]{2,1,0:T(8,128)S(1)}, f32[4,96,128]{2,1,0:T(8,128)S(1)}, u32[]{:S(2)}, u32[]{:S(2)}) collective-permute-start(f32[4,96,128]{2,1,0:T(8,128)S(1)} %get-tuple-element.680), channel_id=1, source_target_pairs={{0,32},{16,48},{32,64},{48,80},{64,96},{80,112},{96,0},{112,16},{1... | collective-permute-start | bytes 589832 | tf_op jit(solution)/shard_map/while/body/eval_jaxpr/ppermute | solution.py:42
  95.1 22.6 %collective-permute-start.25 = (f32[2,96,128]{2,1,0:T(8,128)S(1)}, f32[2,96,128]{2,1,0:T(8,128)S(1)}, u32[]{:S(2)}, u32[]{:S(2)}) collective-permute-start(f32[2,96,128]{2,1,0:T(8,128)S(1)} %add_add_fusion.2), channel_id=1, source_target_pairs={{0,0},{1,16},{2,32},{3,48},{4,64},{5,80},{6,96},{7,112},{8,128},{9... | collective-permute-start | bytes 294920 | tf_op jit(solution)/shard_map/while/body/eval_jaxpr/ppermute | solution.py:46
  105.5 12.1 %collective-permute-start.23 = (f32[2,96,128]{2,1,0:T(8,128)S(1)}, f32[2,96,128]{2,1,0:T(8,128)S(1)}, u32[]{:S(2)}, u32[]{:S(2)}) collective-permute-start(f32[2,96,128]{2,1,0:T(8,128)S(1)} %slice_add_fusion.22), channel_id=1, source_target_pairs={{0,128},{16,144},{32,160},{48,176},{64,192},{80,208},{96,224},{112... | collective-permute-start | bytes 294920 | tf_op jit(solution)/shard_map/while/body/eval_jaxpr/ppermute | solution.py:42
  117.7 22.7 %copy-start = (s32[1,1,176]{2,1,0:T(1,128)S(1)}, s32[1,1,176]{2,1,0:T(1,128)}, u32[]{:S(2)}) copy-start(s32[1,1,176]{2,1,0:T(1,128)} %get-tuple-element.723.refs_0_) | copy-start | bytes 2116 | tf_op jit(solution)/shard_map/while
  117.7 22.7 %copy-start.1 = (s32[1,1,176]{2,1,0:T(1,128)S(1)}, s32[1,1,176]{2,1,0:T(1,128)}, u32[]{:S(2)}) copy-start(s32[1,1,176]{2,1,0:T(1,128)} %get-tuple-element.724.refs_1_) | copy-start | bytes 2116 | tf_op jit(solution)/shard_map/while
  117.8 5.7 %collective-permute-start = (f32[2,96,128]{2,1,0:T(8,128)S(1)}, f32[2,96,128]{2,1,0:T(8,128)S(1)}, u32[]{:S(2)}, u32[]{:S(2)}) collective-permute-start(f32[2,96,128]{2,1,0:T(8,128)S(1)} %copy.29), channel_id=1, source_target_pairs={{0,128},{16,144},{32,160},{48,176},{64,192},{80,208},{96,224},{112... | collective-permute-start | bytes 294920 | tf_op jit(solution)/shard_map/while/body/eval_jaxpr/ppermute | solution.py:42
  117.9 11.1 %collective-permute-start.4 = (f32[2,96,128]{2,1,0:T(8,128)S(1)}, f32[2,96,128]{2,1,0:T(8,128)S(1)}, u32[]{:S(2)}, u32[]{:S(2)}) collective-permute-start(f32[2,96,128]{2,1,0:T(8,128)S(1)} %get-tuple-element.704), channel_id=1, source_target_pairs={{0,0},{1,16},{2,32},{3,48},{4,64},{5,80},{6,96},{7,112},{8,128},{9... | collective-permute-start | bytes 294920 | tf_op jit(solution)/shard_map/while/body/eval_jaxpr/ppermute | solution.py:46
  123.5 10.3 %collective-permute-start.1 = (f32[4,96,128]{2,1,0:T(8,128)S(1)}, f32[4,96,128]{2,1,0:T(8,128)S(1)}, u32[]{:S(2)}, u32[]{:S(2)}) collective-permute-start(f32[4,96,128]{2,1,0:T(8,128)S(1)} %get-tuple-element.623), channel_id=1, source_target_pairs={{0,96},{16,112},{32,0},{48,16},{64,32},{80,48},{96,64},{112,80},{1... | collective-permute-start | bytes 589832 | tf_op jit(solution)/shard_map/while/body/eval_jaxpr/ppermute | solution.py:42
  123.6 10.2 %collective-permute-start.2 = (f32[4,96,128]{2,1,0:T(8,128)S(1)}, f32[4,96,128]{2,1,0:T(8,128)S(1)}, u32[]{:S(2)}, u32[]{:S(2)}) collective-permute-start(f32[4,96,128]{2,1,0:T(8,128)S(1)} %get-tuple-element.623), channel_id=1, source_target_pairs={{0,64},{16,80},{32,96},{48,112},{64,0},{80,16},{96,32},{112,48},{1... | collective-permute-start | bytes 589832 | tf_op jit(solution)/shard_map/while/body/eval_jaxpr/ppermute | solution.py:42
  123.7 10.1 %collective-permute-start.3 = (f32[4,96,128]{2,1,0:T(8,128)S(1)}, f32[4,96,128]{2,1,0:T(8,128)S(1)}, u32[]{:S(2)}, u32[]{:S(2)}) collective-permute-start(f32[4,96,128]{2,1,0:T(8,128)S(1)} %get-tuple-element.623), channel_id=1, source_target_pairs={{0,32},{16,48},{32,64},{48,80},{64,96},{80,112},{96,0},{112,16},{1... | collective-permute-start | bytes 589832 | tf_op jit(solution)/shard_map/while/body/eval_jaxpr/ppermute | solution.py:42
  129.9 3.8 %collective-permute-start.5 = (f32[2,96,128]{2,1,0:T(8,128)S(1)}, f32[2,96,128]{2,1,0:T(8,128)S(1)}, u32[]{:S(2)}, u32[]{:S(2)}) collective-permute-start(f32[2,96,128]{2,1,0:T(8,128)S(1)} %select_add_fusion.2), channel_id=1, source_target_pairs={{0,1},{1,0},{2,3},{3,2},{4,5},{5,4},{6,7},{7,6},{8,9},{9,8},{10,11... | collective-permute-start | bytes 294920 | tf_op jit(solution)/shard_map/while/body/eval_jaxpr/ppermute | solution.py:42
  133.8 6.6 %collective-permute-start.8 = (f32[16,96,128]{2,1,0:T(8,128)S(1)}, f32[16,96,128]{2,1,0:T(8,128)S(1)}, u32[]{:S(2)}, u32[]{:S(2)}) collective-permute-start(f32[16,96,128]{2,1,0:T(8,128)S(1)} %constant_dynamic-update-slice_fusion.22.refs_5_), channel_id=1, source_target_pairs={{0,16},{16,0},{32,48},{48,32},{64,80},{80,64},{96,112},{112,96},{1... | collective-permute-start | bytes 2359304 | tf_op jit(solution)/shard_map/while/body/eval_jaxpr/ppermute | solution.py:42
  138.3 6.5 %collective-permute-start.6 = (f32[4,96,128]{2,1,0:T(8,128)S(1)}, f32[4,96,128]{2,1,0:T(8,128)S(1)}, u32[]{:S(2)}, u32[]{:S(2)}) collective-permute-start(f32[4,96,128]{2,1,0:T(8,128)S(1)} %constant_dynamic-update-slice_fusion.19.refs_5_), channel_id=1, source_target_pairs={{0,14},{1,15},{2,0},{3,1},{4,2},{5,3},{6,4},{7,5},{8,6},{9,7},{10,... | collective-permute-start | bytes 589832 | tf_op jit(solution)/shard_map/while/body/eval_jaxpr/ppermute | solution.py:42
  140.4 7.4 %collective-permute-start.7 = (f32[4,96,128]{2,1,0:T(8,128)S(1)}, f32[4,96,128]{2,1,0:T(8,128)S(1)}, u32[]{:S(2)}, u32[]{:S(2)}) collective-permute-start(f32[4,96,128]{2,1,0:T(8,128)S(1)} %constant_dynamic-update-slice_fusion.19.refs_5_), channel_id=1, source_target_pairs={{0,2},{1,3},{2,4},{3,5},{4,6},{5,7},{6,8},{7,9},{8,10},{9,11},{10,... | collective-permute-start | bytes 589832 | tf_op jit(solution)/shard_map/while/body/eval_jaxpr/ppermute | solution.py:42
  147.8 8.9 %collective-permute-start.10 = (f32[4,96,128]{2,1,0:T(8,128)S(1)}, f32[4,96,128]{2,1,0:T(8,128)S(1)}, u32[]{:S(2)}, u32[]{:S(2)}) collective-permute-start(f32[4,96,128]{2,1,0:T(8,128)S(1)} %collective-permute-done.7.refs_13_), channel_id=1, source_target_pairs={{0,2},{1,3},{2,4},{3,5},{4,6},{5,7},{6,8},{7,9},{8,10},{9,11},{10,... | collective-permute-start | bytes 589832 | tf_op jit(solution)/shard_map/while/body/eval_jaxpr/ppermute | solution.py:42
  147.8 8.9 %collective-permute-start.9 = (f32[4,96,128]{2,1,0:T(8,128)S(1)}, f32[4,96,128]{2,1,0:T(8,128)S(1)}, u32[]{:S(2)}, u32[]{:S(2)}) collective-permute-start(f32[4,96,128]{2,1,0:T(8,128)S(1)} %collective-permute-done.6.refs_6_), channel_id=1, source_target_pairs={{0,14},{1,15},{2,0},{3,1},{4,2},{5,3},{6,4},{7,5},{8,6},{9,7},{10,... | collective-permute-start | bytes 589832 | tf_op jit(solution)/shard_map/while/body/eval_jaxpr/ppermute | solution.py:42
  156.7 8.5 %collective-permute-start.12 = (f32[6,96,128]{2,1,0:T(8,128)S(1)}, f32[6,96,128]{2,1,0:T(8,128)S(1)}, u32[]{:S(2)}, u32[]{:S(2)}) collective-permute-start(f32[6,96,128]{2,1,0:T(8,128)S(1)} %pad_maximum_fusion.9), channel_id=1, source_target_pairs={{0,2},{1,3},{2,4},{3,5},{4,6},{5,7},{6,8},{7,9},{8,10},{9,11},{10,... | collective-permute-start | bytes 884744 | tf_op jit(solution)/shard_map/while/body/eval_jaxpr/ppermute | solution.py:42
  156.8 8.4 %collective-permute-start.11 = (f32[6,96,128]{2,1,0:T(8,128)S(1)}, f32[6,96,128]{2,1,0:T(8,128)S(1)}, u32[]{:S(2)}, u32[]{:S(2)}) collective-permute-start(f32[6,96,128]{2,1,0:T(8,128)S(1)} %pad_maximum_fusion.8), channel_id=1, source_target_pairs={{0,14},{1,15},{2,0},{3,1},{4,2},{5,3},{6,4},{7,5},{8,6},{9,7},{10,... | collective-permute-start | bytes 884744 | tf_op jit(solution)/shard_map/while/body/eval_jaxpr/ppermute | solution.py:42
  165.3 7.7 %collective-permute-start.14 = (f32[6,96,128]{2,1,0:T(8,128)S(1)}, f32[6,96,128]{2,1,0:T(8,128)S(1)}, u32[]{:S(2)}, u32[]{:S(2)}) collective-permute-start(f32[6,96,128]{2,1,0:T(8,128)S(1)} %pad_maximum_fusion.11), channel_id=1, source_target_pairs={{0,2},{1,3},{2,4},{3,5},{4,6},{5,7},{6,8},{7,9},{8,10},{9,11},{10,... | collective-permute-start | bytes 884744 | tf_op jit(solution)/shard_map/while/body/eval_jaxpr/ppermute | solution.py:42
  165.4 7.5 %collective-permute-start.13 = (f32[6,96,128]{2,1,0:T(8,128)S(1)}, f32[6,96,128]{2,1,0:T(8,128)S(1)}, u32[]{:S(2)}, u32[]{:S(2)}) collective-permute-start(f32[6,96,128]{2,1,0:T(8,128)S(1)} %pad_maximum_fusion.10), channel_id=1, source_target_pairs={{0,14},{1,15},{2,0},{3,1},{4,2},{5,3},{6,4},{7,5},{8,6},{9,7},{10,... | collective-permute-start | bytes 884744 | tf_op jit(solution)/shard_map/while/body/eval_jaxpr/ppermute | solution.py:42
  173.0 8.5 %collective-permute-start.16 = (f32[4,96,128]{2,1,0:T(8,128)S(1)}, f32[4,96,128]{2,1,0:T(8,128)S(1)}, u32[]{:S(2)}, u32[]{:S(2)}) collective-permute-start(f32[4,96,128]{2,1,0:T(8,128)S(1)} %slice_add_fusion.20), channel_id=1, source_target_pairs={{0,14},{1,15},{2,0},{3,1},{4,2},{5,3},{6,4},{7,5},{8,6},{9,7},{10,... | collective-permute-start | bytes 589832 | tf_op jit(solution)/shard_map/while/body/eval_jaxpr/ppermute | solution.py:42
  175.6 5.9 %collective-permute-start.15 = (f32[4,96,128]{2,1,0:T(8,128)S(1)}, f32[4,96,128]{2,1,0:T(8,128)S(1)}, u32[]{:S(2)}, u32[]{:S(2)}) collective-permute-start(f32[4,96,128]{2,1,0:T(8,128)S(1)} %slice_add_fusion.19), channel_id=1, source_target_pairs={{0,2},{1,3},{2,4},{3,5},{4,6},{5,7},{6,8},{7,9},{8,10},{9,11},{10,... | collective-permute-start | bytes 589832 | tf_op jit(solution)/shard_map/while/body/eval_jaxpr/ppermute | solution.py:42
  181.4 14.1 %collective-permute-start.19 = (f32[16,96,128]{2,1,0:T(8,128)S(1)}, f32[16,96,128]{2,1,0:T(8,128)S(1)}, u32[]{:S(2)}, u32[]{:S(2)}) collective-permute-start(f32[16,96,128]{2,1,0:T(8,128)S(1)} %get-tuple-element.674), channel_id=1, source_target_pairs={{0,16},{16,0},{32,48},{48,32},{64,80},{80,64},{96,112},{112,96},{1... | collective-permute-start | bytes 2359304 | tf_op jit(solution)/shard_map/while/body/eval_jaxpr/ppermute | solution.py:42
  186.2 6.5 %collective-permute-start.18 = (f32[4,96,128]{2,1,0:T(8,128)S(1)}, f32[4,96,128]{2,1,0:T(8,128)S(1)}, u32[]{:S(2)}, u32[]{:S(2)}) collective-permute-start(f32[4,96,128]{2,1,0:T(8,128)S(1)} %add.327), channel_id=1, source_target_pairs={{0,14},{1,15},{2,0},{3,1},{4,2},{5,3},{6,4},{7,5},{8,6},{9,7},{10,... | collective-permute-start | bytes 589832 | tf_op jit(solution)/shard_map/while/body/eval_jaxpr/ppermute | solution.py:42
  188.0 7.6 %collective-permute-start.17 = (f32[4,96,128]{2,1,0:T(8,128)S(1)}, f32[4,96,128]{2,1,0:T(8,128)}, u32[]{:S(2)}, u32[]{:S(2)}) collective-permute-start(f32[4,96,128]{2,1,0:T(8,128)S(1)} %add.326), channel_id=1, source_target_pairs={{0,2},{1,3},{2,4},{3,5},{4,6},{5,7},{6,8},{7,9},{8,10},{9,11},{10,... | collective-permute-start | bytes 589832 | tf_op jit(solution)/shard_map/while/body/eval_jaxpr/ppermute | solution.py:42
  196.5 6.8 %collective-permute-start.24 = (f32[2,96,128]{2,1,0:T(8,128)S(1)}, f32[2,96,128]{2,1,0:T(8,128)S(1)}, u32[]{:S(2)}, u32[]{:S(2)}) collective-permute-start(f32[2,96,128]{2,1,0:T(8,128)S(1)} %slice_add_fusion.23), channel_id=1, source_target_pairs={{0,1},{1,0},{2,3},{3,2},{4,5},{5,4},{6,7},{7,6},{8,9},{9,8},{10,11... | collective-permute-start | bytes 294920 | tf_op jit(solution)/shard_map/while/body/eval_jaxpr/ppermute | solution.py:42
  199.6 10.5 %collective-permute-start.20 = (f32[4,96,128]{2,1,0:T(8,128)S(1)}, f32[4,96,128]{2,1,0:T(8,128)S(1)}, u32[]{:S(2)}, u32[]{:S(2)}) collective-permute-start(f32[4,96,128]{2,1,0:T(8,128)S(1)} %get-tuple-element.678), channel_id=1, source_target_pairs={{0,96},{16,112},{32,0},{48,16},{64,32},{80,48},{96,64},{112,80},{1... | collective-permute-start | bytes 589832 | tf_op jit(solution)/shard_map/while/body/eval_jaxpr/ppermute | solution.py:42
  202.6 7.6 %collective-permute-start.21 = (f32[4,96,128]{2,1,0:T(8,128)S(1)}, f32[4,96,128]{2,1,0:T(8,128)S(1)}, u32[]{:S(2)}, u32[]{:S(2)}) collective-permute-start(f32[4,96,128]{2,1,0:T(8,128)S(1)} %get-tuple-element.679), channel_id=1, source_target_pairs={{0,64},{16,80},{32,96},{48,112},{64,0},{80,16},{96,32},{112,48},{1... | collective-permute-start | bytes 589832 | tf_op jit(solution)/shard_map/while/body/eval_jaxpr/ppermute | solution.py:42
  202.6 12.0 %collective-permute-start.22 = (f32[4,96,128]{2,1,0:T(8,128)S(1)}, f32[4,96,128]{2,1,0:T(8,128)S(1)}, u32[]{:S(2)}, u32[]{:S(2)}) collective-permute-start(f32[4,96,128]{2,1,0:T(8,128)S(1)} %get-tuple-element.680), channel_id=1, source_target_pairs={{0,32},{16,48},{32,64},{48,80},{64,96},{80,112},{96,0},{112,16},{1... | collective-permute-start | bytes 589832 | tf_op jit(solution)/shard_map/while/body/eval_jaxpr/ppermute | solution.py:42
  204.2 21.7 %collective-permute-start.25 = (f32[2,96,128]{2,1,0:T(8,128)S(1)}, f32[2,96,128]{2,1,0:T(8,128)S(1)}, u32[]{:S(2)}, u32[]{:S(2)}) collective-permute-start(f32[2,96,128]{2,1,0:T(8,128)S(1)} %add_add_fusion.2), channel_id=1, source_target_pairs={{0,0},{1,16},{2,32},{3,48},{4,64},{5,80},{6,96},{7,112},{8,128},{9... | collective-permute-start | bytes 294920 | tf_op jit(solution)/shard_map/while/body/eval_jaxpr/ppermute | solution.py:46
  214.6 11.3 %collective-permute-start.23 = (f32[2,96,128]{2,1,0:T(8,128)S(1)}, f32[2,96,128]{2,1,0:T(8,128)S(1)}, u32[]{:S(2)}, u32[]{:S(2)}) collective-permute-start(f32[2,96,128]{2,1,0:T(8,128)S(1)} %slice_add_fusion.22), channel_id=1, source_target_pairs={{0,128},{16,144},{32,160},{48,176},{64,192},{80,208},{96,224},{112... | collective-permute-start | bytes 294920 | tf_op jit(solution)/shard_map/while/body/eval_jaxpr/ppermute | solution.py:42
where the time goes:
time: 227 us
  starting transfers between devices  93.2 us (41%)
  waiting for transfers between devices  92.3 us (41%)
  Pallas kernels  30.5 us (13%)
  other arithmetic  6.71 us (3%)
    ppermute x48, waiting for transfers between devices, send(): return lax.ppermute(x, axis, perm)  88.3 us
    ppermute x48, starting transfers between devices, send(): return lax.ppermute(x, axis, perm)  64.6 us
    pallas_call x6, Pallas kernels, products(): pl.pallas_call(functools.partial(product_kernel, backward, first, last, n...  30.5 us
    ppermute x4, starting transfers between devices, flip(): return lax.ppermute(x, ('row', 'col'), FLIP)  28.7 us
  transfers between devices with their start and end apart: 52, of which 24 were waited for; matrix products, arithmetic and copies ran while one was open for 2% of the time, Pallas kernels for 13%

commit v1 on v0

--- a/solution.py
+++ b/solution.py
@@ -83,8 +83,8 @@
 
 
 def product_kernel(backward, first, last, n_in, runs, out_sizes, *refs):
-    rows, cols, count, here, blocks = refs[:5]
-    parts, refs = refs[5 : 5 + n_in], refs[5 + n_in :]
+    table, blocks = refs[:2]
+    parts, refs = refs[2 : 2 + n_in], refs[2 + n_in :]
     if not first:
         halves, total_in, refs = refs[0], refs[1], refs[2:]
     outs, refs = refs[: len(out_sizes)], refs[len(out_sizes) :]
@@ -92,8 +92,8 @@
         halves, total, held, sems = refs
     else:
         total, held, sems = refs
-    live = count[0, 0]
-    bs = blocks.shape[-1]
+    bs, slots = blocks.shape[-1], blocks.shape[2]
+    live = table[slots]
     full = lax.div(live, UNROLL)
     middle = lax.div(full, 2)
     begin = 0 if first else middle
@@ -127,10 +127,9 @@
         total[...] = jnp.zeros_like(total)
     else:
         total[...] = total_in[...]
-    row, col = here[0], here[1]
 
     def one(s):
-        rb, cb = row_slot(rows[0, 0, s], col), col_slot(cols[0, 0, s], row)
+        rb, cb = table[s] >> 5, table[s] & 31
         high, low = split(held[s])
         zero = jnp.zeros_like(low)
         if backward:
@@ -174,7 +173,7 @@
 
 
 def products(backward, first, last, state, index):
-    blocks = index[4]
+    blocks = index[1]
     slots, bs = blocks.shape[2], blocks.shape[-1]
     vecs = state[0].shape[1]
     n_in = len(state) if first else 0
@@ -198,11 +197,11 @@
     share = 1 if first and last else 2
     return pl.pallas_call(
         functools.partial(product_kernel, backward, first, last, n_in, runs, out_sizes),
-        in_specs=[smem] * 4 + [pl.BlockSpec(memory_space=pltpu.HBM)] + [vmem] * len(state),
+        in_specs=[smem] + [pl.BlockSpec(memory_space=pltpu.HBM)] + [vmem] * len(state),
         out_specs=[vmem] * len(out_shape),
         out_shape=out_shape,
         scratch_shapes=scratch,
-        compiler_params=pltpu.CompilerParams(vmem_limit_bytes=48 << 20),
+        compiler_params=pltpu.CompilerParams(vmem_limit_bytes=45 << 20),
         cost_estimate=pl.CostEstimate(
             flops=24 * slots * vecs * bs * bs // share,
             bytes_accessed=4 * slots * bs * bs // share,
@@ -213,10 +212,11 @@
 
 def body(vectors, blocks, block_row, block_col, block_count, lower_bound, upper_bound):
     vecs, bs = vectors.shape[0], blocks.shape[-1]
-    here = jnp.stack([lax.axis_index("row"), lax.axis_index("col")]).astype(jnp.int32)
     center = (upper_bound[0] + lower_bound[0]) / 2.0
     half_width = (upper_bound[0] - lower_bound[0]) / 2.0
-    index = (block_row, block_col, block_count, here, blocks)
+    row, col = lax.axis_index("row"), lax.axis_index("col")
+    table = row_slot(block_row[0, 0], col) * 32 + col_slot(block_col[0, 0], row)
+    index = (jnp.concatenate([table, block_count[0]]), blocks)
 
     def apply_hamiltonian(a0, flipping, finish):
         a1 = send(a0, "row", X_HI)

time: 227 us -> 229 us (level)
  Pallas kernels: 30.5 us -> 26.5 us
  waiting for transfers between devices: 92.3 us -> 95.3 us
    ppermute x48, starting transfers between devices: 64.6 us -> 70.9 us  [send(): return lax.ppermute(x, axis, perm)]
    ppermute x4, starting transfers between devices: 28.7 us -> 24.2 us  [flip(): return lax.ppermute(x, ('row', 'col'), FLIP)]
    pallas_call x6, Pallas kernels: 30.5 us -> 26.5 us  [products(): pl.pallas_call(functools.partial(product_kernel, backward, first, last, n...]
    ppermute x48, waiting for transfers between devices: 88.3 us -> 91 us  [send(): return lax.ppermute(x, axis, perm)]
  transfers between devices with their start and end apart: 52 -> 52, of which waited for: 24 -> 31; matrix products, arithmetic and copies ran while one was open for 2% -> 2% of each run, Pallas kernels for 13% -> 12%
where the time goes in v1:
time: 229 us
  waiting for transfers between devices  95.3 us (42%)
  starting transfers between devices  95.1 us (42%)
  Pallas kernels  26.5 us (12%)
  other arithmetic  7.42 us (3%)
    ppermute x48, waiting for transfers between devices, send(): return lax.ppermute(x, axis, perm)  91 us
    ppermute x48, starting transfers between devices, send(): return lax.ppermute(x, axis, perm)  70.9 us
    pallas_call x6, Pallas kernels, products(): pl.pallas_call(functools.partial(product_kernel, backward, first, last, n...  26.5 us
    ppermute x4, starting transfers between devices, flip(): return lax.ppermute(x, ('row', 'col'), FLIP)  24.2 us
  transfers between devices with their start and end apart: 52, of which 31 were waited for; matrix products, arithmetic and copies ran while one was open for 2% of the time, Pallas kernels for 12%

profile of v1, /device:TPU:5, one launch (start us, length us, event | category | flops | bytes accessed | tf_op | source)
XLA Modules:
  0.0 228.8 jit_solution(9039232288484890097)
XLA Ops:
  2.8 0.9 reshape.48
  3.8 224.3 %while.23 = (s32[]{:T(128)}, f32[2,96,128]{2,1,0:T(8,128)S(1)}, f32[2,96,128]{2,1,0:T(8,128)S(1)}, f32[2,96,128]{2,1,0:T(8,128)S(1)}, f32[]{:T(128)}, /*index=5*...) while((s32[]{:T(128)}, f32[2,96,128]{2,1,0:T(8,128)S(1)}, ...), condition=%wide.region_1.2_spmd.clone, body=%wide.region_0.1_spmd.clone.sunk | while | flops 13289054208 | bytes 61113520 | solution.py:281
  3.9 11.4 %collective-permute-start.4 = (f32[2,96,128]{2,1,0:T(8,128)S(1)}, f32[2,96,128]{2,1,0:T(8,128)S(1)}, u32[]{:S(2)}, u32[]{:S(2)}) collective-permute-start(f32[2,96,128]{2,1,0:T(8,128)S(1)} %get-tuple-element.614), channel_id=1, source_target_pairs={{0,0},{1,16},{2,32},{3,48},{4,64},{5,80},{6,96},{7,112},{8,128},{9... | collective-permute-start | bytes 294920 | tf_op jit(solution)/shard_map/while/body/eval_jaxpr/ppermute | solution.py:46
  15.4 1.1 collective-permute-start.1
  16.6 1.5 collective-permute-start.2
  18.2 2.2 collective-permute-start.5
  20.4 2.3 %collective-permute-done.5 = f32[2,96,128]{2,1,0:T(8,128)S(1)} collective-permute-done((f32[2,96,128]{2,1,0:T(8,128)S(1)}, f32[2,96,128]{2,1,0:T(8,128)S(1)}, u32[]{:S(2)}, u32[]{:S(2)}) %collective-permute-start.5) | collective-permute-done | bytes 98336 | tf_op jit(solution)/shard_map/while/body/eval_jaxpr/ppermute | solution.py:42
  22.7 3.1 %collective-permute-done.2 = f32[4,96,128]{2,1,0:T(8,128)S(1)} collective-permute-done((f32[4,96,128]{2,1,0:T(8,128)S(1)}, f32[4,96,128]{2,1,0:T(8,128)S(1)}, u32[]{:S(2)}, u32[]{:S(2)}) %collective-permute-start.2) | collective-permute-done | bytes 196640 | tf_op jit(solution)/shard_map/while/body/eval_jaxpr/ppermute | solution.py:42
  25.9 4.2 %collective-permute-done.3 = f32[4,96,128]{2,1,0:T(8,128)S(1)} collective-permute-done((f32[4,96,128]{2,1,0:T(8,128)S(1)}, f32[4,96,128]{2,1,0:T(8,128)S(1)}, u32[]{:S(2)}, u32[]{:S(2)}) %collective-permute-start.3) | collective-permute-done | bytes 196640 | tf_op jit(solution)/shard_map/while/body/eval_jaxpr/ppermute | solution.py:42
  31.6 1.0 collective-permute-start.7
  32.9 2.7 %eval_jaxpr.18 = (bf16[32,96,256]{2,1,0:T(8,128)(2,1)S(1)}, f32[32,96,128]{2,1,0:T(8,128)S(1)}) custom-call(s32[177]{0:T(256)S(1)} %get-tuple-element.630.refs_0_, f32[1,1,176,128,128]{4,3,2,1,0:T(8,128)} %get-tuple-element.631.refs_1_, f32[16,96,128]{2,1,0:T(8,128)S(1)} %constant_dynamic-update-slice_fusion.22.refs_2_, ...), custom_call_target="tpu_custom_call" | custom-call | flops 3321888768 | bytes 5767168 | tf_op jit(solution)/shard_map/while/body/eval_jaxpr/pallas_call | solution.py:198
  35.6 1.9 collective-permute-done.6.refs_3_
  37.5 1.4 collective-permute-done.7.refs_10_
  39.6 1.9 collective-permute-start.9
  41.6 5.5 %eval_jaxpr.19 = (f32[4,96,128]{2,1,0:T(8,128)S(1)}, f32[4,96,128]{2,1,0:T(8,128)S(1)}, f32[4,96,128]{2,1,0:T(8,128)S(1)}, f32[4,96,128]{2,1,0:T(8,128)S(1)}, f3...) custom-call(s32[177]{0:T(256)S(1)} %get-tuple-element.630.refs_0_, ...), custom_call_target="tpu_custom_call" | custom-call | flops 3321888768 | bytes 5767168 | tf_op jit(solution)/shard_map/while/body/eval_jaxpr/pallas_call | solution.py:198
  47.2 1.5 collective-permute-start.12
  48.7 1.4 collective-permute-start.11
  50.1 5.7 %collective-permute-done.12.refs_8_ = f32[6,96,128]{2,1,0:T(8,128)S(1)} collective-permute-done((f32[6,96,128]{2,1,0:T(8,128)S(1)}, f32[6,96,128]{2,1,0:T(8,128)S(1)}, u32[]{:S(2)}, u32[]{:S(2)}) %collective-permute-start.12) | collective-permute-done | bytes 294944 | tf_op jit(solution)/shard_map/while/body/eval_jaxpr/ppermute | solution.py:42
  55.8 0.9 collective-permute-done.11.refs_5_
  57.7 2.0 collective-permute-start.13
  59.7 5.3 %collective-permute-done.14.refs_6_ = f32[6,96,128]{2,1,0:T(8,128)S(1)} collective-permute-done((f32[6,96,128]{2,1,0:T(8,128)S(1)}, f32[6,96,128]{2,1,0:T(8,128)S(1)}, u32[]{:S(2)}, u32[]{:S(2)}) %collective-permute-start.14) | collective-permute-done | bytes 294944 | tf_op jit(solution)/shard_map/while/body/eval_jaxpr/ppermute | solution.py:42
  65.0 2.6 %collective-permute-start.16 = (f32[4,96,128]{2,1,0:T(8,128)S(1)}, f32[4,96,128]{2,1,0:T(8,128)S(1)}, u32[]{:S(2)}, u32[]{:S(2)}) collective-permute-start(f32[4,96,128]{2,1,0:T(8,128)S(1)} %slice_add_fusion.20), channel_id=1, source_target_pairs={{0,14},{1,15},{2,0},{3,1},{4,2},{5,3},{6,4},{7,5},{8,6},{9,7},{10,... | collective-permute-start | bytes 589832 | tf_op jit(solution)/shard_map/while/body/eval_jaxpr/ppermute | solution.py:42
  67.6 5.1 %eval_jaxpr.20 = (f32[4,96,128]{2,1,0:T(8,128)S(1)}, f32[4,96,128]{2,1,0:T(8,128)S(1)}, f32[4,96,128]{2,1,0:T(8,128)S(1)}, f32[4,96,128]{2,1,0:T(8,128)S(1)}, f32[16,96,128]{2,1,0:T(8,128)S(1)}) custom-call(s32[177]{0:T(256)S(1)} %get-tuple-element.630.refs_0_, f32[1,1,176,128,128]{4,3,2,1,0:T(8,128)} %get-tuple-element.631.refs_1_, ...), custom_call_target="tpu_custom_call" | custom-call | flops 6643777536 | bytes 11534336 | tf_op jit(solution)/shard_map/while/body/eval_jaxpr/pallas_call | solution.py:198
  73.4 4.3 %collective-permute-start.19 = (f32[16,96,128]{2,1,0:T(8,128)S(1)}, f32[16,96,128]{2,1,0:T(8,128)S(1)}, u32[]{:S(2)}, u32[]{:S(2)}) collective-permute-start(f32[16,96,128]{2,1,0:T(8,128)S(1)} %get-tuple-element.587), channel_id=1, source_target_pairs={{0,16},{16,0},{32,48},{48,32},{64,80},{80,64},{96,112},{112,96},{1... | collective-permute-start | bytes 2359304 | tf_op jit(solution)/shard_map/while/body/eval_jaxpr/ppermute | solution.py:42
  77.7 1.2 collective-permute-start.18
  79.3 5.0 %collective-permute-done.18 = f32[4,96,128]{2,1,0:T(8,128)S(1)} collective-permute-done((f32[4,96,128]{2,1,0:T(8,128)S(1)}, f32[4,96,128]{2,1,0:T(8,128)S(1)}, u32[]{:S(2)}, u32[]{:S(2)}) %collective-permute-start.18) | collective-permute-done | bytes 196640 | tf_op jit(solution)/shard_map/while/body/eval_jaxpr/ppermute | solution.py:42
  84.3 2.1 collective-permute-done.17
  87.3 2.6 %collective-permute-start.24 = (f32[2,96,128]{2,1,0:T(8,128)S(1)}, f32[2,96,128]{2,1,0:T(8,128)S(1)}, u32[]{:S(2)}, u32[]{:S(2)}) collective-permute-start(f32[2,96,128]{2,1,0:T(8,128)S(1)} %slice_add_fusion.23), channel_id=1, source_target_pairs={{0,1},{1,0},{2,3},{3,2},{4,5},{5,4},{6,7},{7,6},{8,9},{9,8},{10,11... | collective-permute-start | bytes 294920 | tf_op jit(solution)/shard_map/while/body/eval_jaxpr/ppermute | solution.py:42
  90.0 3.5 %collective-permute-start.20 = (f32[4,96,128]{2,1,0:T(8,128)S(1)}, f32[4,96,128]{2,1,0:T(8,128)S(1)}, u32[]{:S(2)}, u32[]{:S(2)}) collective-permute-start(f32[4,96,128]{2,1,0:T(8,128)S(1)} %get-tuple-element.591), channel_id=1, source_target_pairs={{0,96},{16,112},{32,0},{48,16},{64,32},{80,48},{96,64},{112,80},{1... | collective-permute-start | bytes 589832 | tf_op jit(solution)/shard_map/while/body/eval_jaxpr/ppermute | solution.py:42
  94.2 0.9 add_add_fusion.3
  95.1 6.3 %collective-permute-start.25 = (f32[2,96,128]{2,1,0:T(8,128)S(1)}, f32[2,96,128]{2,1,0:T(8,128)S(1)}, u32[]{:S(2)}, u32[]{:S(2)}) collective-permute-start(f32[2,96,128]{2,1,0:T(8,128)S(1)} %add_add_fusion.3), channel_id=1, source_target_pairs={{0,0},{1,16},{2,32},{3,48},{4,64},{5,80},{6,96},{7,112},{8,128},{9... | collective-permute-start | bytes 294920 | tf_op jit(solution)/shard_map/while/body/eval_jaxpr/ppermute | solution.py:46
  101.5 4.0 %collective-permute-done.22 = f32[4,96,128]{2,1,0:T(8,128)S(1)} collective-permute-done((f32[4,96,128]{2,1,0:T(8,128)S(1)}, f32[4,96,128]{2,1,0:T(8,128)S(1)}, u32[]{:S(2)}, u32[]{:S(2)}) %collective-permute-start.22) | collective-permute-done | bytes 196640 | tf_op jit(solution)/shard_map/while/body/eval_jaxpr/ppermute | solution.py:42
  105.5 2.7 %collective-permute-start.23 = (f32[2,96,128]{2,1,0:T(8,128)S(1)}, f32[2,96,128]{2,1,0:T(8,128)S(1)}, u32[]{:S(2)}, u32[]{:S(2)}) collective-permute-start(f32[2,96,128]{2,1,0:T(8,128)S(1)} %slice_add_fusion.22), channel_id=1, source_target_pairs={{0,128},{16,144},{32,160},{48,176},{64,192},{80,208},{96,224},{112... | collective-permute-start | bytes 294920 | tf_op jit(solution)/shard_map/while/body/eval_jaxpr/ppermute | solution.py:42
  108.9 8.5 %collective-permute-done.23 = f32[2,96,128]{2,1,0:T(8,128)S(1)} collective-permute-done((f32[2,96,128]{2,1,0:T(8,128)S(1)}, f32[2,96,128]{2,1,0:T(8,128)S(1)}, u32[]{:S(2)}, u32[]{:S(2)}) %collective-permute-start.23) | collective-permute-done | bytes 98336 | tf_op jit(solution)/shard_map/while/body/eval_jaxpr/ppermute | solution.py:42
  117.7 3.1 %collective-permute-start.4 = (f32[2,96,128]{2,1,0:T(8,128)S(1)}, f32[2,96,128]{2,1,0:T(8,128)S(1)}, u32[]{:S(2)}, u32[]{:S(2)}) collective-permute-start(f32[2,96,128]{2,1,0:T(8,128)S(1)} %get-tuple-element.614), channel_id=1, source_target_pairs={{0,0},{1,16},{2,32},{3,48},{4,64},{5,80},{6,96},{7,112},{8,128},{9... | collective-permute-start | bytes 294920 | tf_op jit(solution)/shard_map/while/body/eval_jaxpr/ppermute | solution.py:46
  120.8 2.3 collective-permute-done
  123.3 1.4 collective-permute-start.3
  124.6 4.3 %collective-permute-done.4 = f32[2,96,128]{2,1,0:T(8,128)S(1)} collective-permute-done((f32[2,96,128]{2,1,0:T(8,128)S(1)}, f32[2,96,128]{2,1,0:T(8,128)S(1)}, u32[]{:S(2)}, u32[]{:S(2)}) %collective-permute-start.4) | collective-permute-done | bytes 98336 | tf_op jit(solution)/shard_map/while/body/eval_jaxpr/ppermute | solution.py:46
  129.8 1.0 collective-permute-start.5
  130.8 2.8 %collective-permute-done.5 = f32[2,96,128]{2,1,0:T(8,128)S(1)} collective-permute-done((f32[2,96,128]{2,1,0:T(8,128)S(1)}, f32[2,96,128]{2,1,0:T(8,128)S(1)}, u32[]{:S(2)}, u32[]{:S(2)}) %collective-permute-start.5) | collective-permute-done | bytes 98336 | tf_op jit(solution)/shard_map/while/body/eval_jaxpr/ppermute | solution.py:42
  133.8 4.5 %collective-permute-start.8 = (f32[16,96,128]{2,1,0:T(8,128)S(1)}, f32[16,96,128]{2,1,0:T(8,128)S(1)}, u32[]{:S(2)}, u32[]{:S(2)}) collective-permute-start(f32[16,96,128]{2,1,0:T(8,128)S(1)} %constant_dynamic-update-slice_fusion.22.refs_2_), channel_id=1, source_target_pairs={{0,16},{16,0},{32,48},{48,32},{64,80},{80,64},{96,112},{112,96},{1... | collective-permute-start | bytes 2359304 | tf_op jit(solution)/shard_map/while/body/eval_jaxpr/ppermute | solution.py:42
  138.3 1.7 collective-permute-start.6
  140.2 2.7 %eval_jaxpr.18 = (bf16[32,96,256]{2,1,0:T(8,128)(2,1)S(1)}, f32[32,96,128]{2,1,0:T(8,128)S(1)}) custom-call(s32[177]{0:T(256)S(1)} %get-tuple-element.630.refs_0_, f32[1,1,176,128,128]{4,3,2,1,0:T(8,128)} %get-tuple-element.631.refs_1_, f32[16,96,128]{2,1,0:T(8,128)S(1)} %constant_dynamic-update-slice_fusion.22.refs_2_, ...), custom_call_target="tpu_custom_call" | custom-call | flops 3321888768 | bytes 5767168 | tf_op jit(solution)/shard_map/while/body/eval_jaxpr/pallas_call | solution.py:198
  142.8 1.9 collective-permute-done.6.refs_3_
  144.8 2.6 %collective-permute-done.7.refs_10_ = f32[4,96,128]{2,1,0:T(8,128)S(1)} collective-permute-done((f32[4,96,128]{2,1,0:T(8,128)S(1)}, f32[4,96,128]{2,1,0:T(8,128)S(1)}, u32[]{:S(2)}, u32[]{:S(2)}) %collective-permute-start.7) | collective-permute-done | bytes 196640 | tf_op jit(solution)/shard_map/while/body/eval_jaxpr/ppermute | solution.py:42
  147.4 2.7 %collective-permute-start.9 = (f32[4,96,128]{2,1,0:T(8,128)S(1)}, f32[4,96,128]{2,1,0:T(8,128)S(1)}, u32[]{:S(2)}, u32[]{:S(2)}) collective-permute-start(f32[4,96,128]{2,1,0:T(8,128)S(1)} %collective-permute-done.6.refs_3_), channel_id=1, source_target_pairs={{0,14},{1,15},{2,0},{3,1},{4,2},{5,3},{6,4},{7,5},{8,6},{9,7},{10,... | collective-permute-start | bytes 589832 | tf_op jit(solution)/shard_map/while/body/eval_jaxpr/ppermute | solution.py:42
  150.0 5.5 %eval_jaxpr.19 = (f32[4,96,128]{2,1,0:T(8,128)S(1)}, f32[4,96,128]{2,1,0:T(8,128)S(1)}, f32[4,96,128]{2,1,0:T(8,128)S(1)}, f32[4,96,128]{2,1,0:T(8,128)S(1)}, f3...) custom-call(s32[177]{0:T(256)S(1)} %get-tuple-element.630.refs_0_, ...), custom_call_target="tpu_custom_call" | custom-call | flops 3321888768 | bytes 5767168 | tf_op jit(solution)/shard_map/while/body/eval_jaxpr/pallas_call | solution.py:198
  156.1 2.3 %collective-permute-start.11 = (f32[6,96,128]{2,1,0:T(8,128)S(1)}, f32[6,96,128]{2,1,0:T(8,128)S(1)}, u32[]{:S(2)}, u32[]{:S(2)}) collective-permute-start(f32[6,96,128]{2,1,0:T(8,128)S(1)} %pad_maximum_fusion.8), channel_id=1, source_target_pairs={{0,14},{1,15},{2,0},{3,1},{4,2},{5,3},{6,4},{7,5},{8,6},{9,7},{10,... | collective-permute-start | bytes 884744 | tf_op jit(solution)/shard_map/while/body/eval_jaxpr/ppermute | solution.py:42
  158.5 5.7 %collective-permute-done.12.refs_8_ = f32[6,96,128]{2,1,0:T(8,128)S(1)} collective-permute-done((f32[6,96,128]{2,1,0:T(8,128)S(1)}, f32[6,96,128]{2,1,0:T(8,128)S(1)}, u32[]{:S(2)}, u32[]{:S(2)}) %collective-permute-start.12) | collective-permute-done | bytes 294944 | tf_op jit(solution)/shard_map/while/body/eval_jaxpr/ppermute | solution.py:42
  164.2 1.5 collective-permute-start.14
  165.8 1.3 collective-permute-start.13
  167.1 4.8 %collective-permute-done.14.refs_6_ = f32[6,96,128]{2,1,0:T(8,128)S(1)} collective-permute-done((f32[6,96,128]{2,1,0:T(8,128)S(1)}, f32[6,96,128]{2,1,0:T(8,128)S(1)}, u32[]{:S(2)}, u32[]{:S(2)}) %collective-permute-start.14) | collective-permute-done | bytes 294944 | tf_op jit(solution)/shard_map/while/body/eval_jaxpr/ppermute | solution.py:42
  172.4 2.1 collective-permute-start.16
  174.7 5.1 %eval_jaxpr.20 = (f32[4,96,128]{2,1,0:T(8,128)S(1)}, f32[4,96,128]{2,1,0:T(8,128)S(1)}, f32[4,96,128]{2,1,0:T(8,128)S(1)}, f32[4,96,128]{2,1,0:T(8,128)S(1)}, f32[16,96,128]{2,1,0:T(8,128)S(1)}) custom-call(s32[177]{0:T(256)S(1)} %get-tuple-element.630.refs_0_, f32[1,1,176,128,128]{4,3,2,1,0:T(8,128)} %get-tuple-element.631.refs_1_, ...), custom_call_target="tpu_custom_call" | custom-call | flops 6643777536 | bytes 11534336 | tf_op jit(solution)/shard_map/while/body/eval_jaxpr/pallas_call | solution.py:198
  180.4 4.7 %collective-permute-start.19 = (f32[16,96,128]{2,1,0:T(8,128)S(1)}, f32[16,96,128]{2,1,0:T(8,128)S(1)}, u32[]{:S(2)}, u32[]{:S(2)}) collective-permute-start(f32[16,96,128]{2,1,0:T(8,128)S(1)} %get-tuple-element.587), channel_id=1, source_target_pairs={{0,16},{16,0},{32,48},{48,32},{64,80},{80,64},{96,112},{112,96},{1... | collective-permute-start | bytes 2359304 | tf_op jit(solution)/shard_map/while/body/eval_jaxpr/ppermute | solution.py:42
  185.1 1.2 collective-permute-start.18
  186.8 5.0 %collective-permute-done.18 = f32[4,96,128]{2,1,0:T(8,128)S(1)} collective-permute-done((f32[4,96,128]{2,1,0:T(8,128)S(1)}, f32[4,96,128]{2,1,0:T(8,128)S(1)}, u32[]{:S(2)}, u32[]{:S(2)}) %collective-permute-start.18) | collective-permute-done | bytes 196640 | tf_op jit(solution)/shard_map/while/body/eval_jaxpr/ppermute | solution.py:42
  191.8 2.1 collective-permute-done.17
  194.8 8.8 %collective-permute-start.24 = (f32[2,96,128]{2,1,0:T(8,128)S(1)}, f32[2,96,128]{2,1,0:T(8,128)S(1)}, u32[]{:S(2)}, u32[]{:S(2)}) collective-permute-start(f32[2,96,128]{2,1,0:T(8,128)S(1)} %slice_add_fusion.23), channel_id=1, source_target_pairs={{0,1},{1,0},{2,3},{3,2},{4,5},{5,4},{6,7},{7,6},{8,9},{9,8},{10,11... | collective-permute-start | bytes 294920 | tf_op jit(solution)/shard_map/while/body/eval_jaxpr/ppermute | solution.py:42
  203.8 1.4 collective-permute-start.22
  206.5 3.4 %collective-permute-start.25 = (f32[2,96,128]{2,1,0:T(8,128)S(1)}, f32[2,96,128]{2,1,0:T(8,128)S(1)}, u32[]{:S(2)}, u32[]{:S(2)}) collective-permute-start(f32[2,96,128]{2,1,0:T(8,128)S(1)} %add_add_fusion.3), channel_id=1, source_target_pairs={{0,0},{1,16},{2,32},{3,48},{4,64},{5,80},{6,96},{7,112},{8,128},{9... | collective-permute-start | bytes 294920 | tf_op jit(solution)/shard_map/while/body/eval_jaxpr/ppermute | solution.py:46
  210.4 5.8 %collective-permute-done.22 = f32[4,96,128]{2,1,0:T(8,128)S(1)} collective-permute-done((f32[4,96,128]{2,1,0:T(8,128)S(1)}, f32[4,96,128]{2,1,0:T(8,128)S(1)}, u32[]{:S(2)}, u32[]{:S(2)}) %collective-permute-start.22) | collective-permute-done | bytes 196640 | tf_op jit(solution)/shard_map/while/body/eval_jaxpr/ppermute | solution.py:42
  216.2 0.9 collective-permute-start.23
  217.8 10.3 %collective-permute-done.23 = f32[2,96,128]{2,1,0:T(8,128)S(1)} collective-permute-done((f32[2,96,128]{2,1,0:T(8,128)S(1)}, f32[2,96,128]{2,1,0:T(8,128)S(1)}, u32[]{:S(2)}, u32[]{:S(2)}) %collective-permute-start.23) | collective-permute-done | bytes 98336 | tf_op jit(solution)/shard_map/while/body/eval_jaxpr/ppermute | solution.py:42
  (107 shorter events, 16.6 us)
Async XLA Ops:
  3.8 11.6 %collective-permute-start = (f32[2,96,128]{2,1,0:T(8,128)S(1)}, f32[2,96,128]{2,1,0:T(8,128)S(1)}, u32[]{:S(2)}, u32[]{:S(2)}) collective-permute-start(f32[2,96,128]{2,1,0:T(8,128)S(1)} %copy.29), channel_id=1, source_target_pairs={{0,128},{16,144},{32,160},{48,176},{64,192},{80,208},{96,224},{112... | collective-permute-start | bytes 294920 | tf_op jit(solution)/shard_map/while/body/eval_jaxpr/ppermute | solution.py:42
  3.9 14.3 %collective-permute-start.4 = (f32[2,96,128]{2,1,0:T(8,128)S(1)}, f32[2,96,128]{2,1,0:T(8,128)S(1)}, u32[]{:S(2)}, u32[]{:S(2)}) collective-permute-start(f32[2,96,128]{2,1,0:T(8,128)S(1)} %get-tuple-element.614), channel_id=1, source_target_pairs={{0,0},{1,16},{2,32},{3,48},{4,64},{5,80},{6,96},{7,112},{8,128},{9... | collective-permute-start | bytes 294920 | tf_op jit(solution)/shard_map/while/body/eval_jaxpr/ppermute | solution.py:46
  15.4 7.3 %collective-permute-start.1 = (f32[4,96,128]{2,1,0:T(8,128)S(1)}, f32[4,96,128]{2,1,0:T(8,128)S(1)}, u32[]{:S(2)}, u32[]{:S(2)}) collective-permute-start(f32[4,96,128]{2,1,0:T(8,128)S(1)} %get-tuple-element.536), channel_id=1, source_target_pairs={{0,96},{16,112},{32,0},{48,16},{64,32},{80,48},{96,64},{112,80},{1... | collective-permute-start | bytes 589832 | tf_op jit(solution)/shard_map/while/body/eval_jaxpr/ppermute | solution.py:42
  16.6 9.3 %collective-permute-start.2 = (f32[4,96,128]{2,1,0:T(8,128)S(1)}, f32[4,96,128]{2,1,0:T(8,128)S(1)}, u32[]{:S(2)}, u32[]{:S(2)}) collective-permute-start(f32[4,96,128]{2,1,0:T(8,128)S(1)} %get-tuple-element.536), channel_id=1, source_target_pairs={{0,64},{16,80},{32,96},{48,112},{64,0},{80,16},{96,32},{112,48},{1... | collective-permute-start | bytes 589832 | tf_op jit(solution)/shard_map/while/body/eval_jaxpr/ppermute | solution.py:42
  18.0 12.0 %collective-permute-start.3 = (f32[4,96,128]{2,1,0:T(8,128)S(1)}, f32[4,96,128]{2,1,0:T(8,128)S(1)}, u32[]{:S(2)}, u32[]{:S(2)}) collective-permute-start(f32[4,96,128]{2,1,0:T(8,128)S(1)} %get-tuple-element.536), channel_id=1, source_target_pairs={{0,32},{16,48},{32,64},{48,80},{64,96},{80,112},{96,0},{112,16},{1... | collective-permute-start | bytes 589832 | tf_op jit(solution)/shard_map/while/body/eval_jaxpr/ppermute | solution.py:42
  18.2 4.5 %collective-permute-start.5 = (f32[2,96,128]{2,1,0:T(8,128)S(1)}, f32[2,96,128]{2,1,0:T(8,128)S(1)}, u32[]{:S(2)}, u32[]{:S(2)}) collective-permute-start(f32[2,96,128]{2,1,0:T(8,128)S(1)} %select_add_fusion.2), channel_id=1, source_target_pairs={{0,1},{1,0},{2,3},{3,2},{4,5},{5,4},{6,7},{7,6},{8,9},{9,8},{10,11... | collective-permute-start | bytes 294920 | tf_op jit(solution)/shard_map/while/body/eval_jaxpr/ppermute | solution.py:42
  30.1 2.8 %collective-permute-start.8 = (f32[16,96,128]{2,1,0:T(8,128)S(1)}, f32[16,96,128]{2,1,0:T(8,128)S(1)}, u32[]{:S(2)}, u32[]{:S(2)}) collective-permute-start(f32[16,96,128]{2,1,0:T(8,128)S(1)} %constant_dynamic-update-slice_fusion.22.refs_2_), channel_id=1, source_target_pairs={{0,16},{16,0},{32,48},{48,32},{64,80},{80,64},{96,112},{112,96},{1... | collective-permute-start | bytes 2359304 | tf_op jit(solution)/shard_map/while/body/eval_jaxpr/ppermute | solution.py:42
  31.0 6.5 %collective-permute-start.6 = (f32[4,96,128]{2,1,0:T(8,128)S(1)}, f32[4,96,128]{2,1,0:T(8,128)S(1)}, u32[]{:S(2)}, u32[]{:S(2)}) collective-permute-start(f32[4,96,128]{2,1,0:T(8,128)S(1)} %constant_dynamic-update-slice_fusion.19.refs_2_), channel_id=1, source_target_pairs={{0,14},{1,15},{2,0},{3,1},{4,2},{5,3},{6,4},{7,5},{8,6},{9,7},{10,... | collective-permute-start | bytes 589832 | tf_op jit(solution)/shard_map/while/body/eval_jaxpr/ppermute | solution.py:42
  31.6 7.3 %collective-permute-start.7 = (f32[4,96,128]{2,1,0:T(8,128)S(1)}, f32[4,96,128]{2,1,0:T(8,128)S(1)}, u32[]{:S(2)}, u32[]{:S(2)}) collective-permute-start(f32[4,96,128]{2,1,0:T(8,128)S(1)} %constant_dynamic-update-slice_fusion.19.refs_2_), channel_id=1, source_target_pairs={{0,2},{1,3},{2,4},{3,5},{4,6},{5,7},{6,8},{7,9},{8,10},{9,11},{10,... | collective-permute-start | bytes 589832 | tf_op jit(solution)/shard_map/while/body/eval_jaxpr/ppermute | solution.py:42
  38.9 8.2 %collective-permute-start.10 = (f32[4,96,128]{2,1,0:T(8,128)S(1)}, f32[4,96,128]{2,1,0:T(8,128)S(1)}, u32[]{:S(2)}, u32[]{:S(2)}) collective-permute-start(f32[4,96,128]{2,1,0:T(8,128)S(1)} %collective-permute-done.7.refs_10_), channel_id=1, source_target_pairs={{0,2},{1,3},{2,4},{3,5},{4,6},{5,7},{6,8},{7,9},{8,10},{9,11},{10,... | collective-permute-start | bytes 589832 | tf_op jit(solution)/shard_map/while/body/eval_jaxpr/ppermute | solution.py:42
  39.6 7.6 %collective-permute-start.9 = (f32[4,96,128]{2,1,0:T(8,128)S(1)}, f32[4,96,128]{2,1,0:T(8,128)S(1)}, u32[]{:S(2)}, u32[]{:S(2)}) collective-permute-start(f32[4,96,128]{2,1,0:T(8,128)S(1)} %collective-permute-done.6.refs_3_), channel_id=1, source_target_pairs={{0,14},{1,15},{2,0},{3,1},{4,2},{5,3},{6,4},{7,5},{8,6},{9,7},{10,... | collective-permute-start | bytes 589832 | tf_op jit(solution)/shard_map/while/body/eval_jaxpr/ppermute | solution.py:42
  47.2 8.6 %collective-permute-start.12 = (f32[6,96,128]{2,1,0:T(8,128)S(1)}, f32[6,96,128]{2,1,0:T(8,128)S(1)}, u32[]{:S(2)}, u32[]{:S(2)}) collective-permute-start(f32[6,96,128]{2,1,0:T(8,128)S(1)} %pad_maximum_fusion.9), channel_id=1, source_target_pairs={{0,2},{1,3},{2,4},{3,5},{4,6},{5,7},{6,8},{7,9},{8,10},{9,11},{10,... | collective-permute-start | bytes 884744 | tf_op jit(solution)/shard_map/while/body/eval_jaxpr/ppermute | solution.py:42
  48.7 8.0 %collective-permute-start.11 = (f32[6,96,128]{2,1,0:T(8,128)S(1)}, f32[6,96,128]{2,1,0:T(8,128)S(1)}, u32[]{:S(2)}, u32[]{:S(2)}) collective-permute-start(f32[6,96,128]{2,1,0:T(8,128)S(1)} %pad_maximum_fusion.8), channel_id=1, source_target_pairs={{0,14},{1,15},{2,0},{3,1},{4,2},{5,3},{6,4},{7,5},{8,6},{9,7},{10,... | collective-permute-start | bytes 884744 | tf_op jit(solution)/shard_map/while/body/eval_jaxpr/ppermute | solution.py:42
  56.8 8.1 %collective-permute-start.14 = (f32[6,96,128]{2,1,0:T(8,128)S(1)}, f32[6,96,128]{2,1,0:T(8,128)S(1)}, u32[]{:S(2)}, u32[]{:S(2)}) collective-permute-start(f32[6,96,128]{2,1,0:T(8,128)S(1)} %pad_maximum_fusion.11), channel_id=1, source_target_pairs={{0,2},{1,3},{2,4},{3,5},{4,6},{5,7},{6,8},{7,9},{8,10},{9,11},{10,... | collective-permute-start | bytes 884744 | tf_op jit(solution)/shard_map/while/body/eval_jaxpr/ppermute | solution.py:42
  57.7 7.3 %collective-permute-start.13 = (f32[6,96,128]{2,1,0:T(8,128)S(1)}, f32[6,96,128]{2,1,0:T(8,128)S(1)}, u32[]{:S(2)}, u32[]{:S(2)}) collective-permute-start(f32[6,96,128]{2,1,0:T(8,128)S(1)} %pad_maximum_fusion.10), channel_id=1, source_target_pairs={{0,14},{1,15},{2,0},{3,1},{4,2},{5,3},{6,4},{7,5},{8,6},{9,7},{10,... | collective-permute-start | bytes 884744 | tf_op jit(solution)/shard_map/while/body/eval_jaxpr/ppermute | solution.py:42
  65.0 7.8 %collective-permute-start.16 = (f32[4,96,128]{2,1,0:T(8,128)S(1)}, f32[4,96,128]{2,1,0:T(8,128)S(1)}, u32[]{:S(2)}, u32[]{:S(2)}) collective-permute-start(f32[4,96,128]{2,1,0:T(8,128)S(1)} %slice_add_fusion.20), channel_id=1, source_target_pairs={{0,14},{1,15},{2,0},{3,1},{4,2},{5,3},{6,4},{7,5},{8,6},{9,7},{10,... | collective-permute-start | bytes 589832 | tf_op jit(solution)/shard_map/while/body/eval_jaxpr/ppermute | solution.py:42
  67.6 5.8 %collective-permute-start.15 = (f32[4,96,128]{2,1,0:T(8,128)S(1)}, f32[4,96,128]{2,1,0:T(8,128)S(1)}, u32[]{:S(2)}, u32[]{:S(2)}) collective-permute-start(f32[4,96,128]{2,1,0:T(8,128)S(1)} %slice_add_fusion.19), channel_id=1, source_target_pairs={{0,2},{1,3},{2,4},{3,5},{4,6},{5,7},{6,8},{7,9},{8,10},{9,11},{10,... | collective-permute-start | bytes 589832 | tf_op jit(solution)/shard_map/while/body/eval_jaxpr/ppermute | solution.py:42
  73.4 13.1 %collective-permute-start.19 = (f32[16,96,128]{2,1,0:T(8,128)S(1)}, f32[16,96,128]{2,1,0:T(8,128)S(1)}, u32[]{:S(2)}, u32[]{:S(2)}) collective-permute-start(f32[16,96,128]{2,1,0:T(8,128)S(1)} %get-tuple-element.587), channel_id=1, source_target_pairs={{0,16},{16,0},{32,48},{48,32},{64,80},{80,64},{96,112},{112,96},{1... | collective-permute-start | bytes 2359304 | tf_op jit(solution)/shard_map/while/body/eval_jaxpr/ppermute | solution.py:42
  77.7 6.6 %collective-permute-start.18 = (f32[4,96,128]{2,1,0:T(8,128)S(1)}, f32[4,96,128]{2,1,0:T(8,128)S(1)}, u32[]{:S(2)}, u32[]{:S(2)}) collective-permute-start(f32[4,96,128]{2,1,0:T(8,128)S(1)} %add.363), channel_id=1, source_target_pairs={{0,14},{1,15},{2,0},{3,1},{4,2},{5,3},{6,4},{7,5},{8,6},{9,7},{10,... | collective-permute-start | bytes 589832 | tf_op jit(solution)/shard_map/while/body/eval_jaxpr/ppermute | solution.py:42
  78.9 7.6 %collective-permute-start.17 = (f32[4,96,128]{2,1,0:T(8,128)S(1)}, f32[4,96,128]{2,1,0:T(8,128)}, u32[]{:S(2)}, u32[]{:S(2)}) collective-permute-start(f32[4,96,128]{2,1,0:T(8,128)S(1)} %add.362), channel_id=1, source_target_pairs={{0,2},{1,3},{2,4},{3,5},{4,6},{5,7},{6,8},{7,9},{8,10},{9,11},{10,... | collective-permute-start | bytes 589832 | tf_op jit(solution)/shard_map/while/body/eval_jaxpr/ppermute | solution.py:42
  87.3 6.9 %collective-permute-start.24 = (f32[2,96,128]{2,1,0:T(8,128)S(1)}, f32[2,96,128]{2,1,0:T(8,128)S(1)}, u32[]{:S(2)}, u32[]{:S(2)}) collective-permute-start(f32[2,96,128]{2,1,0:T(8,128)S(1)} %slice_add_fusion.23), channel_id=1, source_target_pairs={{0,1},{1,0},{2,3},{3,2},{4,5},{5,4},{6,7},{7,6},{8,9},{9,8},{10,11... | collective-permute-start | bytes 294920 | tf_op jit(solution)/shard_map/while/body/eval_jaxpr/ppermute | solution.py:42
  90.0 11.4 %collective-permute-start.20 = (f32[4,96,128]{2,1,0:T(8,128)S(1)}, f32[4,96,128]{2,1,0:T(8,128)S(1)}, u32[]{:S(2)}, u32[]{:S(2)}) collective-permute-start(f32[4,96,128]{2,1,0:T(8,128)S(1)} %get-tuple-element.591), channel_id=1, source_target_pairs={{0,96},{16,112},{32,0},{48,16},{64,32},{80,48},{96,64},{112,80},{1... | collective-permute-start | bytes 589832 | tf_op jit(solution)/shard_map/while/body/eval_jaxpr/ppermute | solution.py:42
  93.5 7.9 %collective-permute-start.21 = (f32[4,96,128]{2,1,0:T(8,128)S(1)}, f32[4,96,128]{2,1,0:T(8,128)S(1)}, u32[]{:S(2)}, u32[]{:S(2)}) collective-permute-start(f32[4,96,128]{2,1,0:T(8,128)S(1)} %get-tuple-element.592), channel_id=1, source_target_pairs={{0,64},{16,80},{32,96},{48,112},{64,0},{80,16},{96,32},{112,48},{1... | collective-permute-start | bytes 589832 | tf_op jit(solution)/shard_map/while/body/eval_jaxpr/ppermute | solution.py:42
  93.5 12.0 %collective-permute-start.22 = (f32[4,96,128]{2,1,0:T(8,128)S(1)}, f32[4,96,128]{2,1,0:T(8,128)S(1)}, u32[]{:S(2)}, u32[]{:S(2)}) collective-permute-start(f32[4,96,128]{2,1,0:T(8,128)S(1)} %get-tuple-element.593), channel_id=1, source_target_pairs={{0,32},{16,48},{32,64},{48,80},{64,96},{80,112},{96,0},{112,16},{1... | collective-permute-start | bytes 589832 | tf_op jit(solution)/shard_map/while/body/eval_jaxpr/ppermute | solution.py:42
  95.1 22.3 %collective-permute-start.25 = (f32[2,96,128]{2,1,0:T(8,128)S(1)}, f32[2,96,128]{2,1,0:T(8,128)S(1)}, u32[]{:S(2)}, u32[]{:S(2)}) collective-permute-start(f32[2,96,128]{2,1,0:T(8,128)S(1)} %add_add_fusion.3), channel_id=1, source_target_pairs={{0,0},{1,16},{2,32},{3,48},{4,64},{5,80},{6,96},{7,112},{8,128},{9... | collective-permute-start | bytes 294920 | tf_op jit(solution)/shard_map/while/body/eval_jaxpr/ppermute | solution.py:46
  105.5 11.9 %collective-permute-start.23 = (f32[2,96,128]{2,1,0:T(8,128)S(1)}, f32[2,96,128]{2,1,0:T(8,128)S(1)}, u32[]{:S(2)}, u32[]{:S(2)}) collective-permute-start(f32[2,96,128]{2,1,0:T(8,128)S(1)} %slice_add_fusion.22), channel_id=1, source_target_pairs={{0,128},{16,144},{32,160},{48,176},{64,192},{80,208},{96,224},{112... | collective-permute-start | bytes 294920 | tf_op jit(solution)/shard_map/while/body/eval_jaxpr/ppermute | solution.py:42
  117.6 5.5 %collective-permute-start = (f32[2,96,128]{2,1,0:T(8,128)S(1)}, f32[2,96,128]{2,1,0:T(8,128)S(1)}, u32[]{:S(2)}, u32[]{:S(2)}) collective-permute-start(f32[2,96,128]{2,1,0:T(8,128)S(1)} %copy.29), channel_id=1, source_target_pairs={{0,128},{16,144},{32,160},{48,176},{64,192},{80,208},{96,224},{112... | collective-permute-start | bytes 294920 | tf_op jit(solution)/shard_map/while/body/eval_jaxpr/ppermute | solution.py:42
  117.7 11.3 %collective-permute-start.4 = (f32[2,96,128]{2,1,0:T(8,128)S(1)}, f32[2,96,128]{2,1,0:T(8,128)S(1)}, u32[]{:S(2)}, u32[]{:S(2)}) collective-permute-start(f32[2,96,128]{2,1,0:T(8,128)S(1)} %get-tuple-element.614), channel_id=1, source_target_pairs={{0,0},{1,16},{2,32},{3,48},{4,64},{5,80},{6,96},{7,112},{8,128},{9... | collective-permute-start | bytes 294920 | tf_op jit(solution)/shard_map/while/body/eval_jaxpr/ppermute | solution.py:46
  123.1 10.6 %collective-permute-start.1 = (f32[4,96,128]{2,1,0:T(8,128)S(1)}, f32[4,96,128]{2,1,0:T(8,128)S(1)}, u32[]{:S(2)}, u32[]{:S(2)}) collective-permute-start(f32[4,96,128]{2,1,0:T(8,128)S(1)} %get-tuple-element.536), channel_id=1, source_target_pairs={{0,96},{16,112},{32,0},{48,16},{64,32},{80,48},{96,64},{112,80},{1... | collective-permute-start | bytes 589832 | tf_op jit(solution)/shard_map/while/body/eval_jaxpr/ppermute | solution.py:42
  123.2 10.5 %collective-permute-start.2 = (f32[4,96,128]{2,1,0:T(8,128)S(1)}, f32[4,96,128]{2,1,0:T(8,128)S(1)}, u32[]{:S(2)}, u32[]{:S(2)}) collective-permute-start(f32[4,96,128]{2,1,0:T(8,128)S(1)} %get-tuple-element.536), channel_id=1, source_target_pairs={{0,64},{16,80},{32,96},{48,112},{64,0},{80,16},{96,32},{112,48},{1... | collective-permute-start | bytes 589832 | tf_op jit(solution)/shard_map/while/body/eval_jaxpr/ppermute | solution.py:42
  123.3 10.4 %collective-permute-start.3 = (f32[4,96,128]{2,1,0:T(8,128)S(1)}, f32[4,96,128]{2,1,0:T(8,128)S(1)}, u32[]{:S(2)}, u32[]{:S(2)}) collective-permute-start(f32[4,96,128]{2,1,0:T(8,128)S(1)} %get-tuple-element.536), channel_id=1, source_target_pairs={{0,32},{16,48},{32,64},{48,80},{64,96},{80,112},{96,0},{112,16},{1... | collective-permute-start | bytes 589832 | tf_op jit(solution)/shard_map/while/body/eval_jaxpr/ppermute | solution.py:42
  129.8 3.8 %collective-permute-start.5 = (f32[2,96,128]{2,1,0:T(8,128)S(1)}, f32[2,96,128]{2,1,0:T(8,128)S(1)}, u32[]{:S(2)}, u32[]{:S(2)}) collective-permute-start(f32[2,96,128]{2,1,0:T(8,128)S(1)} %select_add_fusion.2), channel_id=1, source_target_pairs={{0,1},{1,0},{2,3},{3,2},{4,5},{5,4},{6,7},{7,6},{8,9},{9,8},{10,11... | collective-permute-start | bytes 294920 | tf_op jit(solution)/shard_map/while/body/eval_jaxpr/ppermute | solution.py:42
  133.8 6.4 %collective-permute-start.8 = (f32[16,96,128]{2,1,0:T(8,128)S(1)}, f32[16,96,128]{2,1,0:T(8,128)S(1)}, u32[]{:S(2)}, u32[]{:S(2)}) collective-permute-start(f32[16,96,128]{2,1,0:T(8,128)S(1)} %constant_dynamic-update-slice_fusion.22.refs_2_), channel_id=1, source_target_pairs={{0,16},{16,0},{32,48},{48,32},{64,80},{80,64},{96,112},{112,96},{1... | collective-permute-start | bytes 2359304 | tf_op jit(solution)/shard_map/while/body/eval_jaxpr/ppermute | solution.py:42
  138.3 6.5 %collective-permute-start.6 = (f32[4,96,128]{2,1,0:T(8,128)S(1)}, f32[4,96,128]{2,1,0:T(8,128)S(1)}, u32[]{:S(2)}, u32[]{:S(2)}) collective-permute-start(f32[4,96,128]{2,1,0:T(8,128)S(1)} %constant_dynamic-update-slice_fusion.19.refs_2_), channel_id=1, source_target_pairs={{0,14},{1,15},{2,0},{3,1},{4,2},{5,3},{6,4},{7,5},{8,6},{9,7},{10,... | collective-permute-start | bytes 589832 | tf_op jit(solution)/shard_map/while/body/eval_jaxpr/ppermute | solution.py:42
  140.0 7.4 %collective-permute-start.7 = (f32[4,96,128]{2,1,0:T(8,128)S(1)}, f32[4,96,128]{2,1,0:T(8,128)S(1)}, u32[]{:S(2)}, u32[]{:S(2)}) collective-permute-start(f32[4,96,128]{2,1,0:T(8,128)S(1)} %constant_dynamic-update-slice_fusion.19.refs_2_), channel_id=1, source_target_pairs={{0,2},{1,3},{2,4},{3,5},{4,6},{5,7},{6,8},{7,9},{8,10},{9,11},{10,... | collective-permute-start | bytes 589832 | tf_op jit(solution)/shard_map/while/body/eval_jaxpr/ppermute | solution.py:42
  147.4 8.2 %collective-permute-start.10 = (f32[4,96,128]{2,1,0:T(8,128)S(1)}, f32[4,96,128]{2,1,0:T(8,128)S(1)}, u32[]{:S(2)}, u32[]{:S(2)}) collective-permute-start(f32[4,96,128]{2,1,0:T(8,128)S(1)} %collective-permute-done.7.refs_10_), channel_id=1, source_target_pairs={{0,2},{1,3},{2,4},{3,5},{4,6},{5,7},{6,8},{7,9},{8,10},{9,11},{10,... | collective-permute-start | bytes 589832 | tf_op jit(solution)/shard_map/while/body/eval_jaxpr/ppermute | solution.py:42
  147.4 8.2 %collective-permute-start.9 = (f32[4,96,128]{2,1,0:T(8,128)S(1)}, f32[4,96,128]{2,1,0:T(8,128)S(1)}, u32[]{:S(2)}, u32[]{:S(2)}) collective-permute-start(f32[4,96,128]{2,1,0:T(8,128)S(1)} %collective-permute-done.6.refs_3_), channel_id=1, source_target_pairs={{0,14},{1,15},{2,0},{3,1},{4,2},{5,3},{6,4},{7,5},{8,6},{9,7},{10,... | collective-permute-start | bytes 589832 | tf_op jit(solution)/shard_map/while/body/eval_jaxpr/ppermute | solution.py:42
  155.6 8.5 %collective-permute-start.12 = (f32[6,96,128]{2,1,0:T(8,128)S(1)}, f32[6,96,128]{2,1,0:T(8,128)S(1)}, u32[]{:S(2)}, u32[]{:S(2)}) collective-permute-start(f32[6,96,128]{2,1,0:T(8,128)S(1)} %pad_maximum_fusion.9), channel_id=1, source_target_pairs={{0,2},{1,3},{2,4},{3,5},{4,6},{5,7},{6,8},{7,9},{8,10},{9,11},{10,... | collective-permute-start | bytes 884744 | tf_op jit(solution)/shard_map/while/body/eval_jaxpr/ppermute | solution.py:42
  156.1 8.0 %collective-permute-start.11 = (f32[6,96,128]{2,1,0:T(8,128)S(1)}, f32[6,96,128]{2,1,0:T(8,128)S(1)}, u32[]{:S(2)}, u32[]{:S(2)}) collective-permute-start(f32[6,96,128]{2,1,0:T(8,128)S(1)} %pad_maximum_fusion.8), channel_id=1, source_target_pairs={{0,14},{1,15},{2,0},{3,1},{4,2},{5,3},{6,4},{7,5},{8,6},{9,7},{10,... | collective-permute-start | bytes 884744 | tf_op jit(solution)/shard_map/while/body/eval_jaxpr/ppermute | solution.py:42
  164.2 7.7 %collective-permute-start.14 = (f32[6,96,128]{2,1,0:T(8,128)S(1)}, f32[6,96,128]{2,1,0:T(8,128)S(1)}, u32[]{:S(2)}, u32[]{:S(2)}) collective-permute-start(f32[6,96,128]{2,1,0:T(8,128)S(1)} %pad_maximum_fusion.11), channel_id=1, source_target_pairs={{0,2},{1,3},{2,4},{3,5},{4,6},{5,7},{6,8},{7,9},{8,10},{9,11},{10,... | collective-permute-start | bytes 884744 | tf_op jit(solution)/shard_map/while/body/eval_jaxpr/ppermute | solution.py:42
  165.8 6.6 %collective-permute-start.13 = (f32[6,96,128]{2,1,0:T(8,128)S(1)}, f32[6,96,128]{2,1,0:T(8,128)S(1)}, u32[]{:S(2)}, u32[]{:S(2)}) collective-permute-start(f32[6,96,128]{2,1,0:T(8,128)S(1)} %pad_maximum_fusion.10), channel_id=1, source_target_pairs={{0,14},{1,15},{2,0},{3,1},{4,2},{5,3},{6,4},{7,5},{8,6},{9,7},{10,... | collective-permute-start | bytes 884744 | tf_op jit(solution)/shard_map/while/body/eval_jaxpr/ppermute | solution.py:42
  172.4 7.3 %collective-permute-start.16 = (f32[4,96,128]{2,1,0:T(8,128)S(1)}, f32[4,96,128]{2,1,0:T(8,128)S(1)}, u32[]{:S(2)}, u32[]{:S(2)}) collective-permute-start(f32[4,96,128]{2,1,0:T(8,128)S(1)} %slice_add_fusion.20), channel_id=1, source_target_pairs={{0,14},{1,15},{2,0},{3,1},{4,2},{5,3},{6,4},{7,5},{8,6},{9,7},{10,... | collective-permute-start | bytes 589832 | tf_op jit(solution)/shard_map/while/body/eval_jaxpr/ppermute | solution.py:42
  174.6 5.8 %collective-permute-start.15 = (f32[4,96,128]{2,1,0:T(8,128)S(1)}, f32[4,96,128]{2,1,0:T(8,128)S(1)}, u32[]{:S(2)}, u32[]{:S(2)}) collective-permute-start(f32[4,96,128]{2,1,0:T(8,128)S(1)} %slice_add_fusion.19), channel_id=1, source_target_pairs={{0,2},{1,3},{2,4},{3,5},{4,6},{5,7},{6,8},{7,9},{8,10},{9,11},{10,... | collective-permute-start | bytes 589832 | tf_op jit(solution)/shard_map/while/body/eval_jaxpr/ppermute | solution.py:42
  180.4 13.5 %collective-permute-start.19 = (f32[16,96,128]{2,1,0:T(8,128)S(1)}, f32[16,96,128]{2,1,0:T(8,128)S(1)}, u32[]{:S(2)}, u32[]{:S(2)}) collective-permute-start(f32[16,96,128]{2,1,0:T(8,128)S(1)} %get-tuple-element.587), channel_id=1, source_target_pairs={{0,16},{16,0},{32,48},{48,32},{64,80},{80,64},{96,112},{112,96},{1... | collective-permute-start | bytes 2359304 | tf_op jit(solution)/shard_map/while/body/eval_jaxpr/ppermute | solution.py:42
  185.1 6.6 %collective-permute-start.18 = (f32[4,96,128]{2,1,0:T(8,128)S(1)}, f32[4,96,128]{2,1,0:T(8,128)S(1)}, u32[]{:S(2)}, u32[]{:S(2)}) collective-permute-start(f32[4,96,128]{2,1,0:T(8,128)S(1)} %add.363), channel_id=1, source_target_pairs={{0,14},{1,15},{2,0},{3,1},{4,2},{5,3},{6,4},{7,5},{8,6},{9,7},{10,... | collective-permute-start | bytes 589832 | tf_op jit(solution)/shard_map/while/body/eval_jaxpr/ppermute | solution.py:42
  186.3 7.6 %collective-permute-start.17 = (f32[4,96,128]{2,1,0:T(8,128)S(1)}, f32[4,96,128]{2,1,0:T(8,128)}, u32[]{:S(2)}, u32[]{:S(2)}) collective-permute-start(f32[4,96,128]{2,1,0:T(8,128)S(1)} %add.362), channel_id=1, source_target_pairs={{0,2},{1,3},{2,4},{3,5},{4,6},{5,7},{6,8},{7,9},{8,10},{9,11},{10,... | collective-permute-start | bytes 589832 | tf_op jit(solution)/shard_map/while/body/eval_jaxpr/ppermute | solution.py:42
  194.8 10.8 %collective-permute-start.24 = (f32[2,96,128]{2,1,0:T(8,128)S(1)}, f32[2,96,128]{2,1,0:T(8,128)S(1)}, u32[]{:S(2)}, u32[]{:S(2)}) collective-permute-start(f32[2,96,128]{2,1,0:T(8,128)S(1)} %slice_add_fusion.23), channel_id=1, source_target_pairs={{0,1},{1,0},{2,3},{3,2},{4,5},{5,4},{6,7},{7,6},{8,9},{9,8},{10,11... | collective-permute-start | bytes 294920 | tf_op jit(solution)/shard_map/while/body/eval_jaxpr/ppermute | solution.py:42
  203.7 6.2 %collective-permute-start.20 = (f32[4,96,128]{2,1,0:T(8,128)S(1)}, f32[4,96,128]{2,1,0:T(8,128)S(1)}, u32[]{:S(2)}, u32[]{:S(2)}) collective-permute-start(f32[4,96,128]{2,1,0:T(8,128)S(1)} %get-tuple-element.591), channel_id=1, source_target_pairs={{0,96},{16,112},{32,0},{48,16},{64,32},{80,48},{96,64},{112,80},{1... | collective-permute-start | bytes 589832 | tf_op jit(solution)/shard_map/while/body/eval_jaxpr/ppermute | solution.py:42
  203.7 6.6 %collective-permute-start.21 = (f32[4,96,128]{2,1,0:T(8,128)S(1)}, f32[4,96,128]{2,1,0:T(8,128)S(1)}, u32[]{:S(2)}, u32[]{:S(2)}) collective-permute-start(f32[4,96,128]{2,1,0:T(8,128)S(1)} %get-tuple-element.592), channel_id=1, source_target_pairs={{0,64},{16,80},{32,96},{48,112},{64,0},{80,16},{96,32},{112,48},{1... | collective-permute-start | bytes 589832 | tf_op jit(solution)/shard_map/while/body/eval_jaxpr/ppermute | solution.py:42
  203.8 12.3 %collective-permute-start.22 = (f32[4,96,128]{2,1,0:T(8,128)S(1)}, f32[4,96,128]{2,1,0:T(8,128)S(1)}, u32[]{:S(2)}, u32[]{:S(2)}) collective-permute-start(f32[4,96,128]{2,1,0:T(8,128)S(1)} %get-tuple-element.593), channel_id=1, source_target_pairs={{0,32},{16,48},{32,64},{48,80},{64,96},{80,112},{96,0},{112,16},{1... | collective-permute-start | bytes 589832 | tf_op jit(solution)/shard_map/while/body/eval_jaxpr/ppermute | solution.py:42
  206.5 21.5 %collective-permute-start.25 = (f32[2,96,128]{2,1,0:T(8,128)S(1)}, f32[2,96,128]{2,1,0:T(8,128)S(1)}, u32[]{:S(2)}, u32[]{:S(2)}) collective-permute-start(f32[2,96,128]{2,1,0:T(8,128)S(1)} %add_add_fusion.3), channel_id=1, source_target_pairs={{0,0},{1,16},{2,32},{3,48},{4,64},{5,80},{6,96},{7,112},{8,128},{9... | collective-permute-start | bytes 294920 | tf_op jit(solution)/shard_map/while/body/eval_jaxpr/ppermute | solution.py:46
  216.2 11.8 %collective-permute-start.23 = (f32[2,96,128]{2,1,0:T(8,128)S(1)}, f32[2,96,128]{2,1,0:T(8,128)S(1)}, u32[]{:S(2)}, u32[]{:S(2)}) collective-permute-start(f32[2,96,128]{2,1,0:T(8,128)S(1)} %slice_add_fusion.22), channel_id=1, source_target_pairs={{0,128},{16,144},{32,160},{48,176},{64,192},{80,208},{96,224},{112... | collective-permute-start | bytes 294920 | tf_op jit(solution)/shard_map/while/body/eval_jaxpr/ppermute | solution.py:42

commit v2 on v0

--- a/solution.py
+++ b/solution.py
@@ -83,8 +83,8 @@
 
 
 def product_kernel(backward, first, last, n_in, runs, out_sizes, *refs):
-    rows, cols, count, here, blocks = refs[:5]
-    parts, refs = refs[5 : 5 + n_in], refs[5 + n_in :]
+    rows, cols, info, blocks = refs[:4]
+    parts, refs = refs[4 : 4 + n_in], refs[4 + n_in :]
     if not first:
         halves, total_in, refs = refs[0], refs[1], refs[2:]
     outs, refs = refs[: len(out_sizes)], refs[len(out_sizes) :]
@@ -92,8 +92,8 @@
         halves, total, held, sems = refs
     else:
         total, held, sems = refs
-    live = count[0, 0]
     bs = blocks.shape[-1]
+    row, col, live = info[0], info[1], info[2]
     full = lax.div(live, UNROLL)
     middle = lax.div(full, 2)
     begin = 0 if first else middle
@@ -127,7 +127,6 @@
         total[...] = jnp.zeros_like(total)
     else:
         total[...] = total_in[...]
-    row, col = here[0], here[1]
 
     def one(s):
         rb, cb = row_slot(rows[0, 0, s], col), col_slot(cols[0, 0, s], row)
@@ -174,7 +173,7 @@
 
 
 def products(backward, first, last, state, index):
-    blocks = index[4]
+    blocks = index[3]
     slots, bs = blocks.shape[2], blocks.shape[-1]
     vecs = state[0].shape[1]
     n_in = len(state) if first else 0
@@ -198,11 +197,11 @@
     share = 1 if first and last else 2
     return pl.pallas_call(
         functools.partial(product_kernel, backward, first, last, n_in, runs, out_sizes),
-        in_specs=[smem] * 4 + [pl.BlockSpec(memory_space=pltpu.HBM)] + [vmem] * len(state),
+        in_specs=[smem] * 3 + [pl.BlockSpec(memory_space=pltpu.HBM)] + [vmem] * len(state),
         out_specs=[vmem] * len(out_shape),
         out_shape=out_shape,
         scratch_shapes=scratch,
-        compiler_params=pltpu.CompilerParams(vmem_limit_bytes=48 << 20),
+        compiler_params=pltpu.CompilerParams(vmem_limit_bytes=49 << 20),
         cost_estimate=pl.CostEstimate(
             flops=24 * slots * vecs * bs * bs // share,
             bytes_accessed=4 * slots * bs * bs // share,
@@ -213,10 +212,10 @@
 
 def body(vectors, blocks, block_row, block_col, block_count, lower_bound, upper_bound):
     vecs, bs = vectors.shape[0], blocks.shape[-1]
-    here = jnp.stack([lax.axis_index("row"), lax.axis_index("col")]).astype(jnp.int32)
     center = (upper_bound[0] + lower_bound[0]) / 2.0
     half_width = (upper_bound[0] - lower_bound[0]) / 2.0
-    index = (block_row, block_col, block_count, here, blocks)
+    here = (lax.axis_index("row"), lax.axis_index("col"), block_count[0, 0])
+    index = (block_row, block_col, jnp.stack(here).astype(jnp.int32), blocks)
 
     def apply_hamiltonian(a0, flipping, finish):
         a1 = send(a0, "row", X_HI)
@@ -247,15 +246,15 @@
         up4, down4 = bar(up4, down4)
         u = send(f2 + down4[2:], "col", Z_UP)
         d = send(f6 + up4[2:], "col", Z_DOWN)
+        u, d = bar(u, d)
+        u = send(f1 + u, "col", Z_UP)
+        d = send(f7 + d, "col", Z_DOWN)
         state = (z0, up1, up2, up3, down4, up4, down3, down2, down1)
         backward = products(True, True, True, state, index)
         u, d, *backward = bar(u, d, *backward)
         g0, g1, g2, g3, other = backward
-        u = send(f1 + u, "col", Z_UP)
-        d = send(f7 + d, "col", Z_DOWN)
+        h = send(f0[2:] + u[2:] + d[2:], "col", X_LO)
         o = send(other, "row", CORE)
-        u, d, o = bar(u, d, o)
-        h = send(f0[2:] + u[2:] + d[2:], "col", X_LO)
         q1 = send(g1 + o[4:8], "row", Y_UP)
         q2 = send(g2 + o[8:12], "row", Y_FAR)
         q3 = send(g3 + o[12:], "row", Y_DOWN)

time: 227 us -> 226 us (level)
  the two profiles are of different devices: /device:TPU:5 before, /device:TPU:7 now
where the time goes in v2:
time: 226 us
  starting transfers between devices  103 us (46%)
  waiting for transfers between devices  101 us (45%)
  Pallas kernels  16.9 us (7%)
    ppermute x48, waiting for transfers between devices, send(): return lax.ppermute(x, axis, perm)  95.2 us
    ppermute x48, starting transfers between devices, send(): return lax.ppermute(x, axis, perm)  79.1 us
    ppermute x4, starting transfers between devices, flip(): return lax.ppermute(x, ('row', 'col'), FLIP)  23.6 us
    pallas_call x6, Pallas kernels, products(): pl.pallas_call(functools.partial(product_kernel, backward, first, last, n...  16.9 us
    ppermute x4, waiting for transfers between devices, flip(): return lax.ppermute(x, ('row', 'col'), FLIP)  5.41 us
  transfers between devices with their start and end apart: 52, of which 39 were waited for; matrix products, arithmetic and copies ran while one was open for 0% of the time, Pallas kernels for 7%

profile of v2, /device:TPU:7, one launch (start us, length us, event | category | flops | bytes accessed | tf_op | source)
XLA Modules:
  0.0 225.5 jit_solution(8806953293737177958)
XLA Ops:
  3.1 221.8 %while.23 = (s32[]{:T(128)}, f32[2,96,128]{2,1,0:T(8,128)S(1)}, f32[2,96,128]{2,1,0:T(8,128)S(1)}, f32[2,96,128]{2,1,0:T(8,128)S(1)}, f32[]{:T(128)}, /*index=5*...) while((s32[]{:T(128)}, f32[2,96,128]{2,1,0:T(8,128)S(1)}, ...), condition=%wide.region_1.2_spmd.clone, body=%wide.region_0.1_spmd.clone.sunk | while | flops 13289054208 | bytes 61119224 | solution.py:280
  4.3 10.4 %collective-permute-start.4 = (f32[2,96,128]{2,1,0:T(8,128)S(1)}, f32[2,96,128]{2,1,0:T(8,128)S(1)}, u32[]{:S(2)}, u32[]{:S(2)}) collective-permute-start(f32[2,96,128]{2,1,0:T(8,128)S(1)} %get-tuple-element.670), channel_id=1, source_target_pairs={{0,0},{1,16},{2,32},{3,48},{4,64},{5,80},{6,96},{7,112},{8,128},{9... | collective-permute-start | bytes 294920 | tf_op jit(solution)/shard_map/while/body/eval_jaxpr/ppermute | solution.py:46
  15.9 1.5 collective-permute-start.2
  18.8 4.1 %collective-permute-done.5 = f32[2,96,128]{2,1,0:T(8,128)S(1)} collective-permute-done((f32[2,96,128]{2,1,0:T(8,128)S(1)}, f32[2,96,128]{2,1,0:T(8,128)S(1)}, u32[]{:S(2)}, u32[]{:S(2)}) %collective-permute-start.5) | collective-permute-done | bytes 98336 | tf_op jit(solution)/shard_map/while/body/eval_jaxpr/ppermute | solution.py:42
  22.9 2.2 collective-permute-done.2
  25.1 4.2 %collective-permute-done.3 = f32[4,96,128]{2,1,0:T(8,128)S(1)} collective-permute-done((f32[4,96,128]{2,1,0:T(8,128)S(1)}, f32[4,96,128]{2,1,0:T(8,128)S(1)}, u32[]{:S(2)}, u32[]{:S(2)}) %collective-permute-start.3) | collective-permute-done | bytes 196640 | tf_op jit(solution)/shard_map/while/body/eval_jaxpr/ppermute | solution.py:42
  32.0 2.7 %eval_jaxpr.18 = (bf16[32,96,256]{2,1,0:T(8,128)(2,1)S(1)}, f32[32,96,128]{2,1,0:T(8,128)S(1)}) custom-call(s32[1,1,176]{2,1,0:T(1,128)S(1)} %copy-done, s32[1,1,176]{2,1,0:T(1,128)S(1)} %copy-done.1, s32[3]{0:T(128)S(1)} %get-tuple-element.690.refs_2_, f32[1,1,176,128,128]{4,3,2,1,0:T(8,128)} %get-tuple-element.691.refs_3_, ...), custom_call_target="tpu_custom_call" | custom-call | flops 3321888768 | bytes 5767168 | tf_op jit(solution)/shard_map/while/body/eval_jaxpr/pallas_call | solution.py:198
  34.7 1.9 collective-permute-done.6.refs_5_
  36.6 1.4 collective-permute-done.7.refs_12_
  38.0 2.7 %collective-permute-start.9 = (f32[4,96,128]{2,1,0:T(8,128)S(1)}, f32[4,96,128]{2,1,0:T(8,128)S(1)}, u32[]{:S(2)}, u32[]{:S(2)}) collective-permute-start(f32[4,96,128]{2,1,0:T(8,128)S(1)} %collective-permute-done.6.refs_5_), channel_id=1, source_target_pairs={{0,14},{1,15},{2,0},{3,1},{4,2},{5,3},{6,4},{7,5},{8,6},{9,7},{10,... | collective-permute-start | bytes 589832 | tf_op jit(solution)/shard_map/while/body/eval_jaxpr/ppermute | solution.py:42
  40.7 2.8 %eval_jaxpr.19 = (f32[4,96,128]{2,1,0:T(8,128)S(1)}, f32[4,96,128]{2,1,0:T(8,128)S(1)}, f32[4,96,128]{2,1,0:T(8,128)S(1)}, f32[4,96,128]{2,1,0:T(8,128)S(1)}, f3...) custom-call(s32[1,1,176]{2,1,0:T(1,128)S(1)} %copy-done, ...), custom_call_target="tpu_custom_call" | custom-call | flops 3321888768 | bytes 5767168 | tf_op jit(solution)/shard_map/while/body/eval_jaxpr/pallas_call | solution.py:198
  44.6 2.7 %collective-permute-start.11 = (f32[6,96,128]{2,1,0:T(8,128)S(1)}, f32[6,96,128]{2,1,0:T(8,128)S(1)}, u32[]{:S(2)}, u32[]{:S(2)}) collective-permute-start(f32[6,96,128]{2,1,0:T(8,128)S(1)} %pad_maximum_fusion.8), channel_id=1, source_target_pairs={{0,14},{1,15},{2,0},{3,1},{4,2},{5,3},{6,4},{7,5},{8,6},{9,7},{10,... | collective-permute-start | bytes 884744 | tf_op jit(solution)/shard_map/while/body/eval_jaxpr/ppermute | solution.py:42
  47.4 4.0 %collective-permute-done.12.refs_10_ = f32[6,96,128]{2,1,0:T(8,128)S(1)} collective-permute-done((f32[6,96,128]{2,1,0:T(8,128)S(1)}, f32[6,96,128]{2,1,0:T(8,128)S(1)}, u32[]{:S(2)}, u32[]{:S(2)}) %collective-permute-start.12) | collective-permute-done | bytes 294944 | tf_op jit(solution)/shard_map/while/body/eval_jaxpr/ppermute | solution.py:42
  51.5 3.0 %collective-permute-start.14 = (f32[6,96,128]{2,1,0:T(8,128)S(1)}, f32[6,96,128]{2,1,0:T(8,128)S(1)}, u32[]{:S(2)}, u32[]{:S(2)}) collective-permute-start(f32[6,96,128]{2,1,0:T(8,128)S(1)} %pad_maximum_fusion.11), channel_id=1, source_target_pairs={{0,2},{1,3},{2,4},{3,5},{4,6},{5,7},{6,8},{7,9},{8,10},{9,11},{10,... | collective-permute-start | bytes 884744 | tf_op jit(solution)/shard_map/while/body/eval_jaxpr/ppermute | solution.py:42
  54.6 4.6 %collective-permute-done.14.refs_8_ = f32[6,96,128]{2,1,0:T(8,128)S(1)} collective-permute-done((f32[6,96,128]{2,1,0:T(8,128)S(1)}, f32[6,96,128]{2,1,0:T(8,128)S(1)}, u32[]{:S(2)}, u32[]{:S(2)}) %collective-permute-start.14) | collective-permute-done | bytes 294944 | tf_op jit(solution)/shard_map/while/body/eval_jaxpr/ppermute | solution.py:42
  59.2 1.4 collective-permute-done.13.refs_9_
  60.6 1.8 collective-permute-start.16
  62.4 2.6 %collective-permute-start.15 = (f32[4,96,128]{2,1,0:T(8,128)S(1)}, f32[4,96,128]{2,1,0:T(8,128)S(1)}, u32[]{:S(2)}, u32[]{:S(2)}) collective-permute-start(f32[4,96,128]{2,1,0:T(8,128)S(1)} %slice_add_fusion.21), channel_id=1, source_target_pairs={{0,2},{1,3},{2,4},{3,5},{4,6},{5,7},{6,8},{7,9},{8,10},{9,11},{10,... | collective-permute-start | bytes 589832 | tf_op jit(solution)/shard_map/while/body/eval_jaxpr/ppermute | solution.py:42
  65.0 2.9 %collective-permute-done.16 = f32[4,96,128]{2,1,0:T(8,128)S(1)} collective-permute-done((f32[4,96,128]{2,1,0:T(8,128)S(1)}, f32[4,96,128]{2,1,0:T(8,128)S(1)}, u32[]{:S(2)}, u32[]{:S(2)}) %collective-permute-start.16) | collective-permute-done | bytes 196640 | tf_op jit(solution)/shard_map/while/body/eval_jaxpr/ppermute | solution.py:42
  68.2 2.4 %collective-permute-start.18 = (f32[4,96,128]{2,1,0:T(8,128)S(1)}, f32[4,96,128]{2,1,0:T(8,128)S(1)}, u32[]{:S(2)}, u32[]{:S(2)}) collective-permute-start(f32[4,96,128]{2,1,0:T(8,128)S(1)} %add.333), channel_id=1, source_target_pairs={{0,14},{1,15},{2,0},{3,1},{4,2},{5,3},{6,4},{7,5},{8,6},{9,7},{10,... | collective-permute-start | bytes 589832 | tf_op jit(solution)/shard_map/while/body/eval_jaxpr/ppermute | solution.py:42
  70.7 3.0 %eval_jaxpr.20 = (f32[4,96,128]{2,1,0:T(8,128)S(1)}, f32[4,96,128]{2,1,0:T(8,128)S(1)}, f32[4,96,128]{2,1,0:T(8,128)S(1)}, f32[4,96,128]{2,1,0:T(8,128)S(1)}, f32[16,96,128]{2,1,0:T(8,128)S(1)}) custom-call(s32[1,1,176]{2,1,0:T(1,128)S(1)} %copy-done, s32[1,1,176]{2,1,0:T(1,128)S(1)} %copy-done.1, s32[3]{0:T(128)S(1)} %get-tuple-element.690.refs_2_, ...), custom_call_target="tpu_custom_call" | custom-call | flops 6643777536 | bytes 11534336 | tf_op jit(solution)/shard_map/while/body/eval_jaxpr/pallas_call | solution.py:198
  73.7 1.2 collective-permute-done.18
  75.0 2.6 %collective-permute-done.17 = f32[4,96,128]{2,1,0:T(8,128)S(1)} collective-permute-done((f32[4,96,128]{2,1,0:T(8,128)S(1)}, f32[4,96,128]{2,1,0:T(8,128)S(1)}, u32[]{:S(2)}, u32[]{:S(2)}) %collective-permute-start.17) | collective-permute-done | bytes 196640 | tf_op jit(solution)/shard_map/while/body/eval_jaxpr/ppermute | solution.py:42
  77.6 10.2 %collective-permute-start.19 = (f32[16,96,128]{2,1,0:T(8,128)S(1)}, f32[16,96,128]{2,1,0:T(8,128)S(1)}, u32[]{:S(2)}, u32[]{:S(2)}) collective-permute-start(f32[16,96,128]{2,1,0:T(8,128)S(1)} %get-tuple-element.642), channel_id=1, source_target_pairs={{0,16},{16,0},{32,48},{48,32},{64,80},{80,64},{96,112},{112,96},{1... | collective-permute-start | bytes 2359304 | tf_op jit(solution)/shard_map/while/body/eval_jaxpr/ppermute | solution.py:42
  88.0 1.8 collective-permute-done.19
  89.8 1.8 collective-permute-start.20
  92.3 5.9 %collective-permute-start.25 = (f32[2,96,128]{2,1,0:T(8,128)S(1)}, f32[2,96,128]{2,1,0:T(8,128)S(1)}, u32[]{:S(2)}, u32[]{:S(2)}) collective-permute-start(f32[2,96,128]{2,1,0:T(8,128)S(1)} %add_add_fusion.2), channel_id=1, source_target_pairs={{0,0},{1,16},{2,32},{3,48},{4,64},{5,80},{6,96},{7,112},{8,128},{9... | collective-permute-start | bytes 294920 | tf_op jit(solution)/shard_map/while/body/eval_jaxpr/ppermute | solution.py:46
  99.0 4.6 %collective-permute-done.22 = f32[4,96,128]{2,1,0:T(8,128)S(1)} collective-permute-done((f32[4,96,128]{2,1,0:T(8,128)S(1)}, f32[4,96,128]{2,1,0:T(8,128)S(1)}, u32[]{:S(2)}, u32[]{:S(2)}) %collective-permute-start.22) | collective-permute-done | bytes 196640 | tf_op jit(solution)/shard_map/while/body/eval_jaxpr/ppermute | solution.py:42
  103.6 4.2 %collective-permute-start.23 = (f32[2,96,128]{2,1,0:T(8,128)S(1)}, f32[2,96,128]{2,1,0:T(8,128)S(1)}, u32[]{:S(2)}, u32[]{:S(2)}) collective-permute-start(f32[2,96,128]{2,1,0:T(8,128)S(1)} %slice_add_fusion.24), channel_id=1, source_target_pairs={{0,128},{16,144},{32,160},{48,176},{64,192},{80,208},{96,224},{112... | collective-permute-start | bytes 294920 | tf_op jit(solution)/shard_map/while/body/eval_jaxpr/ppermute | solution.py:42
  107.8 5.4 %collective-permute-done.23 = f32[2,96,128]{2,1,0:T(8,128)S(1)} collective-permute-done((f32[2,96,128]{2,1,0:T(8,128)S(1)}, f32[2,96,128]{2,1,0:T(8,128)S(1)}, u32[]{:S(2)}, u32[]{:S(2)}) %collective-permute-start.23) | collective-permute-done | bytes 98336 | tf_op jit(solution)/shard_map/while/body/eval_jaxpr/ppermute | solution.py:42
  113.4 4.7 %collective-permute-start.4 = (f32[2,96,128]{2,1,0:T(8,128)S(1)}, f32[2,96,128]{2,1,0:T(8,128)S(1)}, u32[]{:S(2)}, u32[]{:S(2)}) collective-permute-start(f32[2,96,128]{2,1,0:T(8,128)S(1)} %get-tuple-element.670), channel_id=1, source_target_pairs={{0,0},{1,16},{2,32},{3,48},{4,64},{5,80},{6,96},{7,112},{8,128},{9... | collective-permute-start | bytes 294920 | tf_op jit(solution)/shard_map/while/body/eval_jaxpr/ppermute | solution.py:46
  118.2 2.2 collective-permute-done
  120.4 1.3 collective-permute-start.1
  122.3 4.2 %collective-permute-done.4 = f32[2,96,128]{2,1,0:T(8,128)S(1)} collective-permute-done((f32[2,96,128]{2,1,0:T(8,128)S(1)}, f32[2,96,128]{2,1,0:T(8,128)S(1)}, u32[]{:S(2)}, u32[]{:S(2)}) %collective-permute-start.4) | collective-permute-done | bytes 98336 | tf_op jit(solution)/shard_map/while/body/eval_jaxpr/ppermute | solution.py:46
  126.7 3.7 %collective-permute-done.5 = f32[2,96,128]{2,1,0:T(8,128)S(1)} collective-permute-done((f32[2,96,128]{2,1,0:T(8,128)S(1)}, f32[2,96,128]{2,1,0:T(8,128)S(1)}, u32[]{:S(2)}, u32[]{:S(2)}) %collective-permute-start.5) | collective-permute-done | bytes 98336 | tf_op jit(solution)/shard_map/while/body/eval_jaxpr/ppermute | solution.py:42
  131.4 2.2 collective-permute-done.3
  133.7 1.6 collective-permute-start.8
  135.4 1.9 collective-permute-start.6
  137.3 9.0 %collective-permute-start.7 = (f32[4,96,128]{2,1,0:T(8,128)S(1)}, f32[4,96,128]{2,1,0:T(8,128)S(1)}, u32[]{:S(2)}, u32[]{:S(2)}) collective-permute-start(f32[4,96,128]{2,1,0:T(8,128)S(1)} %constant_dynamic-update-slice_fusion.19.refs_4_), channel_id=1, source_target_pairs={{0,2},{1,3},{2,4},{3,5},{4,6},{5,7},{6,8},{7,9},{8,10},{9,11},{10,... | collective-permute-start | bytes 589832 | tf_op jit(solution)/shard_map/while/body/eval_jaxpr/ppermute | solution.py:42
  146.3 2.7 %eval_jaxpr.18 = (bf16[32,96,256]{2,1,0:T(8,128)(2,1)S(1)}, f32[32,96,128]{2,1,0:T(8,128)S(1)}) custom-call(s32[1,1,176]{2,1,0:T(1,128)S(1)} %copy-done, s32[1,1,176]{2,1,0:T(1,128)S(1)} %copy-done.1, s32[3]{0:T(128)S(1)} %get-tuple-element.690.refs_2_, f32[1,1,176,128,128]{4,3,2,1,0:T(8,128)} %get-tuple-element.691.refs_3_, ...), custom_call_target="tpu_custom_call" | custom-call | flops 3321888768 | bytes 5767168 | tf_op jit(solution)/shard_map/while/body/eval_jaxpr/pallas_call | solution.py:198
  149.0 2.5 %collective-permute-done.6.refs_5_ = f32[4,96,128]{2,1,0:T(8,128)S(1)} collective-permute-done((f32[4,96,128]{2,1,0:T(8,128)S(1)}, f32[4,96,128]{2,1,0:T(8,128)S(1)}, u32[]{:S(2)}, u32[]{:S(2)}) %collective-permute-start.6) | collective-permute-done | bytes 196640 | tf_op jit(solution)/shard_map/while/body/eval_jaxpr/ppermute | solution.py:42
  151.5 1.3 collective-permute-start.10
  152.7 1.4 collective-permute-start.9
  154.1 2.8 %eval_jaxpr.19 = (f32[4,96,128]{2,1,0:T(8,128)S(1)}, f32[4,96,128]{2,1,0:T(8,128)S(1)}, f32[4,96,128]{2,1,0:T(8,128)S(1)}, f32[4,96,128]{2,1,0:T(8,128)S(1)}, f3...) custom-call(s32[1,1,176]{2,1,0:T(1,128)S(1)} %copy-done, ...), custom_call_target="tpu_custom_call" | custom-call | flops 3321888768 | bytes 5767168 | tf_op jit(solution)/shard_map/while/body/eval_jaxpr/pallas_call | solution.py:198
  156.9 1.6 collective-permute-done.10.refs_11_
  159.3 2.1 collective-permute-start.11
  161.4 4.0 %collective-permute-done.12.refs_10_ = f32[6,96,128]{2,1,0:T(8,128)S(1)} collective-permute-done((f32[6,96,128]{2,1,0:T(8,128)S(1)}, f32[6,96,128]{2,1,0:T(8,128)S(1)}, u32[]{:S(2)}, u32[]{:S(2)}) %collective-permute-start.12) | collective-permute-done | bytes 294944 | tf_op jit(solution)/shard_map/while/body/eval_jaxpr/ppermute | solution.py:42
  165.5 1.6 collective-permute-start.14
  167.1 1.4 collective-permute-start.13
  168.5 4.0 %collective-permute-done.14.refs_8_ = f32[6,96,128]{2,1,0:T(8,128)S(1)} collective-permute-done((f32[6,96,128]{2,1,0:T(8,128)S(1)}, f32[6,96,128]{2,1,0:T(8,128)S(1)}, u32[]{:S(2)}, u32[]{:S(2)}) %collective-permute-start.14) | collective-permute-done | bytes 294944 | tf_op jit(solution)/shard_map/while/body/eval_jaxpr/ppermute | solution.py:42
  172.8 2.6 %collective-permute-start.16 = (f32[4,96,128]{2,1,0:T(8,128)S(1)}, f32[4,96,128]{2,1,0:T(8,128)S(1)}, u32[]{:S(2)}, u32[]{:S(2)}) collective-permute-start(f32[4,96,128]{2,1,0:T(8,128)S(1)} %slice_add_fusion.22), channel_id=1, source_target_pairs={{0,14},{1,15},{2,0},{3,1},{4,2},{5,3},{6,4},{7,5},{8,6},{9,7},{10,... | collective-permute-start | bytes 589832 | tf_op jit(solution)/shard_map/while/body/eval_jaxpr/ppermute | solution.py:42
  175.4 1.4 collective-permute-start.15
  176.8 2.9 %collective-permute-done.16 = f32[4,96,128]{2,1,0:T(8,128)S(1)} collective-permute-done((f32[4,96,128]{2,1,0:T(8,128)S(1)}, f32[4,96,128]{2,1,0:T(8,128)S(1)}, u32[]{:S(2)}, u32[]{:S(2)}) %collective-permute-start.16) | collective-permute-done | bytes 196640 | tf_op jit(solution)/shard_map/while/body/eval_jaxpr/ppermute | solution.py:42
  179.8 1.4 collective-permute-done.15
  181.2 1.2 collective-permute-start.18
  182.9 3.0 %eval_jaxpr.20 = (f32[4,96,128]{2,1,0:T(8,128)S(1)}, f32[4,96,128]{2,1,0:T(8,128)S(1)}, f32[4,96,128]{2,1,0:T(8,128)S(1)}, f32[4,96,128]{2,1,0:T(8,128)S(1)}, f32[16,96,128]{2,1,0:T(8,128)S(1)}) custom-call(s32[1,1,176]{2,1,0:T(1,128)S(1)} %copy-done, s32[1,1,176]{2,1,0:T(1,128)S(1)} %copy-done.1, s32[3]{0:T(128)S(1)} %get-tuple-element.690.refs_2_, ...), custom_call_target="tpu_custom_call" | custom-call | flops 6643777536 | bytes 11534336 | tf_op jit(solution)/shard_map/while/body/eval_jaxpr/pallas_call | solution.py:198
  186.9 3.2 %collective-permute-done.17 = f32[4,96,128]{2,1,0:T(8,128)S(1)} collective-permute-done((f32[4,96,128]{2,1,0:T(8,128)S(1)}, f32[4,96,128]{2,1,0:T(8,128)S(1)}, u32[]{:S(2)}, u32[]{:S(2)}) %collective-permute-start.17) | collective-permute-done | bytes 196640 | tf_op jit(solution)/shard_map/while/body/eval_jaxpr/ppermute | solution.py:42
  190.1 9.6 %collective-permute-start.19 = (f32[16,96,128]{2,1,0:T(8,128)S(1)}, f32[16,96,128]{2,1,0:T(8,128)S(1)}, u32[]{:S(2)}, u32[]{:S(2)}) collective-permute-start(f32[16,96,128]{2,1,0:T(8,128)S(1)} %get-tuple-element.642), channel_id=1, source_target_pairs={{0,16},{16,0},{32,48},{48,32},{64,80},{80,64},{96,112},{112,96},{1... | collective-permute-start | bytes 2359304 | tf_op jit(solution)/shard_map/while/body/eval_jaxpr/ppermute | solution.py:42
  199.8 1.8 collective-permute-done.19
  201.9 1.3 collective-permute-start.22
  204.1 2.6 %collective-permute-start.25 = (f32[2,96,128]{2,1,0:T(8,128)S(1)}, f32[2,96,128]{2,1,0:T(8,128)S(1)}, u32[]{:S(2)}, u32[]{:S(2)}) collective-permute-start(f32[2,96,128]{2,1,0:T(8,128)S(1)} %add_add_fusion.2), channel_id=1, source_target_pairs={{0,0},{1,16},{2,32},{3,48},{4,64},{5,80},{6,96},{7,112},{8,128},{9... | collective-permute-start | bytes 294920 | tf_op jit(solution)/shard_map/while/body/eval_jaxpr/ppermute | solution.py:46
  207.8 1.4 collective-permute-done.21
  209.2 5.2 %collective-permute-done.22 = f32[4,96,128]{2,1,0:T(8,128)S(1)} collective-permute-done((f32[4,96,128]{2,1,0:T(8,128)S(1)}, f32[4,96,128]{2,1,0:T(8,128)S(1)}, u32[]{:S(2)}, u32[]{:S(2)}) %collective-permute-start.22) | collective-permute-done | bytes 196640 | tf_op jit(solution)/shard_map/while/body/eval_jaxpr/ppermute | solution.py:42
  214.9 9.8 %collective-permute-done.23 = f32[2,96,128]{2,1,0:T(8,128)S(1)} collective-permute-done((f32[2,96,128]{2,1,0:T(8,128)S(1)}, f32[2,96,128]{2,1,0:T(8,128)S(1)}, u32[]{:S(2)}, u32[]{:S(2)}) %collective-permute-start.23) | collective-permute-done | bytes 98336 | tf_op jit(solution)/shard_map/while/body/eval_jaxpr/ppermute | solution.py:42
  (114 shorter events, 19.3 us)
Async XLA Ops:
  3.1 28.9 %copy-start = (s32[1,1,176]{2,1,0:T(1,128)S(1)}, s32[1,1,176]{2,1,0:T(1,128)}, u32[]{:S(2)}) copy-start(s32[1,1,176]{2,1,0:T(1,128)} %get-tuple-element.688.refs_0_) | copy-start | bytes 2116 | tf_op jit(solution)/shard_map/while
  3.1 28.9 %copy-start.1 = (s32[1,1,176]{2,1,0:T(1,128)S(1)}, s32[1,1,176]{2,1,0:T(1,128)}, u32[]{:S(2)}) copy-start(s32[1,1,176]{2,1,0:T(1,128)} %get-tuple-element.689.refs_1_) | copy-start | bytes 2116 | tf_op jit(solution)/shard_map/while
  3.1 11.6 %collective-permute-start = (f32[2,96,128]{2,1,0:T(8,128)S(1)}, f32[2,96,128]{2,1,0:T(8,128)S(1)}, u32[]{:S(2)}, u32[]{:S(2)}) collective-permute-start(f32[2,96,128]{2,1,0:T(8,128)S(1)} %copy.29), channel_id=1, source_target_pairs={{0,128},{16,144},{32,160},{48,176},{64,192},{80,208},{96,224},{112... | collective-permute-start | bytes 294920 | tf_op jit(solution)/shard_map/while/body/eval_jaxpr/ppermute | solution.py:42
  4.3 14.3 %collective-permute-start.4 = (f32[2,96,128]{2,1,0:T(8,128)S(1)}, f32[2,96,128]{2,1,0:T(8,128)S(1)}, u32[]{:S(2)}, u32[]{:S(2)}) collective-permute-start(f32[2,96,128]{2,1,0:T(8,128)S(1)} %get-tuple-element.670), channel_id=1, source_target_pairs={{0,0},{1,16},{2,32},{3,48},{4,64},{5,80},{6,96},{7,112},{8,128},{9... | collective-permute-start | bytes 294920 | tf_op jit(solution)/shard_map/while/body/eval_jaxpr/ppermute | solution.py:46
  14.7 8.2 %collective-permute-start.1 = (f32[4,96,128]{2,1,0:T(8,128)S(1)}, f32[4,96,128]{2,1,0:T(8,128)S(1)}, u32[]{:S(2)}, u32[]{:S(2)}) collective-permute-start(f32[4,96,128]{2,1,0:T(8,128)S(1)} %get-tuple-element.591), channel_id=1, source_target_pairs={{0,96},{16,112},{32,0},{48,16},{64,32},{80,48},{96,64},{112,80},{1... | collective-permute-start | bytes 589832 | tf_op jit(solution)/shard_map/while/body/eval_jaxpr/ppermute | solution.py:42
  15.9 9.3 %collective-permute-start.2 = (f32[4,96,128]{2,1,0:T(8,128)S(1)}, f32[4,96,128]{2,1,0:T(8,128)S(1)}, u32[]{:S(2)}, u32[]{:S(2)}) collective-permute-start(f32[4,96,128]{2,1,0:T(8,128)S(1)} %get-tuple-element.591), channel_id=1, source_target_pairs={{0,64},{16,80},{32,96},{48,112},{64,0},{80,16},{96,32},{112,48},{1... | collective-permute-start | bytes 589832 | tf_op jit(solution)/shard_map/while/body/eval_jaxpr/ppermute | solution.py:42
  17.3 12.0 %collective-permute-start.3 = (f32[4,96,128]{2,1,0:T(8,128)S(1)}, f32[4,96,128]{2,1,0:T(8,128)S(1)}, u32[]{:S(2)}, u32[]{:S(2)}) collective-permute-start(f32[4,96,128]{2,1,0:T(8,128)S(1)} %get-tuple-element.591), channel_id=1, source_target_pairs={{0,32},{16,48},{32,64},{48,80},{64,96},{80,112},{96,0},{112,16},{1... | collective-permute-start | bytes 589832 | tf_op jit(solution)/shard_map/while/body/eval_jaxpr/ppermute | solution.py:42
  18.7 4.2 %collective-permute-start.5 = (f32[2,96,128]{2,1,0:T(8,128)S(1)}, f32[2,96,128]{2,1,0:T(8,128)S(1)}, u32[]{:S(2)}, u32[]{:S(2)}) collective-permute-start(f32[2,96,128]{2,1,0:T(8,128)S(1)} %select_add_fusion.2), channel_id=1, source_target_pairs={{0,1},{1,0},{2,3},{3,2},{4,5},{5,4},{6,7},{7,6},{8,9},{9,8},{10,11... | collective-permute-start | bytes 294920 | tf_op jit(solution)/shard_map/while/body/eval_jaxpr/ppermute | solution.py:42
  29.4 2.6 %collective-permute-start.8 = (f32[16,96,128]{2,1,0:T(8,128)S(1)}, f32[16,96,128]{2,1,0:T(8,128)S(1)}, u32[]{:S(2)}, u32[]{:S(2)}) collective-permute-start(f32[16,96,128]{2,1,0:T(8,128)S(1)} %constant_dynamic-update-slice_fusion.22.refs_4_), channel_id=1, source_target_pairs={{0,16},{16,0},{32,48},{48,32},{64,80},{80,64},{96,112},{112,96},{1... | collective-permute-start | bytes 2359304 | tf_op jit(solution)/shard_map/while/body/eval_jaxpr/ppermute | solution.py:42
  30.1 6.5 %collective-permute-start.6 = (f32[4,96,128]{2,1,0:T(8,128)S(1)}, f32[4,96,128]{2,1,0:T(8,128)S(1)}, u32[]{:S(2)}, u32[]{:S(2)}) collective-permute-start(f32[4,96,128]{2,1,0:T(8,128)S(1)} %constant_dynamic-update-slice_fusion.19.refs_4_), channel_id=1, source_target_pairs={{0,14},{1,15},{2,0},{3,1},{4,2},{5,3},{6,4},{7,5},{8,6},{9,7},{10,... | collective-permute-start | bytes 589832 | tf_op jit(solution)/shard_map/while/body/eval_jaxpr/ppermute | solution.py:42
  30.6 7.4 %collective-permute-start.7 = (f32[4,96,128]{2,1,0:T(8,128)S(1)}, f32[4,96,128]{2,1,0:T(8,128)S(1)}, u32[]{:S(2)}, u32[]{:S(2)}) collective-permute-start(f32[4,96,128]{2,1,0:T(8,128)S(1)} %constant_dynamic-update-slice_fusion.19.refs_4_), channel_id=1, source_target_pairs={{0,2},{1,3},{2,4},{3,5},{4,6},{5,7},{6,8},{7,9},{8,10},{9,11},{10,... | collective-permute-start | bytes 589832 | tf_op jit(solution)/shard_map/while/body/eval_jaxpr/ppermute | solution.py:42
  38.0 6.5 %collective-permute-start.10 = (f32[4,96,128]{2,1,0:T(8,128)S(1)}, f32[4,96,128]{2,1,0:T(8,128)S(1)}, u32[]{:S(2)}, u32[]{:S(2)}) collective-permute-start(f32[4,96,128]{2,1,0:T(8,128)S(1)} %collective-permute-done.7.refs_12_), channel_id=1, source_target_pairs={{0,2},{1,3},{2,4},{3,5},{4,6},{5,7},{6,8},{7,9},{8,10},{9,11},{10,... | collective-permute-start | bytes 589832 | tf_op jit(solution)/shard_map/while/body/eval_jaxpr/ppermute | solution.py:42
  38.0 6.5 %collective-permute-start.9 = (f32[4,96,128]{2,1,0:T(8,128)S(1)}, f32[4,96,128]{2,1,0:T(8,128)S(1)}, u32[]{:S(2)}, u32[]{:S(2)}) collective-permute-start(f32[4,96,128]{2,1,0:T(8,128)S(1)} %collective-permute-done.6.refs_5_), channel_id=1, source_target_pairs={{0,14},{1,15},{2,0},{3,1},{4,2},{5,3},{6,4},{7,5},{8,6},{9,7},{10,... | collective-permute-start | bytes 589832 | tf_op jit(solution)/shard_map/while/body/eval_jaxpr/ppermute | solution.py:42
  44.5 6.9 %collective-permute-start.12 = (f32[6,96,128]{2,1,0:T(8,128)S(1)}, f32[6,96,128]{2,1,0:T(8,128)S(1)}, u32[]{:S(2)}, u32[]{:S(2)}) collective-permute-start(f32[6,96,128]{2,1,0:T(8,128)S(1)} %pad_maximum_fusion.9), channel_id=1, source_target_pairs={{0,2},{1,3},{2,4},{3,5},{4,6},{5,7},{6,8},{7,9},{8,10},{9,11},{10,... | collective-permute-start | bytes 884744 | tf_op jit(solution)/shard_map/while/body/eval_jaxpr/ppermute | solution.py:42
  44.6 6.7 %collective-permute-start.11 = (f32[6,96,128]{2,1,0:T(8,128)S(1)}, f32[6,96,128]{2,1,0:T(8,128)S(1)}, u32[]{:S(2)}, u32[]{:S(2)}) collective-permute-start(f32[6,96,128]{2,1,0:T(8,128)S(1)} %pad_maximum_fusion.8), channel_id=1, source_target_pairs={{0,14},{1,15},{2,0},{3,1},{4,2},{5,3},{6,4},{7,5},{8,6},{9,7},{10,... | collective-permute-start | bytes 884744 | tf_op jit(solution)/shard_map/while/body/eval_jaxpr/ppermute | solution.py:42
  51.5 7.8 %collective-permute-start.14 = (f32[6,96,128]{2,1,0:T(8,128)S(1)}, f32[6,96,128]{2,1,0:T(8,128)S(1)}, u32[]{:S(2)}, u32[]{:S(2)}) collective-permute-start(f32[6,96,128]{2,1,0:T(8,128)S(1)} %pad_maximum_fusion.11), channel_id=1, source_target_pairs={{0,2},{1,3},{2,4},{3,5},{4,6},{5,7},{6,8},{7,9},{8,10},{9,11},{10,... | collective-permute-start | bytes 884744 | tf_op jit(solution)/shard_map/while/body/eval_jaxpr/ppermute | solution.py:42
  54.5 6.1 %collective-permute-start.13 = (f32[6,96,128]{2,1,0:T(8,128)S(1)}, f32[6,96,128]{2,1,0:T(8,128)S(1)}, u32[]{:S(2)}, u32[]{:S(2)}) collective-permute-start(f32[6,96,128]{2,1,0:T(8,128)S(1)} %pad_maximum_fusion.10), channel_id=1, source_target_pairs={{0,14},{1,15},{2,0},{3,1},{4,2},{5,3},{6,4},{7,5},{8,6},{9,7},{10,... | collective-permute-start | bytes 884744 | tf_op jit(solution)/shard_map/while/body/eval_jaxpr/ppermute | solution.py:42
  60.6 7.3 %collective-permute-start.16 = (f32[4,96,128]{2,1,0:T(8,128)S(1)}, f32[4,96,128]{2,1,0:T(8,128)S(1)}, u32[]{:S(2)}, u32[]{:S(2)}) collective-permute-start(f32[4,96,128]{2,1,0:T(8,128)S(1)} %slice_add_fusion.22), channel_id=1, source_target_pairs={{0,14},{1,15},{2,0},{3,1},{4,2},{5,3},{6,4},{7,5},{8,6},{9,7},{10,... | collective-permute-start | bytes 589832 | tf_op jit(solution)/shard_map/while/body/eval_jaxpr/ppermute | solution.py:42
  62.4 5.8 %collective-permute-start.15 = (f32[4,96,128]{2,1,0:T(8,128)S(1)}, f32[4,96,128]{2,1,0:T(8,128)S(1)}, u32[]{:S(2)}, u32[]{:S(2)}) collective-permute-start(f32[4,96,128]{2,1,0:T(8,128)S(1)} %slice_add_fusion.21), channel_id=1, source_target_pairs={{0,2},{1,3},{2,4},{3,5},{4,6},{5,7},{6,8},{7,9},{8,10},{9,11},{10,... | collective-permute-start | bytes 589832 | tf_op jit(solution)/shard_map/while/body/eval_jaxpr/ppermute | solution.py:42
  68.2 6.7 %collective-permute-start.18 = (f32[4,96,128]{2,1,0:T(8,128)S(1)}, f32[4,96,128]{2,1,0:T(8,128)S(1)}, u32[]{:S(2)}, u32[]{:S(2)}) collective-permute-start(f32[4,96,128]{2,1,0:T(8,128)S(1)} %add.333), channel_id=1, source_target_pairs={{0,14},{1,15},{2,0},{3,1},{4,2},{5,3},{6,4},{7,5},{8,6},{9,7},{10,... | collective-permute-start | bytes 589832 | tf_op jit(solution)/shard_map/while/body/eval_jaxpr/ppermute | solution.py:42
  70.6 7.0 %collective-permute-start.17 = (f32[4,96,128]{2,1,0:T(8,128)S(1)}, f32[4,96,128]{2,1,0:T(8,128)S(1)}, u32[]{:S(2)}, u32[]{:S(2)}) collective-permute-start(f32[4,96,128]{2,1,0:T(8,128)S(1)} %add.332), channel_id=1, source_target_pairs={{0,2},{1,3},{2,4},{3,5},{4,6},{5,7},{6,8},{7,9},{8,10},{9,11},{10,... | collective-permute-start | bytes 589832 | tf_op jit(solution)/shard_map/while/body/eval_jaxpr/ppermute | solution.py:42
  77.6 12.2 %collective-permute-start.19 = (f32[16,96,128]{2,1,0:T(8,128)S(1)}, f32[16,96,128]{2,1,0:T(8,128)S(1)}, u32[]{:S(2)}, u32[]{:S(2)}) collective-permute-start(f32[16,96,128]{2,1,0:T(8,128)S(1)} %get-tuple-element.642), channel_id=1, source_target_pairs={{0,16},{16,0},{32,48},{48,32},{64,80},{80,64},{96,112},{112,96},{1... | collective-permute-start | bytes 2359304 | tf_op jit(solution)/shard_map/while/body/eval_jaxpr/ppermute | solution.py:42
  87.9 4.4 %collective-permute-start.24 = (f32[2,96,128]{2,1,0:T(8,128)S(1)}, f32[2,96,128]{2,1,0:T(8,128)S(1)}, u32[]{:S(2)}, u32[]{:S(2)}) collective-permute-start(f32[2,96,128]{2,1,0:T(8,128)S(1)} %slice_add_fusion.25), channel_id=1, source_target_pairs={{0,1},{1,0},{2,3},{3,2},{4,5},{5,4},{6,7},{7,6},{8,9},{9,8},{10,11... | collective-permute-start | bytes 294920 | tf_op jit(solution)/shard_map/while/body/eval_jaxpr/ppermute | solution.py:42
  89.8 8.4 %collective-permute-start.20 = (f32[4,96,128]{2,1,0:T(8,128)S(1)}, f32[4,96,128]{2,1,0:T(8,128)S(1)}, u32[]{:S(2)}, u32[]{:S(2)}) collective-permute-start(f32[4,96,128]{2,1,0:T(8,128)S(1)} %get-tuple-element.645), channel_id=1, source_target_pairs={{0,96},{16,112},{32,0},{48,16},{64,32},{80,48},{96,64},{112,80},{1... | collective-permute-start | bytes 589832 | tf_op jit(solution)/shard_map/while/body/eval_jaxpr/ppermute | solution.py:42
  91.6 7.4 %collective-permute-start.21 = (f32[4,96,128]{2,1,0:T(8,128)S(1)}, f32[4,96,128]{2,1,0:T(8,128)S(1)}, u32[]{:S(2)}, u32[]{:S(2)}) collective-permute-start(f32[4,96,128]{2,1,0:T(8,128)S(1)} %get-tuple-element.646), channel_id=1, source_target_pairs={{0,64},{16,80},{32,96},{48,112},{64,0},{80,16},{96,32},{112,48},{1... | collective-permute-start | bytes 589832 | tf_op jit(solution)/shard_map/while/body/eval_jaxpr/ppermute | solution.py:42
  91.6 12.0 %collective-permute-start.22 = (f32[4,96,128]{2,1,0:T(8,128)S(1)}, f32[4,96,128]{2,1,0:T(8,128)S(1)}, u32[]{:S(2)}, u32[]{:S(2)}) collective-permute-start(f32[4,96,128]{2,1,0:T(8,128)S(1)} %get-tuple-element.647), channel_id=1, source_target_pairs={{0,32},{16,48},{32,64},{48,80},{64,96},{80,112},{96,0},{112,16},{1... | collective-permute-start | bytes 589832 | tf_op jit(solution)/shard_map/while/body/eval_jaxpr/ppermute | solution.py:42
  92.3 20.9 %collective-permute-start.25 = (f32[2,96,128]{2,1,0:T(8,128)S(1)}, f32[2,96,128]{2,1,0:T(8,128)S(1)}, u32[]{:S(2)}, u32[]{:S(2)}) collective-permute-start(f32[2,96,128]{2,1,0:T(8,128)S(1)} %add_add_fusion.2), channel_id=1, source_target_pairs={{0,0},{1,16},{2,32},{3,48},{4,64},{5,80},{6,96},{7,112},{8,128},{9... | collective-permute-start | bytes 294920 | tf_op jit(solution)/shard_map/while/body/eval_jaxpr/ppermute | solution.py:46
  103.6 9.6 %collective-permute-start.23 = (f32[2,96,128]{2,1,0:T(8,128)S(1)}, f32[2,96,128]{2,1,0:T(8,128)S(1)}, u32[]{:S(2)}, u32[]{:S(2)}) collective-permute-start(f32[2,96,128]{2,1,0:T(8,128)S(1)} %slice_add_fusion.24), channel_id=1, source_target_pairs={{0,128},{16,144},{32,160},{48,176},{64,192},{80,208},{96,224},{112... | collective-permute-start | bytes 294920 | tf_op jit(solution)/shard_map/while/body/eval_jaxpr/ppermute | solution.py:42
  113.3 33.0 %copy-start = (s32[1,1,176]{2,1,0:T(1,128)S(1)}, s32[1,1,176]{2,1,0:T(1,128)}, u32[]{:S(2)}) copy-start(s32[1,1,176]{2,1,0:T(1,128)} %get-tuple-element.688.refs_0_) | copy-start | bytes 2116 | tf_op jit(solution)/shard_map/while
  113.3 33.0 %copy-start.1 = (s32[1,1,176]{2,1,0:T(1,128)S(1)}, s32[1,1,176]{2,1,0:T(1,128)}, u32[]{:S(2)}) copy-start(s32[1,1,176]{2,1,0:T(1,128)} %get-tuple-element.689.refs_1_) | copy-start | bytes 2116 | tf_op jit(solution)/shard_map/while
  113.3 7.0 %collective-permute-start = (f32[2,96,128]{2,1,0:T(8,128)S(1)}, f32[2,96,128]{2,1,0:T(8,128)S(1)}, u32[]{:S(2)}, u32[]{:S(2)}) collective-permute-start(f32[2,96,128]{2,1,0:T(8,128)S(1)} %copy.29), channel_id=1, source_target_pairs={{0,128},{16,144},{32,160},{48,176},{64,192},{80,208},{96,224},{112... | collective-permute-start | bytes 294920 | tf_op jit(solution)/shard_map/while/body/eval_jaxpr/ppermute | solution.py:42
  113.4 13.1 %collective-permute-start.4 = (f32[2,96,128]{2,1,0:T(8,128)S(1)}, f32[2,96,128]{2,1,0:T(8,128)S(1)}, u32[]{:S(2)}, u32[]{:S(2)}) collective-permute-start(f32[2,96,128]{2,1,0:T(8,128)S(1)} %get-tuple-element.670), channel_id=1, source_target_pairs={{0,0},{1,16},{2,32},{3,48},{4,64},{5,80},{6,96},{7,112},{8,128},{9... | collective-permute-start | bytes 294920 | tf_op jit(solution)/shard_map/while/body/eval_jaxpr/ppermute | solution.py:46
  120.4 11.0 %collective-permute-start.1 = (f32[4,96,128]{2,1,0:T(8,128)S(1)}, f32[4,96,128]{2,1,0:T(8,128)S(1)}, u32[]{:S(2)}, u32[]{:S(2)}) collective-permute-start(f32[4,96,128]{2,1,0:T(8,128)S(1)} %get-tuple-element.591), channel_id=1, source_target_pairs={{0,96},{16,112},{32,0},{48,16},{64,32},{80,48},{96,64},{112,80},{1... | collective-permute-start | bytes 589832 | tf_op jit(solution)/shard_map/while/body/eval_jaxpr/ppermute | solution.py:42
  121.7 9.7 %collective-permute-start.2 = (f32[4,96,128]{2,1,0:T(8,128)S(1)}, f32[4,96,128]{2,1,0:T(8,128)S(1)}, u32[]{:S(2)}, u32[]{:S(2)}) collective-permute-start(f32[4,96,128]{2,1,0:T(8,128)S(1)} %get-tuple-element.591), channel_id=1, source_target_pairs={{0,64},{16,80},{32,96},{48,112},{64,0},{80,16},{96,32},{112,48},{1... | collective-permute-start | bytes 589832 | tf_op jit(solution)/shard_map/while/body/eval_jaxpr/ppermute | solution.py:42
  121.7 12.0 %collective-permute-start.3 = (f32[4,96,128]{2,1,0:T(8,128)S(1)}, f32[4,96,128]{2,1,0:T(8,128)S(1)}, u32[]{:S(2)}, u32[]{:S(2)}) collective-permute-start(f32[4,96,128]{2,1,0:T(8,128)S(1)} %get-tuple-element.591), channel_id=1, source_target_pairs={{0,32},{16,48},{32,64},{48,80},{64,96},{80,112},{96,0},{112,16},{1... | collective-permute-start | bytes 589832 | tf_op jit(solution)/shard_map/while/body/eval_jaxpr/ppermute | solution.py:42
  126.6 3.8 %collective-permute-start.5 = (f32[2,96,128]{2,1,0:T(8,128)S(1)}, f32[2,96,128]{2,1,0:T(8,128)S(1)}, u32[]{:S(2)}, u32[]{:S(2)}) collective-permute-start(f32[2,96,128]{2,1,0:T(8,128)S(1)} %select_add_fusion.2), channel_id=1, source_target_pairs={{0,1},{1,0},{2,3},{3,2},{4,5},{5,4},{6,7},{7,6},{8,9},{9,8},{10,11... | collective-permute-start | bytes 294920 | tf_op jit(solution)/shard_map/while/body/eval_jaxpr/ppermute | solution.py:42
  133.7 12.6 %collective-permute-start.8 = (f32[16,96,128]{2,1,0:T(8,128)S(1)}, f32[16,96,128]{2,1,0:T(8,128)S(1)}, u32[]{:S(2)}, u32[]{:S(2)}) collective-permute-start(f32[16,96,128]{2,1,0:T(8,128)S(1)} %constant_dynamic-update-slice_fusion.22.refs_4_), channel_id=1, source_target_pairs={{0,16},{16,0},{32,48},{48,32},{64,80},{80,64},{96,112},{112,96},{1... | collective-permute-start | bytes 2359304 | tf_op jit(solution)/shard_map/while/body/eval_jaxpr/ppermute | solution.py:42
  135.4 16.1 %collective-permute-start.6 = (f32[4,96,128]{2,1,0:T(8,128)S(1)}, f32[4,96,128]{2,1,0:T(8,128)S(1)}, u32[]{:S(2)}, u32[]{:S(2)}) collective-permute-start(f32[4,96,128]{2,1,0:T(8,128)S(1)} %constant_dynamic-update-slice_fusion.19.refs_4_), channel_id=1, source_target_pairs={{0,14},{1,15},{2,0},{3,1},{4,2},{5,3},{6,4},{7,5},{8,6},{9,7},{10,... | collective-permute-start | bytes 589832 | tf_op jit(solution)/shard_map/while/body/eval_jaxpr/ppermute | solution.py:42
  137.3 14.2 %collective-permute-start.7 = (f32[4,96,128]{2,1,0:T(8,128)S(1)}, f32[4,96,128]{2,1,0:T(8,128)S(1)}, u32[]{:S(2)}, u32[]{:S(2)}) collective-permute-start(f32[4,96,128]{2,1,0:T(8,128)S(1)} %constant_dynamic-update-slice_fusion.19.refs_4_), channel_id=1, source_target_pairs={{0,2},{1,3},{2,4},{3,5},{4,6},{5,7},{6,8},{7,9},{8,10},{9,11},{10,... | collective-permute-start | bytes 589832 | tf_op jit(solution)/shard_map/while/body/eval_jaxpr/ppermute | solution.py:42
  151.5 7.1 %collective-permute-start.10 = (f32[4,96,128]{2,1,0:T(8,128)S(1)}, f32[4,96,128]{2,1,0:T(8,128)S(1)}, u32[]{:S(2)}, u32[]{:S(2)}) collective-permute-start(f32[4,96,128]{2,1,0:T(8,128)S(1)} %collective-permute-done.7.refs_12_), channel_id=1, source_target_pairs={{0,2},{1,3},{2,4},{3,5},{4,6},{5,7},{6,8},{7,9},{8,10},{9,11},{10,... | collective-permute-start | bytes 589832 | tf_op jit(solution)/shard_map/while/body/eval_jaxpr/ppermute | solution.py:42
  152.7 5.8 %collective-permute-start.9 = (f32[4,96,128]{2,1,0:T(8,128)S(1)}, f32[4,96,128]{2,1,0:T(8,128)S(1)}, u32[]{:S(2)}, u32[]{:S(2)}) collective-permute-start(f32[4,96,128]{2,1,0:T(8,128)S(1)} %collective-permute-done.6.refs_5_), channel_id=1, source_target_pairs={{0,14},{1,15},{2,0},{3,1},{4,2},{5,3},{6,4},{7,5},{8,6},{9,7},{10,... | collective-permute-start | bytes 589832 | tf_op jit(solution)/shard_map/while/body/eval_jaxpr/ppermute | solution.py:42
  158.6 6.9 %collective-permute-start.12 = (f32[6,96,128]{2,1,0:T(8,128)S(1)}, f32[6,96,128]{2,1,0:T(8,128)S(1)}, u32[]{:S(2)}, u32[]{:S(2)}) collective-permute-start(f32[6,96,128]{2,1,0:T(8,128)S(1)} %pad_maximum_fusion.9), channel_id=1, source_target_pairs={{0,2},{1,3},{2,4},{3,5},{4,6},{5,7},{6,8},{7,9},{8,10},{9,11},{10,... | collective-permute-start | bytes 884744 | tf_op jit(solution)/shard_map/while/body/eval_jaxpr/ppermute | solution.py:42
  159.3 6.1 %collective-permute-start.11 = (f32[6,96,128]{2,1,0:T(8,128)S(1)}, f32[6,96,128]{2,1,0:T(8,128)S(1)}, u32[]{:S(2)}, u32[]{:S(2)}) collective-permute-start(f32[6,96,128]{2,1,0:T(8,128)S(1)} %pad_maximum_fusion.8), channel_id=1, source_target_pairs={{0,14},{1,15},{2,0},{3,1},{4,2},{5,3},{6,4},{7,5},{8,6},{9,7},{10,... | collective-permute-start | bytes 884744 | tf_op jit(solution)/shard_map/while/body/eval_jaxpr/ppermute | solution.py:42
  165.5 7.0 %collective-permute-start.14 = (f32[6,96,128]{2,1,0:T(8,128)S(1)}, f32[6,96,128]{2,1,0:T(8,128)S(1)}, u32[]{:S(2)}, u32[]{:S(2)}) collective-permute-start(f32[6,96,128]{2,1,0:T(8,128)S(1)} %pad_maximum_fusion.11), channel_id=1, source_target_pairs={{0,2},{1,3},{2,4},{3,5},{4,6},{5,7},{6,8},{7,9},{8,10},{9,11},{10,... | collective-permute-start | bytes 884744 | tf_op jit(solution)/shard_map/while/body/eval_jaxpr/ppermute | solution.py:42
  167.1 5.7 %collective-permute-start.13 = (f32[6,96,128]{2,1,0:T(8,128)S(1)}, f32[6,96,128]{2,1,0:T(8,128)S(1)}, u32[]{:S(2)}, u32[]{:S(2)}) collective-permute-start(f32[6,96,128]{2,1,0:T(8,128)S(1)} %pad_maximum_fusion.10), channel_id=1, source_target_pairs={{0,14},{1,15},{2,0},{3,1},{4,2},{5,3},{6,4},{7,5},{8,6},{9,7},{10,... | collective-permute-start | bytes 884744 | tf_op jit(solution)/shard_map/while/body/eval_jaxpr/ppermute | solution.py:42
  172.8 7.0 %collective-permute-start.16 = (f32[4,96,128]{2,1,0:T(8,128)S(1)}, f32[4,96,128]{2,1,0:T(8,128)S(1)}, u32[]{:S(2)}, u32[]{:S(2)}) collective-permute-start(f32[4,96,128]{2,1,0:T(8,128)S(1)} %slice_add_fusion.22), channel_id=1, source_target_pairs={{0,14},{1,15},{2,0},{3,1},{4,2},{5,3},{6,4},{7,5},{8,6},{9,7},{10,... | collective-permute-start | bytes 589832 | tf_op jit(solution)/shard_map/while/body/eval_jaxpr/ppermute | solution.py:42
  175.4 5.8 %collective-permute-start.15 = (f32[4,96,128]{2,1,0:T(8,128)S(1)}, f32[4,96,128]{2,1,0:T(8,128)S(1)}, u32[]{:S(2)}, u32[]{:S(2)}) collective-permute-start(f32[4,96,128]{2,1,0:T(8,128)S(1)} %slice_add_fusion.21), channel_id=1, source_target_pairs={{0,2},{1,3},{2,4},{3,5},{4,6},{5,7},{6,8},{7,9},{8,10},{9,11},{10,... | collective-permute-start | bytes 589832 | tf_op jit(solution)/shard_map/while/body/eval_jaxpr/ppermute | solution.py:42
  181.2 5.7 %collective-permute-start.18 = (f32[4,96,128]{2,1,0:T(8,128)S(1)}, f32[4,96,128]{2,1,0:T(8,128)S(1)}, u32[]{:S(2)}, u32[]{:S(2)}) collective-permute-start(f32[4,96,128]{2,1,0:T(8,128)S(1)} %add.333), channel_id=1, source_target_pairs={{0,14},{1,15},{2,0},{3,1},{4,2},{5,3},{6,4},{7,5},{8,6},{9,7},{10,... | collective-permute-start | bytes 589832 | tf_op jit(solution)/shard_map/while/body/eval_jaxpr/ppermute | solution.py:42
  182.5 7.6 %collective-permute-start.17 = (f32[4,96,128]{2,1,0:T(8,128)S(1)}, f32[4,96,128]{2,1,0:T(8,128)S(1)}, u32[]{:S(2)}, u32[]{:S(2)}) collective-permute-start(f32[4,96,128]{2,1,0:T(8,128)S(1)} %add.332), channel_id=1, source_target_pairs={{0,2},{1,3},{2,4},{3,5},{4,6},{5,7},{6,8},{7,9},{8,10},{9,11},{10,... | collective-permute-start | bytes 589832 | tf_op jit(solution)/shard_map/while/body/eval_jaxpr/ppermute | solution.py:42
  190.1 11.5 %collective-permute-start.19 = (f32[16,96,128]{2,1,0:T(8,128)S(1)}, f32[16,96,128]{2,1,0:T(8,128)S(1)}, u32[]{:S(2)}, u32[]{:S(2)}) collective-permute-start(f32[16,96,128]{2,1,0:T(8,128)S(1)} %get-tuple-element.642), channel_id=1, source_target_pairs={{0,16},{16,0},{32,48},{48,32},{64,80},{80,64},{96,112},{112,96},{1... | collective-permute-start | bytes 2359304 | tf_op jit(solution)/shard_map/while/body/eval_jaxpr/ppermute | solution.py:42
  199.7 4.4 %collective-permute-start.24 = (f32[2,96,128]{2,1,0:T(8,128)S(1)}, f32[2,96,128]{2,1,0:T(8,128)S(1)}, u32[]{:S(2)}, u32[]{:S(2)}) collective-permute-start(f32[2,96,128]{2,1,0:T(8,128)S(1)} %slice_add_fusion.25), channel_id=1, source_target_pairs={{0,1},{1,0},{2,3},{3,2},{4,5},{5,4},{6,7},{7,6},{8,9},{9,8},{10,11... | collective-permute-start | bytes 294920 | tf_op jit(solution)/shard_map/while/body/eval_jaxpr/ppermute | solution.py:42
  201.7 6.2 %collective-permute-start.20 = (f32[4,96,128]{2,1,0:T(8,128)S(1)}, f32[4,96,128]{2,1,0:T(8,128)S(1)}, u32[]{:S(2)}, u32[]{:S(2)}) collective-permute-start(f32[4,96,128]{2,1,0:T(8,128)S(1)} %get-tuple-element.645), channel_id=1, source_target_pairs={{0,96},{16,112},{32,0},{48,16},{64,32},{80,48},{96,64},{112,80},{1... | collective-permute-start | bytes 589832 | tf_op jit(solution)/shard_map/while/body/eval_jaxpr/ppermute | solution.py:42
  201.8 7.4 %collective-permute-start.21 = (f32[4,96,128]{2,1,0:T(8,128)S(1)}, f32[4,96,128]{2,1,0:T(8,128)S(1)}, u32[]{:S(2)}, u32[]{:S(2)}) collective-permute-start(f32[4,96,128]{2,1,0:T(8,128)S(1)} %get-tuple-element.646), channel_id=1, source_target_pairs={{0,64},{16,80},{32,96},{48,112},{64,0},{80,16},{96,32},{112,48},{1... | collective-permute-start | bytes 589832 | tf_op jit(solution)/shard_map/while/body/eval_jaxpr/ppermute | solution.py:42
  201.9 12.4 %collective-permute-start.22 = (f32[4,96,128]{2,1,0:T(8,128)S(1)}, f32[4,96,128]{2,1,0:T(8,128)S(1)}, u32[]{:S(2)}, u32[]{:S(2)}) collective-permute-start(f32[4,96,128]{2,1,0:T(8,128)S(1)} %get-tuple-element.647), channel_id=1, source_target_pairs={{0,32},{16,48},{32,64},{48,80},{64,96},{80,112},{96,0},{112,16},{1... | collective-permute-start | bytes 589832 | tf_op jit(solution)/shard_map/while/body/eval_jaxpr/ppermute | solution.py:42
  204.1 20.7 %collective-permute-start.25 = (f32[2,96,128]{2,1,0:T(8,128)S(1)}, f32[2,96,128]{2,1,0:T(8,128)S(1)}, u32[]{:S(2)}, u32[]{:S(2)}) collective-permute-start(f32[2,96,128]{2,1,0:T(8,128)S(1)} %add_add_fusion.2), channel_id=1, source_target_pairs={{0,0},{1,16},{2,32},{3,48},{4,64},{5,80},{6,96},{7,112},{8,128},{9... | collective-permute-start | bytes 294920 | tf_op jit(solution)/shard_map/while/body/eval_jaxpr/ppermute | solution.py:46
  214.4 10.4 %collective-permute-start.23 = (f32[2,96,128]{2,1,0:T(8,128)S(1)}, f32[2,96,128]{2,1,0:T(8,128)S(1)}, u32[]{:S(2)}, u32[]{:S(2)}) collective-permute-start(f32[2,96,128]{2,1,0:T(8,128)S(1)} %slice_add_fusion.24), channel_id=1, source_target_pairs={{0,128},{16,144},{32,160},{48,176},{64,192},{80,208},{96,224},{112... | collective-permute-start | bytes 294920 | tf_op jit(solution)/shard_map/while/body/eval_jaxpr/ppermute | solution.py:42

commit v3 on v2

--- a/solution.py
+++ b/solution.py
@@ -56,10 +56,9 @@
 
 FORWARD_OUT = (4, 4, 4, 4, 2, 2, 4, 4, 4)
 BACKWARD_OUT = (4, 4, 4, 4, 16)
-FORWARD_IN = ((0, 0, 16), (1, 0, 16))
-BACKWARD_IN = (
-    (0, 0, 4), (1, 0, 4), (2, 0, 4), (3, 0, 4), (4, 0, 2), (5, 0, 2), (6, 0, 4), (7, 0, 4), (8, 0, 4)
-)
+FORWARD_IN = ((0, 0, 0, 16), (1, 0, 16, 16))
+BACKWARD_IN = tuple((k, 0, at, 4) for k, at in enumerate((0, 4, 8, 12, 20, 24, 28)))
+FAR = 16
 
 
 def split(x):
@@ -82,17 +81,48 @@
     return ((z * 2 + l) << 1) + (rb & 1)
 
 
+def spread_halves(parts, runs, halves):
+    bs = halves.shape[-1] // 2
+    for array, at, slot, size in runs:
+
+        @pl.loop(0, size)
+        def _(k, part=parts[array], at=at, slot=slot):
+            high, low = split(part[at + k])
+            halves[slot + k, :, :bs] = high
+            halves[slot + k, :, bs:] = low
+
+
+def product(source, block, backward):
+    bs = block.shape[-1]
+    high, low = split(block)
+    zero = jnp.zeros_like(low)
+    side, down = (1, 0) if backward else (0, 1)
+    first = jnp.concatenate([high, low], side)
+    weights = jnp.concatenate([first, jnp.concatenate([high, zero], side)], down)
+    contract = (((1,), (0 if backward else 1,)), ((), ()))
+    out = lax.dot_general(source, weights, contract, preferred_element_type=f32)
+    return out[:, :bs] + out[:, bs:]
+
+
+def write_out(total, outs, sizes):
+    offset = 0
+    for out, size in zip(outs, sizes):
+        out[...] = total[offset : offset + size]
+        offset += size
+
+
 def product_kernel(backward, first, last, n_in, runs, out_sizes, *refs):
     rows, cols, info, blocks = refs[:4]
     parts, refs = refs[4 : 4 + n_in], refs[4 + n_in :]
     if not first:
         halves, total_in, refs = refs[0], refs[1], refs[2:]
     outs, refs = refs[: len(out_sizes)], refs[len(out_sizes) :]
-    if first:
+    if backward:
+        total, halves, held, sems = refs
+    elif first:
         halves, total, held, sems = refs
     else:
         total, held, sems = refs
-    bs = blocks.shape[-1]
     row, col, live = info[0], info[1], info[2]
     full = lax.div(live, UNROLL)
     middle = lax.div(full, 2)
@@ -114,38 +144,17 @@
             copy(full).start()
 
     if first:
-        offset = 0
-        for array, at, size in runs:
-
-            @pl.loop(0, size)
-            def _(k, part=parts[array], at=at, offset=offset):
-                high, low = split(part[at + k])
-                halves[offset + k, :, :bs] = high
-                halves[offset + k, :, bs:] = low
-
-            offset += size
+        spread_halves(parts, runs, halves)
         total[...] = jnp.zeros_like(total)
+        if backward:
+            halves[FAR : FAR + 4] = jnp.zeros((4,) + halves.shape[1:], bf16)
     else:
         total[...] = total_in[...]
 
     def one(s):
         rb, cb = row_slot(rows[0, 0, s], col), col_slot(cols[0, 0, s], row)
-        high, low = split(held[s])
-        zero = jnp.zeros_like(low)
-        if backward:
-            weights = jnp.concatenate(
-                [jnp.concatenate([high, low], 1), jnp.concatenate([high, zero], 1)], 0
-            )
-            out = jnp.dot(halves[rb], weights, preferred_element_type=f32)
-            total[cb] += out[:, :bs] + out[:, bs:]
-        else:
-            weights = jnp.concatenate(
-                [jnp.concatenate([high, high], 1), jnp.concatenate([low, zero], 1)], 0
-            )
-            out = lax.dot_general(
-                halves[cb], weights, (((1,), (1,)), ((), ())), preferred_element_type=f32
-            )
-            total[rb] += out[:, :bs] + out[:, bs:]
+        source, target = (rb, cb) if backward else (cb, rb)
+        total[target] += product(halves[source], held[s], backward)
 
     @pl.loop(begin, end)
     def _(c):
@@ -163,12 +172,54 @@
             def _(s):
                 one(s)
 
-        offset = 0
-        for out, size in zip(outs, out_sizes):
-            out[...] = total[offset : offset + size]
-            offset += size
-
-
+        write_out(total, outs, out_sizes)
+
+
+def far_kernel(runs, out_sizes, *refs):
+    rows, cols, info, blocks, far_a, far_b, total_in = refs[:7]
+    outs, (halves, total, held, picked, sems) = refs[7:-5], refs[-5:]
+    row, col, live = info[0], info[1], info[2]
+
+    def copy(s, n):
+        return pltpu.make_async_copy(blocks.at[0, 0, s], held.at[n], sems.at[n])
+
+    def pick(s, n):
+        far = row_slot(rows[0, 0, s], col) >> 2 == FAR >> 2
+
+        @pl.when(far)
+        def _():
+            picked[n] = s
+            copy(s, n).start()
+
+        return n + far.astype(jnp.int32)
+
+    found = lax.fori_loop(0, live, pick, jnp.int32(0))
+    spread_halves((far_a, far_b), runs, halves)
+    spare = total_in.shape[0]
+    total[:spare] = total_in[...]
+    total[spare] = jnp.zeros(total.shape[1:], f32)
+
+    @pl.loop(0, lax.div(found + FAR_UNROLL - 1, FAR_UNROLL))
+    def _(g):
+        for k in range(FAR_UNROLL):
+            n = g * FAR_UNROLL + k
+
+            @pl.when(n < found)
+            def _(n=n):
+                copy(picked[n], n).wait()
+
+        for k in range(FAR_UNROLL):
+            n = g * FAR_UNROLL + k
+            at = jnp.minimum(n, found - 1)
+            s = picked[at]
+            rb, cb = row_slot(rows[0, 0, s], col), col_slot(cols[0, 0, s], row)
+            cb = jnp.where(n < found, cb, spare)
+            total[cb] += product(halves[rb & 3], held[at], True)
+
+    write_out(total, outs, out_sizes)
+
+
+FAR_UNROLL = 4
 UNROLL = 16
 
 
@@ -176,31 +227,38 @@
     blocks = index[3]
     slots, bs = blocks.shape[2], blocks.shape[-1]
     vecs = state[0].shape[1]
-    n_in = len(state) if first else 0
-    runs = BACKWARD_IN if backward else FORWARD_IN
+    far = backward and not first
     out_sizes = () if not last else BACKWARD_OUT if backward else FORWARD_OUT
     smem = pl.BlockSpec(memory_space=pltpu.SMEM)
     vmem = pl.BlockSpec(memory_space=pltpu.VMEM)
     halves, total = (32, vecs, 2 * bs), (32, vecs, bs)
     out_shape = [jax.ShapeDtypeStruct((n, vecs, bs), f32) for n in out_sizes]
     scratch = []
-    if first and not last:
-        out_shape += [jax.ShapeDtypeStruct(halves, bf16), jax.ShapeDtypeStruct(total, f32)]
-    elif first:
-        scratch = [pltpu.VMEM(halves, bf16), pltpu.VMEM(total, f32)]
+    held = [pltpu.VMEM((slots, bs, bs), f32), pltpu.SemaphoreType.DMA((slots // UNROLL,))]
+    if far:
+        kernel = functools.partial(far_kernel, ((0, 0, 0, 2), (1, 0, 2, 2)), out_sizes)
+        scratch = [pltpu.VMEM((4,) + halves[1:], bf16), pltpu.VMEM((33,) + total[1:], f32), held[0]]
+        held = [pltpu.SMEM((slots,), jnp.int32), pltpu.SemaphoreType.DMA((slots,))]
     else:
-        scratch = [pltpu.VMEM(total, f32)]
-    scratch += [
-        pltpu.VMEM((slots, bs, bs), f32),
-        pltpu.SemaphoreType.DMA((slots // UNROLL,)),
-    ]
-    share = 1 if first and last else 2
+        n_in = len(state) if first else 0
+        runs = BACKWARD_IN if backward else FORWARD_IN
+        kernel = functools.partial(
+            product_kernel, backward, first, last or backward, n_in, runs, out_sizes
+        )
+        if backward:
+            out_shape += [jax.ShapeDtypeStruct(total, f32)]
+            scratch = [pltpu.VMEM(halves, bf16)]
+        elif first:
+            out_shape += [jax.ShapeDtypeStruct(halves, bf16), jax.ShapeDtypeStruct(total, f32)]
+        else:
+            scratch = [pltpu.VMEM(total, f32)]
+    share = 8 if far else 1 if backward else 2
     return pl.pallas_call(
-        functools.partial(product_kernel, backward, first, last, n_in, runs, out_sizes),
+        kernel,
         in_specs=[smem] * 3 + [pl.BlockSpec(memory_space=pltpu.HBM)] + [vmem] * len(state),
         out_specs=[vmem] * len(out_shape),
         out_shape=out_shape,
-        scratch_shapes=scratch,
+        scratch_shapes=scratch + held,
         compiler_params=pltpu.CompilerParams(vmem_limit_bytes=49 << 20),
         cost_estimate=pl.CostEstimate(
             flops=24 * slots * vecs * bs * bs // share,
@@ -243,18 +301,19 @@
         up3, down3 = bar(up3, down3)
         up4 = send(cat(up3[2:4], f5[:2], f5[2:] + up3[4:]), "col", Z_DOWN)
         down4 = send(cat(down3[:2], f3[:2] + down3[4:], f3[2:]), "col", Z_UP)
-        up4, down4 = bar(up4, down4)
+        state = (z0, up1, up2, up3, down3, down2, down1)
+        (total,) = products(True, True, False, state, index)
+        up4, down4, total = bar(up4, down4, total)
         u = send(f2 + down4[2:], "col", Z_UP)
         d = send(f6 + up4[2:], "col", Z_DOWN)
-        u, d = bar(u, d)
+        backward = products(True, False, True, (down4, up4, total), index)
+        u, d, *backward = bar(u, d, *backward)
+        g0, g1, g2, g3, other = backward
         u = send(f1 + u, "col", Z_UP)
         d = send(f7 + d, "col", Z_DOWN)
-        state = (z0, up1, up2, up3, down4, up4, down3, down2, down1)
-        backward = products(True, True, True, state, index)
-        u, d, *backward = bar(u, d, *backward)
-        g0, g1, g2, g3, other = backward
+        o = send(other, "row", CORE)
+        u, d, o = bar(u, d, o)
         h = send(f0[2:] + u[2:] + d[2:], "col", X_LO)
-        o = send(other, "row", CORE)
         q1 = send(g1 + o[4:8], "row", Y_UP)
         q2 = send(g2 + o[8:12], "row", Y_FAR)
         q3 = send(g3 + o[12:], "row", Y_DOWN)

time: 226 us -> 227 us (level)
  the two profiles are of different devices: /device:TPU:7 before, /device:TPU:5 now
where the time goes in v3:
time: 227 us; the launch traced here: 226 us
  starting transfers between devices  95 us (42%)
  waiting for transfers between devices  85.7 us (38%)
  Pallas kernels  34.6 us (15%)
  other arithmetic  6.71 us (3%)
    ppermute x48, waiting for transfers between devices, send(): return lax.ppermute(x, axis, perm)  81.5 us
    ppermute x48, starting transfers between devices, send(): return lax.ppermute(x, axis, perm)  69.4 us
    pallas_call x8, Pallas kernels, products(): pl.pallas_call(kernel, in_specs=[smem] * 3 + [pl.BlockSpec(memory_space=p...  34.6 us
    ppermute x4, starting transfers between devices, flip(): return lax.ppermute(x, ('row', 'col'), FLIP)  25.6 us
  transfers between devices with their start and end apart: 52, of which 31 were waited for; matrix products, arithmetic and copies ran while one was open for 2% of the time, Pallas kernels for 15%

profile of v3, /device:TPU:5, one launch (start us, length us, event | category | flops | bytes accessed | tf_op | source)
XLA Modules:
  0.0 226.4 jit_solution(12992356218127850003)
XLA Ops:
  1.3 0.9 reshape.12
  3.1 222.7 %while.23 = (s32[]{:T(128)}, f32[2,96,128]{2,1,0:T(8,128)S(1)}, f32[2,96,128]{2,1,0:T(8,128)S(1)}, f32[2,96,128]{2,1,0:T(8,128)S(1)}, f32[]{:T(128)}, /*index=5*...) while((s32[]{:T(128)}, f32[2,96,128]{2,1,0:T(8,128)S(1)}, ...), condition=%wide.region_1.2_spmd.clone, body=%wide.region_0.1_spmd.clone.sunk | while | flops 14119526400 | bytes 62561016 | solution.py:339
  3.2 11.4 %collective-permute-start.4 = (f32[2,96,128]{2,1,0:T(8,128)S(1)}, f32[2,96,128]{2,1,0:T(8,128)S(1)}, u32[]{:S(2)}, u32[]{:S(2)}) collective-permute-start(f32[2,96,128]{2,1,0:T(8,128)S(1)} %get-tuple-element.678), channel_id=1, source_target_pairs={{0,0},{1,16},{2,32},{3,48},{4,64},{5,80},{6,96},{7,112},{8,128},{9... | collective-permute-start | bytes 294920 | tf_op jit(solution)/shard_map/while/body/eval_jaxpr/ppermute | solution.py:46
  14.7 1.1 collective-permute-start.1
  15.8 1.5 collective-permute-start.2
  17.5 2.2 collective-permute-start.5
  19.7 2.3 %collective-permute-done.5 = f32[2,96,128]{2,1,0:T(8,128)S(1)} collective-permute-done((f32[2,96,128]{2,1,0:T(8,128)S(1)}, f32[2,96,128]{2,1,0:T(8,128)S(1)}, u32[]{:S(2)}, u32[]{:S(2)}) %collective-permute-start.5) | collective-permute-done | bytes 98336 | tf_op jit(solution)/shard_map/while/body/eval_jaxpr/ppermute | solution.py:42
  22.0 3.1 %collective-permute-done.2 = f32[4,96,128]{2,1,0:T(8,128)S(1)} collective-permute-done((f32[4,96,128]{2,1,0:T(8,128)S(1)}, f32[4,96,128]{2,1,0:T(8,128)S(1)}, u32[]{:S(2)}, u32[]{:S(2)}) %collective-permute-start.2) | collective-permute-done | bytes 196640 | tf_op jit(solution)/shard_map/while/body/eval_jaxpr/ppermute | solution.py:42
  25.1 4.2 %collective-permute-done.3 = f32[4,96,128]{2,1,0:T(8,128)S(1)} collective-permute-done((f32[4,96,128]{2,1,0:T(8,128)S(1)}, f32[4,96,128]{2,1,0:T(8,128)S(1)}, u32[]{:S(2)}, u32[]{:S(2)}) %collective-permute-start.3) | collective-permute-done | bytes 196640 | tf_op jit(solution)/shard_map/while/body/eval_jaxpr/ppermute | solution.py:42
  30.8 1.0 collective-permute-start.7
  32.2 2.7 %eval_jaxpr.24 = (bf16[32,96,256]{2,1,0:T(8,128)(2,1)S(1)}, f32[32,96,128]{2,1,0:T(8,128)S(1)}) custom-call(s32[1,1,176]{2,1,0:T(1,128)S(1)} %copy-done, s32[1,1,176]{2,1,0:T(1,128)S(1)} %copy-done.1, s32[3]{0:T(128)S(1)} %get-tuple-element.698.refs_2_, f32[1,1,176,128,128]{4,3,2,1,0:T(8,128)} %get-tuple-element.699.refs_3_, ...), custom_call_target="tpu_custom_call" | custom-call | flops 3321888768 | bytes 5767168 | tf_op jit(solution)/shard_map/while/body/eval_jaxpr/pallas_call | solution.py:256
  34.9 1.9 collective-permute-done.6.refs_5_
  36.8 1.4 collective-permute-done.7.refs_10_
  38.9 1.9 collective-permute-start.9
  40.8 5.5 %eval_jaxpr.25 = (f32[4,96,128]{2,1,0:T(8,128)S(1)}, f32[4,96,128]{2,1,0:T(8,128)S(1)}, f32[4,96,128]{2,1,0:T(8,128)S(1)}, f32[4,96,128]{2,1,0:T(8,128)S(1)}, f3...) custom-call(s32[1,1,176]{2,1,0:T(1,128)S(1)} %copy-done, ...), custom_call_target="tpu_custom_call" | custom-call | flops 3321888768 | bytes 5767168 | tf_op jit(solution)/shard_map/while/body/eval_jaxpr/pallas_call | solution.py:256
  46.5 1.5 collective-permute-start.12
  48.0 1.4 collective-permute-start.11
  49.4 5.8 %collective-permute-done.12.refs_8_ = f32[6,96,128]{2,1,0:T(8,128)S(1)} collective-permute-done((f32[6,96,128]{2,1,0:T(8,128)S(1)}, f32[6,96,128]{2,1,0:T(8,128)S(1)}, u32[]{:S(2)}, u32[]{:S(2)}) %collective-permute-start.12) | collective-permute-done | bytes 294944 | tf_op jit(solution)/shard_map/while/body/eval_jaxpr/ppermute | solution.py:42
  57.0 2.0 collective-permute-start.13
  59.0 5.0 %eval_jaxpr.26.refs_6_ = f32[32,96,128]{2,1,0:T(8,128)S(1)} custom-call(s32[1,1,176]{2,1,0:T(1,128)S(1)} %copy-done, s32[1,1,176]{2,1,0:T(1,128)S(1)} %copy-done.1, s32[3]{0:T(128)S(1)} %get-tuple-element.698.refs_2_, f32[1,1,176,128,128]{4,3,2,1,0:T(8,128)} %get-tuple-element.699.refs_3_, f32[4,96,128]{2,1,0:T(8,128)S(1)} %constant_dynamic-update-slice_fusion.19.refs_4_, ...), custom_call_target="tpu_custom_call" | custom-call | flops 6643777536 | bytes 11534336 | tf_op jit(solution)/shard_map/while/body/eval_jaxpr/pallas_call | solution.py:256
  64.3 2.6 %collective-permute-start.16 = (f32[4,96,128]{2,1,0:T(8,128)S(1)}, f32[4,96,128]{2,1,0:T(8,128)S(1)}, u32[]{:S(2)}, u32[]{:S(2)}) collective-permute-start(f32[4,96,128]{2,1,0:T(8,128)S(1)} %slice_add_fusion.20), channel_id=1, source_target_pairs={{0,14},{1,15},{2,0},{3,1},{4,2},{5,3},{6,4},{7,5},{8,6},{9,7},{10,... | collective-permute-start | bytes 589832 | tf_op jit(solution)/shard_map/while/body/eval_jaxpr/ppermute | solution.py:42
  67.0 4.1 %eval_jaxpr.27 = (f32[4,96,128]{2,1,0:T(8,128)S(1)}, f32[4,96,128]{2,1,0:T(8,128)S(1)}, f32[4,96,128]{2,1,0:T(8,128)S(1)}, f32[4,96,128]{2,1,0:T(8,128)S(1)}, f32[16,96,128]{2,1,0:T(8,128)S(1)}) custom-call(s32[1,1,176]{2,1,0:T(1,128)S(1)} %copy-done, s32[1,1,176]{2,1,0:T(1,128)S(1)} %copy-done.1, s32[3]{0:T(128)S(1)} %get-tuple-element.698.refs_2_, ...), custom_call_target="tpu_custom_call" | custom-call | flops 830472192 | bytes 1441792 | tf_op jit(solution)/shard_map/while/body/eval_jaxpr/pallas_call | solution.py:256
  71.1 1.6 collective-permute-done.15
  72.7 4.3 %collective-permute-start.19 = (f32[16,96,128]{2,1,0:T(8,128)S(1)}, f32[16,96,128]{2,1,0:T(8,128)S(1)}, u32[]{:S(2)}, u32[]{:S(2)}) collective-permute-start(f32[16,96,128]{2,1,0:T(8,128)S(1)} %get-tuple-element.649), channel_id=1, source_target_pairs={{0,16},{16,0},{32,48},{48,32},{64,80},{80,64},{96,112},{112,96},{1... | collective-permute-start | bytes 2359304 | tf_op jit(solution)/shard_map/while/body/eval_jaxpr/ppermute | solution.py:42
  77.6 1.0 collective-permute-start.17
  78.7 5.0 %collective-permute-done.18 = f32[4,96,128]{2,1,0:T(8,128)S(1)} collective-permute-done((f32[4,96,128]{2,1,0:T(8,128)S(1)}, f32[4,96,128]{2,1,0:T(8,128)S(1)}, u32[]{:S(2)}, u32[]{:S(2)}) %collective-permute-start.18) | collective-permute-done | bytes 196640 | tf_op jit(solution)/shard_map/while/body/eval_jaxpr/ppermute | solution.py:42
  83.6 1.5 collective-permute-done.17
  86.1 2.4 %collective-permute-start.24 = (f32[2,96,128]{2,1,0:T(8,128)S(1)}, f32[2,96,128]{2,1,0:T(8,128)S(1)}, u32[]{:S(2)}, u32[]{:S(2)}) collective-permute-start(f32[2,96,128]{2,1,0:T(8,128)S(1)} %slice_add_fusion.23), channel_id=1, source_target_pairs={{0,1},{1,0},{2,3},{3,2},{4,5},{5,4},{6,7},{7,6},{8,9},{9,8},{10,11... | collective-permute-start | bytes 294920 | tf_op jit(solution)/shard_map/while/body/eval_jaxpr/ppermute | solution.py:42
  88.6 3.7 %collective-permute-start.20 = (f32[4,96,128]{2,1,0:T(8,128)S(1)}, f32[4,96,128]{2,1,0:T(8,128)S(1)}, u32[]{:S(2)}, u32[]{:S(2)}) collective-permute-start(f32[4,96,128]{2,1,0:T(8,128)S(1)} %get-tuple-element.653), channel_id=1, source_target_pairs={{0,96},{16,112},{32,0},{48,16},{64,32},{80,48},{96,64},{112,80},{1... | collective-permute-start | bytes 589832 | tf_op jit(solution)/shard_map/while/body/eval_jaxpr/ppermute | solution.py:42
  93.9 6.7 %collective-permute-start.25 = (f32[2,96,128]{2,1,0:T(8,128)S(1)}, f32[2,96,128]{2,1,0:T(8,128)S(1)}, u32[]{:S(2)}, u32[]{:S(2)}) collective-permute-start(f32[2,96,128]{2,1,0:T(8,128)S(1)} %add_add_fusion.2), channel_id=1, source_target_pairs={{0,0},{1,16},{2,32},{3,48},{4,64},{5,80},{6,96},{7,112},{8,128},{9... | collective-permute-start | bytes 294920 | tf_op jit(solution)/shard_map/while/body/eval_jaxpr/ppermute | solution.py:46
  100.6 3.7 %collective-permute-done.22 = f32[4,96,128]{2,1,0:T(8,128)S(1)} collective-permute-done((f32[4,96,128]{2,1,0:T(8,128)S(1)}, f32[4,96,128]{2,1,0:T(8,128)S(1)}, u32[]{:S(2)}, u32[]{:S(2)}) %collective-permute-start.22) | collective-permute-done | bytes 196640 | tf_op jit(solution)/shard_map/while/body/eval_jaxpr/ppermute | solution.py:42
  104.3 2.5 %collective-permute-start.23 = (f32[2,96,128]{2,1,0:T(8,128)S(1)}, f32[2,96,128]{2,1,0:T(8,128)S(1)}, u32[]{:S(2)}, u32[]{:S(2)}) collective-permute-start(f32[2,96,128]{2,1,0:T(8,128)S(1)} %slice_add_fusion.22), channel_id=1, source_target_pairs={{0,128},{16,144},{32,160},{48,176},{64,192},{80,208},{96,224},{112... | collective-permute-start | bytes 294920 | tf_op jit(solution)/shard_map/while/body/eval_jaxpr/ppermute | solution.py:42
  107.4 8.5 %collective-permute-done.23 = f32[2,96,128]{2,1,0:T(8,128)S(1)} collective-permute-done((f32[2,96,128]{2,1,0:T(8,128)S(1)}, f32[2,96,128]{2,1,0:T(8,128)S(1)}, u32[]{:S(2)}, u32[]{:S(2)}) %collective-permute-start.23) | collective-permute-done | bytes 98336 | tf_op jit(solution)/shard_map/while/body/eval_jaxpr/ppermute | solution.py:42
  116.2 4.0 %collective-permute-start.4 = (f32[2,96,128]{2,1,0:T(8,128)S(1)}, f32[2,96,128]{2,1,0:T(8,128)S(1)}, u32[]{:S(2)}, u32[]{:S(2)}) collective-permute-start(f32[2,96,128]{2,1,0:T(8,128)S(1)} %get-tuple-element.678), channel_id=1, source_target_pairs={{0,0},{1,16},{2,32},{3,48},{4,64},{5,80},{6,96},{7,112},{8,128},{9... | collective-permute-start | bytes 294920 | tf_op jit(solution)/shard_map/while/body/eval_jaxpr/ppermute | solution.py:46
  120.3 1.3 collective-permute-done
  121.8 1.4 collective-permute-start.3
  123.1 4.1 %collective-permute-done.4 = f32[2,96,128]{2,1,0:T(8,128)S(1)} collective-permute-done((f32[2,96,128]{2,1,0:T(8,128)S(1)}, f32[2,96,128]{2,1,0:T(8,128)S(1)}, u32[]{:S(2)}, u32[]{:S(2)}) %collective-permute-start.4) | collective-permute-done | bytes 98336 | tf_op jit(solution)/shard_map/while/body/eval_jaxpr/ppermute | solution.py:46
  128.2 1.6 collective-permute-start.5
  129.7 2.3 %collective-permute-done.5 = f32[2,96,128]{2,1,0:T(8,128)S(1)} collective-permute-done((f32[2,96,128]{2,1,0:T(8,128)S(1)}, f32[2,96,128]{2,1,0:T(8,128)S(1)}, u32[]{:S(2)}, u32[]{:S(2)}) %collective-permute-start.5) | collective-permute-done | bytes 98336 | tf_op jit(solution)/shard_map/while/body/eval_jaxpr/ppermute | solution.py:42
  132.1 4.7 %collective-permute-start.8 = (f32[16,96,128]{2,1,0:T(8,128)S(1)}, f32[16,96,128]{2,1,0:T(8,128)S(1)}, u32[]{:S(2)}, u32[]{:S(2)}) collective-permute-start(f32[16,96,128]{2,1,0:T(8,128)S(1)} %constant_dynamic-update-slice_fusion.22.refs_4_), channel_id=1, source_target_pairs={{0,16},{16,0},{32,48},{48,32},{64,80},{80,64},{96,112},{112,96},{1... | collective-permute-start | bytes 2359304 | tf_op jit(solution)/shard_map/while/body/eval_jaxpr/ppermute | solution.py:42
  136.8 2.0 collective-permute-start.6
  138.9 2.7 %eval_jaxpr.24 = (bf16[32,96,256]{2,1,0:T(8,128)(2,1)S(1)}, f32[32,96,128]{2,1,0:T(8,128)S(1)}) custom-call(s32[1,1,176]{2,1,0:T(1,128)S(1)} %copy-done, s32[1,1,176]{2,1,0:T(1,128)S(1)} %copy-done.1, s32[3]{0:T(128)S(1)} %get-tuple-element.698.refs_2_, f32[1,1,176,128,128]{4,3,2,1,0:T(8,128)} %get-tuple-element.699.refs_3_, ...), custom_call_target="tpu_custom_call" | custom-call | flops 3321888768 | bytes 5767168 | tf_op jit(solution)/shard_map/while/body/eval_jaxpr/pallas_call | solution.py:256
  141.6 1.8 collective-permute-done.6.refs_5_
  143.4 2.9 %collective-permute-done.7.refs_10_ = f32[4,96,128]{2,1,0:T(8,128)S(1)} collective-permute-done((f32[4,96,128]{2,1,0:T(8,128)S(1)}, f32[4,96,128]{2,1,0:T(8,128)S(1)}, u32[]{:S(2)}, u32[]{:S(2)}) %collective-permute-start.7) | collective-permute-done | bytes 196640 | tf_op jit(solution)/shard_map/while/body/eval_jaxpr/ppermute | solution.py:42
  146.4 2.5 %collective-permute-start.9 = (f32[4,96,128]{2,1,0:T(8,128)S(1)}, f32[4,96,128]{2,1,0:T(8,128)S(1)}, u32[]{:S(2)}, u32[]{:S(2)}) collective-permute-start(f32[4,96,128]{2,1,0:T(8,128)S(1)} %collective-permute-done.6.refs_5_), channel_id=1, source_target_pairs={{0,14},{1,15},{2,0},{3,1},{4,2},{5,3},{6,4},{7,5},{8,6},{9,7},{10,... | collective-permute-start | bytes 589832 | tf_op jit(solution)/shard_map/while/body/eval_jaxpr/ppermute | solution.py:42
  148.9 5.5 %eval_jaxpr.25 = (f32[4,96,128]{2,1,0:T(8,128)S(1)}, f32[4,96,128]{2,1,0:T(8,128)S(1)}, f32[4,96,128]{2,1,0:T(8,128)S(1)}, f32[4,96,128]{2,1,0:T(8,128)S(1)}, f3...) custom-call(s32[1,1,176]{2,1,0:T(1,128)S(1)} %copy-done, ...), custom_call_target="tpu_custom_call" | custom-call | flops 3321888768 | bytes 5767168 | tf_op jit(solution)/shard_map/while/body/eval_jaxpr/pallas_call | solution.py:256
  154.5 1.1 collective-permute-start.12
  155.6 1.8 collective-permute-start.11
  157.3 5.7 %collective-permute-done.12.refs_8_ = f32[6,96,128]{2,1,0:T(8,128)S(1)} collective-permute-done((f32[6,96,128]{2,1,0:T(8,128)S(1)}, f32[6,96,128]{2,1,0:T(8,128)S(1)}, u32[]{:S(2)}, u32[]{:S(2)}) %collective-permute-start.12) | collective-permute-done | bytes 294944 | tf_op jit(solution)/shard_map/while/body/eval_jaxpr/ppermute | solution.py:42
  163.7 2.3 %collective-permute-start.14 = (f32[6,96,128]{2,1,0:T(8,128)S(1)}, f32[6,96,128]{2,1,0:T(8,128)S(1)}, u32[]{:S(2)}, u32[]{:S(2)}) collective-permute-start(f32[6,96,128]{2,1,0:T(8,128)S(1)} %pad_maximum_fusion.11), channel_id=1, source_target_pairs={{0,2},{1,3},{2,4},{3,5},{4,6},{5,7},{6,8},{7,9},{8,10},{9,11},{10,... | collective-permute-start | bytes 884744 | tf_op jit(solution)/shard_map/while/body/eval_jaxpr/ppermute | solution.py:42
  166.5 5.0 %eval_jaxpr.26.refs_6_ = f32[32,96,128]{2,1,0:T(8,128)S(1)} custom-call(s32[1,1,176]{2,1,0:T(1,128)S(1)} %copy-done, s32[1,1,176]{2,1,0:T(1,128)S(1)} %copy-done.1, s32[3]{0:T(128)S(1)} %get-tuple-element.698.refs_2_, f32[1,1,176,128,128]{4,3,2,1,0:T(8,128)} %get-tuple-element.699.refs_3_, f32[4,96,128]{2,1,0:T(8,128)S(1)} %constant_dynamic-update-slice_fusion.19.refs_4_, ...), custom_call_target="tpu_custom_call" | custom-call | flops 6643777536 | bytes 11534336 | tf_op jit(solution)/shard_map/while/body/eval_jaxpr/pallas_call | solution.py:256
  171.8 1.5 collective-permute-done.13.refs_5_
  173.4 1.0 collective-permute-start.16
  175.0 4.1 %eval_jaxpr.27 = (f32[4,96,128]{2,1,0:T(8,128)S(1)}, f32[4,96,128]{2,1,0:T(8,128)S(1)}, f32[4,96,128]{2,1,0:T(8,128)S(1)}, f32[4,96,128]{2,1,0:T(8,128)S(1)}, f32[16,96,128]{2,1,0:T(8,128)S(1)}) custom-call(s32[1,1,176]{2,1,0:T(1,128)S(1)} %copy-done, s32[1,1,176]{2,1,0:T(1,128)S(1)} %copy-done.1, s32[3]{0:T(128)S(1)} %get-tuple-element.698.refs_2_, ...), custom_call_target="tpu_custom_call" | custom-call | flops 830472192 | bytes 1441792 | tf_op jit(solution)/shard_map/while/body/eval_jaxpr/pallas_call | solution.py:256
  179.2 1.1 collective-permute-done.15
  180.2 4.3 %collective-permute-start.19 = (f32[16,96,128]{2,1,0:T(8,128)S(1)}, f32[16,96,128]{2,1,0:T(8,128)S(1)}, u32[]{:S(2)}, u32[]{:S(2)}) collective-permute-start(f32[16,96,128]{2,1,0:T(8,128)S(1)} %get-tuple-element.649), channel_id=1, source_target_pairs={{0,16},{16,0},{32,48},{48,32},{64,80},{80,64},{96,112},{112,96},{1... | collective-permute-start | bytes 2359304 | tf_op jit(solution)/shard_map/while/body/eval_jaxpr/ppermute | solution.py:42
  185.2 1.0 collective-permute-start.17
  186.2 5.0 %collective-permute-done.18 = f32[4,96,128]{2,1,0:T(8,128)S(1)} collective-permute-done((f32[4,96,128]{2,1,0:T(8,128)S(1)}, f32[4,96,128]{2,1,0:T(8,128)S(1)}, u32[]{:S(2)}, u32[]{:S(2)}) %collective-permute-start.18) | collective-permute-done | bytes 196640 | tf_op jit(solution)/shard_map/while/body/eval_jaxpr/ppermute | solution.py:42
  191.2 1.5 collective-permute-done.17
  193.6 7.6 %collective-permute-start.24 = (f32[2,96,128]{2,1,0:T(8,128)S(1)}, f32[2,96,128]{2,1,0:T(8,128)S(1)}, u32[]{:S(2)}, u32[]{:S(2)}) collective-permute-start(f32[2,96,128]{2,1,0:T(8,128)S(1)} %slice_add_fusion.23), channel_id=1, source_target_pairs={{0,1},{1,0},{2,3},{3,2},{4,5},{5,4},{6,7},{7,6},{8,9},{9,8},{10,11... | collective-permute-start | bytes 294920 | tf_op jit(solution)/shard_map/while/body/eval_jaxpr/ppermute | solution.py:42
  201.5 1.4 collective-permute-start.22
  204.1 3.4 %collective-permute-start.25 = (f32[2,96,128]{2,1,0:T(8,128)S(1)}, f32[2,96,128]{2,1,0:T(8,128)S(1)}, u32[]{:S(2)}, u32[]{:S(2)}) collective-permute-start(f32[2,96,128]{2,1,0:T(8,128)S(1)} %add_add_fusion.2), channel_id=1, source_target_pairs={{0,0},{1,16},{2,32},{3,48},{4,64},{5,80},{6,96},{7,112},{8,128},{9... | collective-permute-start | bytes 294920 | tf_op jit(solution)/shard_map/while/body/eval_jaxpr/ppermute | solution.py:46
  208.0 5.8 %collective-permute-done.22 = f32[4,96,128]{2,1,0:T(8,128)S(1)} collective-permute-done((f32[4,96,128]{2,1,0:T(8,128)S(1)}, f32[4,96,128]{2,1,0:T(8,128)S(1)}, u32[]{:S(2)}, u32[]{:S(2)}) %collective-permute-start.22) | collective-permute-done | bytes 196640 | tf_op jit(solution)/shard_map/while/body/eval_jaxpr/ppermute | solution.py:42
  215.4 10.3 %collective-permute-done.23 = f32[2,96,128]{2,1,0:T(8,128)S(1)} collective-permute-done((f32[2,96,128]{2,1,0:T(8,128)S(1)}, f32[2,96,128]{2,1,0:T(8,128)S(1)}, u32[]{:S(2)}, u32[]{:S(2)}) %collective-permute-start.23) | collective-permute-done | bytes 98336 | tf_op jit(solution)/shard_map/while/body/eval_jaxpr/ppermute | solution.py:42
  (116 shorter events, 18.9 us)
Async XLA Ops:
  3.1 29.1 %copy-start = (s32[1,1,176]{2,1,0:T(1,128)S(1)}, s32[1,1,176]{2,1,0:T(1,128)}, u32[]{:S(2)}) copy-start(s32[1,1,176]{2,1,0:T(1,128)} %get-tuple-element.696.refs_0_) | copy-start | bytes 2116 | tf_op jit(solution)/shard_map/while
  3.1 29.1 %copy-start.1 = (s32[1,1,176]{2,1,0:T(1,128)S(1)}, s32[1,1,176]{2,1,0:T(1,128)}, u32[]{:S(2)}) copy-start(s32[1,1,176]{2,1,0:T(1,128)} %get-tuple-element.697.refs_1_) | copy-start | bytes 2116 | tf_op jit(solution)/shard_map/while
  3.1 11.6 %collective-permute-start = (f32[2,96,128]{2,1,0:T(8,128)S(1)}, f32[2,96,128]{2,1,0:T(8,128)S(1)}, u32[]{:S(2)}, u32[]{:S(2)}) collective-permute-start(f32[2,96,128]{2,1,0:T(8,128)S(1)} %copy.29), channel_id=1, source_target_pairs={{0,128},{16,144},{32,160},{48,176},{64,192},{80,208},{96,224},{112... | collective-permute-start | bytes 294920 | tf_op jit(solution)/shard_map/while/body/eval_jaxpr/ppermute | solution.py:42
  3.2 14.3 %collective-permute-start.4 = (f32[2,96,128]{2,1,0:T(8,128)S(1)}, f32[2,96,128]{2,1,0:T(8,128)S(1)}, u32[]{:S(2)}, u32[]{:S(2)}) collective-permute-start(f32[2,96,128]{2,1,0:T(8,128)S(1)} %get-tuple-element.678), channel_id=1, source_target_pairs={{0,0},{1,16},{2,32},{3,48},{4,64},{5,80},{6,96},{7,112},{8,128},{9... | collective-permute-start | bytes 294920 | tf_op jit(solution)/shard_map/while/body/eval_jaxpr/ppermute | solution.py:46
  14.7 7.3 %collective-permute-start.1 = (f32[4,96,128]{2,1,0:T(8,128)S(1)}, f32[4,96,128]{2,1,0:T(8,128)S(1)}, u32[]{:S(2)}, u32[]{:S(2)}) collective-permute-start(f32[4,96,128]{2,1,0:T(8,128)S(1)} %get-tuple-element.597), channel_id=1, source_target_pairs={{0,96},{16,112},{32,0},{48,16},{64,32},{80,48},{96,64},{112,80},{1... | collective-permute-start | bytes 589832 | tf_op jit(solution)/shard_map/while/body/eval_jaxpr/ppermute | solution.py:42
  15.8 9.3 %collective-permute-start.2 = (f32[4,96,128]{2,1,0:T(8,128)S(1)}, f32[4,96,128]{2,1,0:T(8,128)S(1)}, u32[]{:S(2)}, u32[]{:S(2)}) collective-permute-start(f32[4,96,128]{2,1,0:T(8,128)S(1)} %get-tuple-element.597), channel_id=1, source_target_pairs={{0,64},{16,80},{32,96},{48,112},{64,0},{80,16},{96,32},{112,48},{1... | collective-permute-start | bytes 589832 | tf_op jit(solution)/shard_map/while/body/eval_jaxpr/ppermute | solution.py:42
  17.3 12.0 %collective-permute-start.3 = (f32[4,96,128]{2,1,0:T(8,128)S(1)}, f32[4,96,128]{2,1,0:T(8,128)S(1)}, u32[]{:S(2)}, u32[]{:S(2)}) collective-permute-start(f32[4,96,128]{2,1,0:T(8,128)S(1)} %get-tuple-element.597), channel_id=1, source_target_pairs={{0,32},{16,48},{32,64},{48,80},{64,96},{80,112},{96,0},{112,16},{1... | collective-permute-start | bytes 589832 | tf_op jit(solution)/shard_map/while/body/eval_jaxpr/ppermute | solution.py:42
  17.5 4.5 %collective-permute-start.5 = (f32[2,96,128]{2,1,0:T(8,128)S(1)}, f32[2,96,128]{2,1,0:T(8,128)S(1)}, u32[]{:S(2)}, u32[]{:S(2)}) collective-permute-start(f32[2,96,128]{2,1,0:T(8,128)S(1)} %select_add_fusion.2), channel_id=1, source_target_pairs={{0,1},{1,0},{2,3},{3,2},{4,5},{5,4},{6,7},{7,6},{8,9},{9,8},{10,11... | collective-permute-start | bytes 294920 | tf_op jit(solution)/shard_map/while/body/eval_jaxpr/ppermute | solution.py:42
  29.4 2.8 %collective-permute-start.8 = (f32[16,96,128]{2,1,0:T(8,128)S(1)}, f32[16,96,128]{2,1,0:T(8,128)S(1)}, u32[]{:S(2)}, u32[]{:S(2)}) collective-permute-start(f32[16,96,128]{2,1,0:T(8,128)S(1)} %constant_dynamic-update-slice_fusion.22.refs_4_), channel_id=1, source_target_pairs={{0,16},{16,0},{32,48},{48,32},{64,80},{80,64},{96,112},{112,96},{1... | collective-permute-start | bytes 2359304 | tf_op jit(solution)/shard_map/while/body/eval_jaxpr/ppermute | solution.py:42
  30.3 6.5 %collective-permute-start.6 = (f32[4,96,128]{2,1,0:T(8,128)S(1)}, f32[4,96,128]{2,1,0:T(8,128)S(1)}, u32[]{:S(2)}, u32[]{:S(2)}) collective-permute-start(f32[4,96,128]{2,1,0:T(8,128)S(1)} %constant_dynamic-update-slice_fusion.19.refs_4_), channel_id=1, source_target_pairs={{0,14},{1,15},{2,0},{3,1},{4,2},{5,3},{6,4},{7,5},{8,6},{9,7},{10,... | collective-permute-start | bytes 589832 | tf_op jit(solution)/shard_map/while/body/eval_jaxpr/ppermute | solution.py:42
  30.8 7.3 %collective-permute-start.7 = (f32[4,96,128]{2,1,0:T(8,128)S(1)}, f32[4,96,128]{2,1,0:T(8,128)S(1)}, u32[]{:S(2)}, u32[]{:S(2)}) collective-permute-start(f32[4,96,128]{2,1,0:T(8,128)S(1)} %constant_dynamic-update-slice_fusion.19.refs_4_), channel_id=1, source_target_pairs={{0,2},{1,3},{2,4},{3,5},{4,6},{5,7},{6,8},{7,9},{8,10},{9,11},{10,... | collective-permute-start | bytes 589832 | tf_op jit(solution)/shard_map/while/body/eval_jaxpr/ppermute | solution.py:42
  38.2 8.2 %collective-permute-start.10 = (f32[4,96,128]{2,1,0:T(8,128)S(1)}, f32[4,96,128]{2,1,0:T(8,128)S(1)}, u32[]{:S(2)}, u32[]{:S(2)}) collective-permute-start(f32[4,96,128]{2,1,0:T(8,128)S(1)} %collective-permute-done.7.refs_10_), channel_id=1, source_target_pairs={{0,2},{1,3},{2,4},{3,5},{4,6},{5,7},{6,8},{7,9},{8,10},{9,11},{10,... | collective-permute-start | bytes 589832 | tf_op jit(solution)/shard_map/while/body/eval_jaxpr/ppermute | solution.py:42
  38.9 7.6 %collective-permute-start.9 = (f32[4,96,128]{2,1,0:T(8,128)S(1)}, f32[4,96,128]{2,1,0:T(8,128)S(1)}, u32[]{:S(2)}, u32[]{:S(2)}) collective-permute-start(f32[4,96,128]{2,1,0:T(8,128)S(1)} %collective-permute-done.6.refs_5_), channel_id=1, source_target_pairs={{0,14},{1,15},{2,0},{3,1},{4,2},{5,3},{6,4},{7,5},{8,6},{9,7},{10,... | collective-permute-start | bytes 589832 | tf_op jit(solution)/shard_map/while/body/eval_jaxpr/ppermute | solution.py:42
  46.5 8.6 %collective-permute-start.12 = (f32[6,96,128]{2,1,0:T(8,128)S(1)}, f32[6,96,128]{2,1,0:T(8,128)S(1)}, u32[]{:S(2)}, u32[]{:S(2)}) collective-permute-start(f32[6,96,128]{2,1,0:T(8,128)S(1)} %pad_maximum_fusion.9), channel_id=1, source_target_pairs={{0,2},{1,3},{2,4},{3,5},{4,6},{5,7},{6,8},{7,9},{8,10},{9,11},{10,... | collective-permute-start | bytes 884744 | tf_op jit(solution)/shard_map/while/body/eval_jaxpr/ppermute | solution.py:42
  48.0 8.0 %collective-permute-start.11 = (f32[6,96,128]{2,1,0:T(8,128)S(1)}, f32[6,96,128]{2,1,0:T(8,128)S(1)}, u32[]{:S(2)}, u32[]{:S(2)}) collective-permute-start(f32[6,96,128]{2,1,0:T(8,128)S(1)} %pad_maximum_fusion.8), channel_id=1, source_target_pairs={{0,14},{1,15},{2,0},{3,1},{4,2},{5,3},{6,4},{7,5},{8,6},{9,7},{10,... | collective-permute-start | bytes 884744 | tf_op jit(solution)/shard_map/while/body/eval_jaxpr/ppermute | solution.py:42
  56.1 8.2 %collective-permute-start.14 = (f32[6,96,128]{2,1,0:T(8,128)S(1)}, f32[6,96,128]{2,1,0:T(8,128)S(1)}, u32[]{:S(2)}, u32[]{:S(2)}) collective-permute-start(f32[6,96,128]{2,1,0:T(8,128)S(1)} %pad_maximum_fusion.11), channel_id=1, source_target_pairs={{0,2},{1,3},{2,4},{3,5},{4,6},{5,7},{6,8},{7,9},{8,10},{9,11},{10,... | collective-permute-start | bytes 884744 | tf_op jit(solution)/shard_map/while/body/eval_jaxpr/ppermute | solution.py:42
  57.0 7.3 %collective-permute-start.13 = (f32[6,96,128]{2,1,0:T(8,128)S(1)}, f32[6,96,128]{2,1,0:T(8,128)S(1)}, u32[]{:S(2)}, u32[]{:S(2)}) collective-permute-start(f32[6,96,128]{2,1,0:T(8,128)S(1)} %pad_maximum_fusion.10), channel_id=1, source_target_pairs={{0,14},{1,15},{2,0},{3,1},{4,2},{5,3},{6,4},{7,5},{8,6},{9,7},{10,... | collective-permute-start | bytes 884744 | tf_op jit(solution)/shard_map/while/body/eval_jaxpr/ppermute | solution.py:42
  64.3 6.8 %collective-permute-start.16 = (f32[4,96,128]{2,1,0:T(8,128)S(1)}, f32[4,96,128]{2,1,0:T(8,128)S(1)}, u32[]{:S(2)}, u32[]{:S(2)}) collective-permute-start(f32[4,96,128]{2,1,0:T(8,128)S(1)} %slice_add_fusion.20), channel_id=1, source_target_pairs={{0,14},{1,15},{2,0},{3,1},{4,2},{5,3},{6,4},{7,5},{8,6},{9,7},{10,... | collective-permute-start | bytes 589832 | tf_op jit(solution)/shard_map/while/body/eval_jaxpr/ppermute | solution.py:42
  66.9 5.8 %collective-permute-start.15 = (f32[4,96,128]{2,1,0:T(8,128)S(1)}, f32[4,96,128]{2,1,0:T(8,128)S(1)}, u32[]{:S(2)}, u32[]{:S(2)}) collective-permute-start(f32[4,96,128]{2,1,0:T(8,128)S(1)} %slice_add_fusion.19), channel_id=1, source_target_pairs={{0,2},{1,3},{2,4},{3,5},{4,6},{5,7},{6,8},{7,9},{8,10},{9,11},{10,... | collective-permute-start | bytes 589832 | tf_op jit(solution)/shard_map/while/body/eval_jaxpr/ppermute | solution.py:42
  72.7 12.5 %collective-permute-start.19 = (f32[16,96,128]{2,1,0:T(8,128)S(1)}, f32[16,96,128]{2,1,0:T(8,128)S(1)}, u32[]{:S(2)}, u32[]{:S(2)}) collective-permute-start(f32[16,96,128]{2,1,0:T(8,128)S(1)} %get-tuple-element.649), channel_id=1, source_target_pairs={{0,16},{16,0},{32,48},{48,32},{64,80},{80,64},{96,112},{112,96},{1... | collective-permute-start | bytes 2359304 | tf_op jit(solution)/shard_map/while/body/eval_jaxpr/ppermute | solution.py:42
  77.0 6.6 %collective-permute-start.18 = (f32[4,96,128]{2,1,0:T(8,128)S(1)}, f32[4,96,128]{2,1,0:T(8,128)S(1)}, u32[]{:S(2)}, u32[]{:S(2)}) collective-permute-start(f32[4,96,128]{2,1,0:T(8,128)S(1)} %add.329), channel_id=1, source_target_pairs={{0,14},{1,15},{2,0},{3,1},{4,2},{5,3},{6,4},{7,5},{8,6},{9,7},{10,... | collective-permute-start | bytes 589832 | tf_op jit(solution)/shard_map/while/body/eval_jaxpr/ppermute | solution.py:42
  77.6 7.6 %collective-permute-start.17 = (f32[4,96,128]{2,1,0:T(8,128)S(1)}, f32[4,96,128]{2,1,0:T(8,128)}, u32[]{:S(2)}, u32[]{:S(2)}) collective-permute-start(f32[4,96,128]{2,1,0:T(8,128)S(1)} %add.328), channel_id=1, source_target_pairs={{0,2},{1,3},{2,4},{3,5},{4,6},{5,7},{6,8},{7,9},{8,10},{9,11},{10,... | collective-permute-start | bytes 589832 | tf_op jit(solution)/shard_map/while/body/eval_jaxpr/ppermute | solution.py:42
  86.1 6.9 %collective-permute-start.24 = (f32[2,96,128]{2,1,0:T(8,128)S(1)}, f32[2,96,128]{2,1,0:T(8,128)S(1)}, u32[]{:S(2)}, u32[]{:S(2)}) collective-permute-start(f32[2,96,128]{2,1,0:T(8,128)S(1)} %slice_add_fusion.23), channel_id=1, source_target_pairs={{0,1},{1,0},{2,3},{3,2},{4,5},{5,4},{6,7},{7,6},{8,9},{9,8},{10,11... | collective-permute-start | bytes 294920 | tf_op jit(solution)/shard_map/while/body/eval_jaxpr/ppermute | solution.py:42
  88.6 12.0 %collective-permute-start.20 = (f32[4,96,128]{2,1,0:T(8,128)S(1)}, f32[4,96,128]{2,1,0:T(8,128)S(1)}, u32[]{:S(2)}, u32[]{:S(2)}) collective-permute-start(f32[4,96,128]{2,1,0:T(8,128)S(1)} %get-tuple-element.653), channel_id=1, source_target_pairs={{0,96},{16,112},{32,0},{48,16},{64,32},{80,48},{96,64},{112,80},{1... | collective-permute-start | bytes 589832 | tf_op jit(solution)/shard_map/while/body/eval_jaxpr/ppermute | solution.py:42
  92.3 8.3 %collective-permute-start.21 = (f32[4,96,128]{2,1,0:T(8,128)S(1)}, f32[4,96,128]{2,1,0:T(8,128)S(1)}, u32[]{:S(2)}, u32[]{:S(2)}) collective-permute-start(f32[4,96,128]{2,1,0:T(8,128)S(1)} %get-tuple-element.654), channel_id=1, source_target_pairs={{0,64},{16,80},{32,96},{48,112},{64,0},{80,16},{96,32},{112,48},{1... | collective-permute-start | bytes 589832 | tf_op jit(solution)/shard_map/while/body/eval_jaxpr/ppermute | solution.py:42
  92.3 12.0 %collective-permute-start.22 = (f32[4,96,128]{2,1,0:T(8,128)S(1)}, f32[4,96,128]{2,1,0:T(8,128)S(1)}, u32[]{:S(2)}, u32[]{:S(2)}) collective-permute-start(f32[4,96,128]{2,1,0:T(8,128)S(1)} %get-tuple-element.655), channel_id=1, source_target_pairs={{0,32},{16,48},{32,64},{48,80},{64,96},{80,112},{96,0},{112,16},{1... | collective-permute-start | bytes 589832 | tf_op jit(solution)/shard_map/while/body/eval_jaxpr/ppermute | solution.py:42
  93.9 22.1 %collective-permute-start.25 = (f32[2,96,128]{2,1,0:T(8,128)S(1)}, f32[2,96,128]{2,1,0:T(8,128)S(1)}, u32[]{:S(2)}, u32[]{:S(2)}) collective-permute-start(f32[2,96,128]{2,1,0:T(8,128)S(1)} %add_add_fusion.2), channel_id=1, source_target_pairs={{0,0},{1,16},{2,32},{3,48},{4,64},{5,80},{6,96},{7,112},{8,128},{9... | collective-permute-start | bytes 294920 | tf_op jit(solution)/shard_map/while/body/eval_jaxpr/ppermute | solution.py:46
  104.3 11.7 %collective-permute-start.23 = (f32[2,96,128]{2,1,0:T(8,128)S(1)}, f32[2,96,128]{2,1,0:T(8,128)S(1)}, u32[]{:S(2)}, u32[]{:S(2)}) collective-permute-start(f32[2,96,128]{2,1,0:T(8,128)S(1)} %slice_add_fusion.22), channel_id=1, source_target_pairs={{0,128},{16,144},{32,160},{48,176},{64,192},{80,208},{96,224},{112... | collective-permute-start | bytes 294920 | tf_op jit(solution)/shard_map/while/body/eval_jaxpr/ppermute | solution.py:42
  116.1 22.8 %copy-start = (s32[1,1,176]{2,1,0:T(1,128)S(1)}, s32[1,1,176]{2,1,0:T(1,128)}, u32[]{:S(2)}) copy-start(s32[1,1,176]{2,1,0:T(1,128)} %get-tuple-element.696.refs_0_) | copy-start | bytes 2116 | tf_op jit(solution)/shard_map/while
  116.1 22.8 %copy-start.1 = (s32[1,1,176]{2,1,0:T(1,128)S(1)}, s32[1,1,176]{2,1,0:T(1,128)}, u32[]{:S(2)}) copy-start(s32[1,1,176]{2,1,0:T(1,128)} %get-tuple-element.697.refs_1_) | copy-start | bytes 2116 | tf_op jit(solution)/shard_map/while
  116.1 5.5 %collective-permute-start = (f32[2,96,128]{2,1,0:T(8,128)S(1)}, f32[2,96,128]{2,1,0:T(8,128)S(1)}, u32[]{:S(2)}, u32[]{:S(2)}) collective-permute-start(f32[2,96,128]{2,1,0:T(8,128)S(1)} %copy.29), channel_id=1, source_target_pairs={{0,128},{16,144},{32,160},{48,176},{64,192},{80,208},{96,224},{112... | collective-permute-start | bytes 294920 | tf_op jit(solution)/shard_map/while/body/eval_jaxpr/ppermute | solution.py:42
  116.2 11.0 %collective-permute-start.4 = (f32[2,96,128]{2,1,0:T(8,128)S(1)}, f32[2,96,128]{2,1,0:T(8,128)S(1)}, u32[]{:S(2)}, u32[]{:S(2)}) collective-permute-start(f32[2,96,128]{2,1,0:T(8,128)S(1)} %get-tuple-element.678), channel_id=1, source_target_pairs={{0,0},{1,16},{2,32},{3,48},{4,64},{5,80},{6,96},{7,112},{8,128},{9... | collective-permute-start | bytes 294920 | tf_op jit(solution)/shard_map/while/body/eval_jaxpr/ppermute | solution.py:46
  121.6 10.5 %collective-permute-start.1 = (f32[4,96,128]{2,1,0:T(8,128)S(1)}, f32[4,96,128]{2,1,0:T(8,128)S(1)}, u32[]{:S(2)}, u32[]{:S(2)}) collective-permute-start(f32[4,96,128]{2,1,0:T(8,128)S(1)} %get-tuple-element.597), channel_id=1, source_target_pairs={{0,96},{16,112},{32,0},{48,16},{64,32},{80,48},{96,64},{112,80},{1... | collective-permute-start | bytes 589832 | tf_op jit(solution)/shard_map/while/body/eval_jaxpr/ppermute | solution.py:42
  121.7 10.4 %collective-permute-start.2 = (f32[4,96,128]{2,1,0:T(8,128)S(1)}, f32[4,96,128]{2,1,0:T(8,128)S(1)}, u32[]{:S(2)}, u32[]{:S(2)}) collective-permute-start(f32[4,96,128]{2,1,0:T(8,128)S(1)} %get-tuple-element.597), channel_id=1, source_target_pairs={{0,64},{16,80},{32,96},{48,112},{64,0},{80,16},{96,32},{112,48},{1... | collective-permute-start | bytes 589832 | tf_op jit(solution)/shard_map/while/body/eval_jaxpr/ppermute | solution.py:42
  121.8 10.3 %collective-permute-start.3 = (f32[4,96,128]{2,1,0:T(8,128)S(1)}, f32[4,96,128]{2,1,0:T(8,128)S(1)}, u32[]{:S(2)}, u32[]{:S(2)}) collective-permute-start(f32[4,96,128]{2,1,0:T(8,128)S(1)} %get-tuple-element.597), channel_id=1, source_target_pairs={{0,32},{16,48},{32,64},{48,80},{64,96},{80,112},{96,0},{112,16},{1... | collective-permute-start | bytes 589832 | tf_op jit(solution)/shard_map/while/body/eval_jaxpr/ppermute | solution.py:42
  128.2 3.9 %collective-permute-start.5 = (f32[2,96,128]{2,1,0:T(8,128)S(1)}, f32[2,96,128]{2,1,0:T(8,128)S(1)}, u32[]{:S(2)}, u32[]{:S(2)}) collective-permute-start(f32[2,96,128]{2,1,0:T(8,128)S(1)} %select_add_fusion.2), channel_id=1, source_target_pairs={{0,1},{1,0},{2,3},{3,2},{4,5},{5,4},{6,7},{7,6},{8,9},{9,8},{10,11... | collective-permute-start | bytes 294920 | tf_op jit(solution)/shard_map/while/body/eval_jaxpr/ppermute | solution.py:42
  132.1 6.7 %collective-permute-start.8 = (f32[16,96,128]{2,1,0:T(8,128)S(1)}, f32[16,96,128]{2,1,0:T(8,128)S(1)}, u32[]{:S(2)}, u32[]{:S(2)}) collective-permute-start(f32[16,96,128]{2,1,0:T(8,128)S(1)} %constant_dynamic-update-slice_fusion.22.refs_4_), channel_id=1, source_target_pairs={{0,16},{16,0},{32,48},{48,32},{64,80},{80,64},{96,112},{112,96},{1... | collective-permute-start | bytes 2359304 | tf_op jit(solution)/shard_map/while/body/eval_jaxpr/ppermute | solution.py:42
  136.8 6.5 %collective-permute-start.6 = (f32[4,96,128]{2,1,0:T(8,128)S(1)}, f32[4,96,128]{2,1,0:T(8,128)S(1)}, u32[]{:S(2)}, u32[]{:S(2)}) collective-permute-start(f32[4,96,128]{2,1,0:T(8,128)S(1)} %constant_dynamic-update-slice_fusion.19.refs_4_), channel_id=1, source_target_pairs={{0,14},{1,15},{2,0},{3,1},{4,2},{5,3},{6,4},{7,5},{8,6},{9,7},{10,... | collective-permute-start | bytes 589832 | tf_op jit(solution)/shard_map/while/body/eval_jaxpr/ppermute | solution.py:42
  138.8 7.4 %collective-permute-start.7 = (f32[4,96,128]{2,1,0:T(8,128)S(1)}, f32[4,96,128]{2,1,0:T(8,128)S(1)}, u32[]{:S(2)}, u32[]{:S(2)}) collective-permute-start(f32[4,96,128]{2,1,0:T(8,128)S(1)} %constant_dynamic-update-slice_fusion.19.refs_4_), channel_id=1, source_target_pairs={{0,2},{1,3},{2,4},{3,5},{4,6},{5,7},{6,8},{7,9},{8,10},{9,11},{10,... | collective-permute-start | bytes 589832 | tf_op jit(solution)/shard_map/while/body/eval_jaxpr/ppermute | solution.py:42
  146.2 8.2 %collective-permute-start.10 = (f32[4,96,128]{2,1,0:T(8,128)S(1)}, f32[4,96,128]{2,1,0:T(8,128)S(1)}, u32[]{:S(2)}, u32[]{:S(2)}) collective-permute-start(f32[4,96,128]{2,1,0:T(8,128)S(1)} %collective-permute-done.7.refs_10_), channel_id=1, source_target_pairs={{0,2},{1,3},{2,4},{3,5},{4,6},{5,7},{6,8},{7,9},{8,10},{9,11},{10,... | collective-permute-start | bytes 589832 | tf_op jit(solution)/shard_map/while/body/eval_jaxpr/ppermute | solution.py:42
  146.4 8.0 %collective-permute-start.9 = (f32[4,96,128]{2,1,0:T(8,128)S(1)}, f32[4,96,128]{2,1,0:T(8,128)S(1)}, u32[]{:S(2)}, u32[]{:S(2)}) collective-permute-start(f32[4,96,128]{2,1,0:T(8,128)S(1)} %collective-permute-done.6.refs_5_), channel_id=1, source_target_pairs={{0,14},{1,15},{2,0},{3,1},{4,2},{5,3},{6,4},{7,5},{8,6},{9,7},{10,... | collective-permute-start | bytes 589832 | tf_op jit(solution)/shard_map/while/body/eval_jaxpr/ppermute | solution.py:42
  154.5 8.5 %collective-permute-start.12 = (f32[6,96,128]{2,1,0:T(8,128)S(1)}, f32[6,96,128]{2,1,0:T(8,128)S(1)}, u32[]{:S(2)}, u32[]{:S(2)}) collective-permute-start(f32[6,96,128]{2,1,0:T(8,128)S(1)} %pad_maximum_fusion.9), channel_id=1, source_target_pairs={{0,2},{1,3},{2,4},{3,5},{4,6},{5,7},{6,8},{7,9},{8,10},{9,11},{10,... | collective-permute-start | bytes 884744 | tf_op jit(solution)/shard_map/while/body/eval_jaxpr/ppermute | solution.py:42
  155.6 8.0 %collective-permute-start.11 = (f32[6,96,128]{2,1,0:T(8,128)S(1)}, f32[6,96,128]{2,1,0:T(8,128)S(1)}, u32[]{:S(2)}, u32[]{:S(2)}) collective-permute-start(f32[6,96,128]{2,1,0:T(8,128)S(1)} %pad_maximum_fusion.8), channel_id=1, source_target_pairs={{0,14},{1,15},{2,0},{3,1},{4,2},{5,3},{6,4},{7,5},{8,6},{9,7},{10,... | collective-permute-start | bytes 884744 | tf_op jit(solution)/shard_map/while/body/eval_jaxpr/ppermute | solution.py:42
  163.7 8.2 %collective-permute-start.14 = (f32[6,96,128]{2,1,0:T(8,128)S(1)}, f32[6,96,128]{2,1,0:T(8,128)S(1)}, u32[]{:S(2)}, u32[]{:S(2)}) collective-permute-start(f32[6,96,128]{2,1,0:T(8,128)S(1)} %pad_maximum_fusion.11), channel_id=1, source_target_pairs={{0,2},{1,3},{2,4},{3,5},{4,6},{5,7},{6,8},{7,9},{8,10},{9,11},{10,... | collective-permute-start | bytes 884744 | tf_op jit(solution)/shard_map/while/body/eval_jaxpr/ppermute | solution.py:42
  166.0 7.4 %collective-permute-start.13 = (f32[6,96,128]{2,1,0:T(8,128)S(1)}, f32[6,96,128]{2,1,0:T(8,128)S(1)}, u32[]{:S(2)}, u32[]{:S(2)}) collective-permute-start(f32[6,96,128]{2,1,0:T(8,128)S(1)} %pad_maximum_fusion.10), channel_id=1, source_target_pairs={{0,14},{1,15},{2,0},{3,1},{4,2},{5,3},{6,4},{7,5},{8,6},{9,7},{10,... | collective-permute-start | bytes 884744 | tf_op jit(solution)/shard_map/while/body/eval_jaxpr/ppermute | solution.py:42
  173.4 5.8 %collective-permute-start.16 = (f32[4,96,128]{2,1,0:T(8,128)S(1)}, f32[4,96,128]{2,1,0:T(8,128)S(1)}, u32[]{:S(2)}, u32[]{:S(2)}) collective-permute-start(f32[4,96,128]{2,1,0:T(8,128)S(1)} %slice_add_fusion.20), channel_id=1, source_target_pairs={{0,14},{1,15},{2,0},{3,1},{4,2},{5,3},{6,4},{7,5},{8,6},{9,7},{10,... | collective-permute-start | bytes 589832 | tf_op jit(solution)/shard_map/while/body/eval_jaxpr/ppermute | solution.py:42
  174.4 5.8 %collective-permute-start.15 = (f32[4,96,128]{2,1,0:T(8,128)S(1)}, f32[4,96,128]{2,1,0:T(8,128)S(1)}, u32[]{:S(2)}, u32[]{:S(2)}) collective-permute-start(f32[4,96,128]{2,1,0:T(8,128)S(1)} %slice_add_fusion.19), channel_id=1, source_target_pairs={{0,2},{1,3},{2,4},{3,5},{4,6},{5,7},{6,8},{7,9},{8,10},{9,11},{10,... | collective-permute-start | bytes 589832 | tf_op jit(solution)/shard_map/while/body/eval_jaxpr/ppermute | solution.py:42
  180.2 12.5 %collective-permute-start.19 = (f32[16,96,128]{2,1,0:T(8,128)S(1)}, f32[16,96,128]{2,1,0:T(8,128)S(1)}, u32[]{:S(2)}, u32[]{:S(2)}) collective-permute-start(f32[16,96,128]{2,1,0:T(8,128)S(1)} %get-tuple-element.649), channel_id=1, source_target_pairs={{0,16},{16,0},{32,48},{48,32},{64,80},{80,64},{96,112},{112,96},{1... | collective-permute-start | bytes 2359304 | tf_op jit(solution)/shard_map/while/body/eval_jaxpr/ppermute | solution.py:42
  184.5 6.6 %collective-permute-start.18 = (f32[4,96,128]{2,1,0:T(8,128)S(1)}, f32[4,96,128]{2,1,0:T(8,128)S(1)}, u32[]{:S(2)}, u32[]{:S(2)}) collective-permute-start(f32[4,96,128]{2,1,0:T(8,128)S(1)} %add.329), channel_id=1, source_target_pairs={{0,14},{1,15},{2,0},{3,1},{4,2},{5,3},{6,4},{7,5},{8,6},{9,7},{10,... | collective-permute-start | bytes 589832 | tf_op jit(solution)/shard_map/while/body/eval_jaxpr/ppermute | solution.py:42
  185.2 7.6 %collective-permute-start.17 = (f32[4,96,128]{2,1,0:T(8,128)S(1)}, f32[4,96,128]{2,1,0:T(8,128)}, u32[]{:S(2)}, u32[]{:S(2)}) collective-permute-start(f32[4,96,128]{2,1,0:T(8,128)S(1)} %add.328), channel_id=1, source_target_pairs={{0,2},{1,3},{2,4},{3,5},{4,6},{5,7},{6,8},{7,9},{8,10},{9,11},{10,... | collective-permute-start | bytes 589832 | tf_op jit(solution)/shard_map/while/body/eval_jaxpr/ppermute | solution.py:42
  193.6 9.6 %collective-permute-start.24 = (f32[2,96,128]{2,1,0:T(8,128)S(1)}, f32[2,96,128]{2,1,0:T(8,128)S(1)}, u32[]{:S(2)}, u32[]{:S(2)}) collective-permute-start(f32[2,96,128]{2,1,0:T(8,128)S(1)} %slice_add_fusion.23), channel_id=1, source_target_pairs={{0,1},{1,0},{2,3},{3,2},{4,5},{5,4},{6,7},{7,6},{8,9},{9,8},{10,11... | collective-permute-start | bytes 294920 | tf_op jit(solution)/shard_map/while/body/eval_jaxpr/ppermute | solution.py:42
  201.3 6.3 %collective-permute-start.20 = (f32[4,96,128]{2,1,0:T(8,128)S(1)}, f32[4,96,128]{2,1,0:T(8,128)S(1)}, u32[]{:S(2)}, u32[]{:S(2)}) collective-permute-start(f32[4,96,128]{2,1,0:T(8,128)S(1)} %get-tuple-element.653), channel_id=1, source_target_pairs={{0,96},{16,112},{32,0},{48,16},{64,32},{80,48},{96,64},{112,80},{1... | collective-permute-start | bytes 589832 | tf_op jit(solution)/shard_map/while/body/eval_jaxpr/ppermute | solution.py:42
  201.4 6.6 %collective-permute-start.21 = (f32[4,96,128]{2,1,0:T(8,128)S(1)}, f32[4,96,128]{2,1,0:T(8,128)S(1)}, u32[]{:S(2)}, u32[]{:S(2)}) collective-permute-start(f32[4,96,128]{2,1,0:T(8,128)S(1)} %get-tuple-element.654), channel_id=1, source_target_pairs={{0,64},{16,80},{32,96},{48,112},{64,0},{80,16},{96,32},{112,48},{1... | collective-permute-start | bytes 589832 | tf_op jit(solution)/shard_map/while/body/eval_jaxpr/ppermute | solution.py:42
  201.5 12.3 %collective-permute-start.22 = (f32[4,96,128]{2,1,0:T(8,128)S(1)}, f32[4,96,128]{2,1,0:T(8,128)S(1)}, u32[]{:S(2)}, u32[]{:S(2)}) collective-permute-start(f32[4,96,128]{2,1,0:T(8,128)S(1)} %get-tuple-element.655), channel_id=1, source_target_pairs={{0,32},{16,48},{32,64},{48,80},{64,96},{80,112},{96,0},{112,16},{1... | collective-permute-start | bytes 589832 | tf_op jit(solution)/shard_map/while/body/eval_jaxpr/ppermute | solution.py:42
  204.1 21.5 %collective-permute-start.25 = (f32[2,96,128]{2,1,0:T(8,128)S(1)}, f32[2,96,128]{2,1,0:T(8,128)S(1)}, u32[]{:S(2)}, u32[]{:S(2)}) collective-permute-start(f32[2,96,128]{2,1,0:T(8,128)S(1)} %add_add_fusion.2), channel_id=1, source_target_pairs={{0,0},{1,16},{2,32},{3,48},{4,64},{5,80},{6,96},{7,112},{8,128},{9... | collective-permute-start | bytes 294920 | tf_op jit(solution)/shard_map/while/body/eval_jaxpr/ppermute | solution.py:46
  213.8 11.9 %collective-permute-start.23 = (f32[2,96,128]{2,1,0:T(8,128)S(1)}, f32[2,96,128]{2,1,0:T(8,128)S(1)}, u32[]{:S(2)}, u32[]{:S(2)}) collective-permute-start(f32[2,96,128]{2,1,0:T(8,128)S(1)} %slice_add_fusion.22), channel_id=1, source_target_pairs={{0,128},{16,144},{32,160},{48,176},{64,192},{80,208},{96,224},{112... | collective-permute-start | bytes 294920 | tf_op jit(solution)/shard_map/while/body/eval_jaxpr/ppermute | solution.py:42

commit v4 on v3

--- a/solution.py
+++ b/solution.py
@@ -259,7 +259,7 @@
         out_specs=[vmem] * len(out_shape),
         out_shape=out_shape,
         scratch_shapes=scratch + held,
-        compiler_params=pltpu.CompilerParams(vmem_limit_bytes=49 << 20),
+        compiler_params=pltpu.CompilerParams(vmem_limit_bytes=24 << 20),
         cost_estimate=pl.CostEstimate(
             flops=24 * slots * vecs * bs * bs // share,
             bytes_accessed=4 * slots * bs * bs // share,
@@ -273,23 +273,24 @@
     center = (upper_bound[0] + lower_bound[0]) / 2.0
     half_width = (upper_bound[0] - lower_bound[0]) / 2.0
     here = (lax.axis_index("row"), lax.axis_index("col"), block_count[0, 0])
-    index = (block_row, block_col, jnp.stack(here).astype(jnp.int32), blocks)
-
-    def apply_hamiltonian(a0, flipping, finish):
+    index = (block_row, block_col, jnp.stack(here).astype(jnp.int32), pltpu.with_memory_space_constraint(blocks, pltpu.HBM))
+
+    def apply_hamiltonian(a0, flipping, offset, finish):
         a1 = send(a0, "row", X_HI)
-        _, flipping = bar(a1, flipping)
+        _, flipping, offset = bar(a1, flipping, offset)
         p0 = cat(a0, a1)
         p1 = send(p0, "row", Y_DOWN)
         p2 = send(p0, "row", Y_FAR)
         p3 = send(p0, "row", Y_UP)
-        t0 = finish(flipping)
+        t0 = finish(flipping, offset)
         t1 = send(t0, "col", X_LO)
         p1, p2, p3, t0, t1 = bar(p1, p2, p3, t0, t1)
         z0 = cat(t0, t1)
         up1 = send(z0, "col", Z_DOWN)
         down1 = send(z0, "col", Z_UP)
         p = cat(p0, p1, p2, p3)
-        state = products(False, True, False, (p, send(p, "row", CORE)), index)
+        c = send(p, "row", CORE)
+        state = products(False, True, False, (p, c), index)
         up1, down1, *state = bar(up1, down1, *state)
         up2 = send(up1, "col", Z_DOWN)
         down2 = send(down1, "col", Z_UP)
@@ -312,12 +313,12 @@
         u = send(f1 + u, "col", Z_UP)
         d = send(f7 + d, "col", Z_DOWN)
         o = send(other, "row", CORE)
-        u, d, o = bar(u, d, o)
-        h = send(f0[2:] + u[2:] + d[2:], "col", X_LO)
+        keep, away = bar(f0[:2] + u[:2] + d[:2], f0[2:] + u[2:] + d[2:])
+        h = send(away, "col", X_LO)
         q1 = send(g1 + o[4:8], "row", Y_UP)
         q2 = send(g2 + o[8:12], "row", Y_FAR)
         q3 = send(g3 + o[12:], "row", Y_DOWN)
-        (flipped,) = bar(f0[:2] + u[:2] + d[:2] + h)
+        (flipped,) = bar(keep + h)
         flipped_back = flip(flipped)
         last = send(g0[2:] + o[2:4] + q1[2:] + q2[2:] + q3[2:], "row", X_HI)
         (own,) = bar(g0[:2] + o[:2] + q1[:2] + q2[:2] + q3[:2] + last)
@@ -328,7 +329,7 @@
     def step(k, carry):
         before, now, flipping, scale, base = carry
         own, flipped, back, now_flipped = apply_hamiltonian(
-            now, flip(flipping), lambda x: x * scale + base
+            now, flip(flipping), base, lambda x, y: x * scale + y
         )
         later = (own + back - center * now) / half_width
         later = jnp.where(k == 0, later, 2.0 * later - before)

time: 227 us -> 217 us (0.956)
  the two profiles are of different devices: /device:TPU:5 before, /device:TPU:7 now
where the time goes in v4:
time: 217 us; the launch traced here: 216 us
  starting transfers between devices  107 us (49%)
  waiting for transfers between devices  79.6 us (37%)
  Pallas kernels  24.1 us (11%)
    ppermute x48, starting transfers between devices, send(): return lax.ppermute(x, axis, perm)  77.2 us
    ppermute x48, waiting for transfers between devices, send(): return lax.ppermute(x, axis, perm)  73.9 us
    ppermute x4, starting transfers between devices, flip(): return lax.ppermute(x, ('row', 'col'), FLIP)  30 us
    pallas_call x8, Pallas kernels, products(): pl.pallas_call(kernel, in_specs=[smem] * 3 + [pl.BlockSpec(memory_space=p...  24.1 us
    ppermute x4, waiting for transfers between devices, flip(): return lax.ppermute(x, ('row', 'col'), FLIP)  5.63 us
  transfers between devices with their start and end apart: 52, of which 28 were waited for; matrix products, arithmetic and copies ran while one was open for 0% of the time, Pallas kernels for 11%

profile of v4, /device:TPU:7, one launch (start us, length us, event | category | flops | bytes accessed | tf_op | source)
XLA Modules:
  0.0 216.4 jit_solution(6064517958086151086)
XLA Ops:
  1.3 0.9 reshape.12
  3.1 212.7 %while.23 = (s32[]{:T(128)}, f32[2,96,128]{2,1,0:T(8,128)S(1)}, f32[2,96,128]{2,1,0:T(8,128)S(1)}, f32[2,96,128]{2,1,0:T(8,128)S(1)}, f32[]{:T(128)}, /*index=5*...) while((s32[]{:T(128)}, f32[2,96,128]{2,1,0:T(8,128)S(1)}, ...), condition=%wide.region_1.2_spmd.clone, body=%wide.region_0.1_spmd.clone.sunk | while | flops 14119526400 | bytes 62954232 | solution.py:340
  3.1 1.2 collective-permute-start
  4.3 10.4 %collective-permute-start.4 = (f32[2,96,128]{2,1,0:T(8,128)S(1)}, f32[2,96,128]{2,1,0:T(8,128)S(1)}, u32[]{:S(2)}, u32[]{:S(2)}) collective-permute-start(f32[2,96,128]{2,1,0:T(8,128)S(1)} %get-tuple-element.684), channel_id=1, source_target_pairs={{0,0},{1,16},{2,32},{3,48},{4,64},{5,80},{6,96},{7,112},{8,128},{9... | collective-permute-start | bytes 294920 | tf_op jit(solution)/shard_map/while/body/eval_jaxpr/ppermute | solution.py:46
  14.8 1.1 collective-permute-start.1
  15.9 1.5 collective-permute-start.2
  17.5 1.2 collective-permute-done.4
  18.8 4.1 %collective-permute-done.5 = f32[2,96,128]{2,1,0:T(8,128)S(1)} collective-permute-done((f32[2,96,128]{2,1,0:T(8,128)S(1)}, f32[2,96,128]{2,1,0:T(8,128)S(1)}, u32[]{:S(2)}, u32[]{:S(2)}) %collective-permute-start.5) | collective-permute-done | bytes 98336 | tf_op jit(solution)/shard_map/while/body/eval_jaxpr/ppermute | solution.py:42
  22.9 2.3 %collective-permute-done.2 = f32[4,96,128]{2,1,0:T(8,128)S(1)} collective-permute-done((f32[4,96,128]{2,1,0:T(8,128)S(1)}, f32[4,96,128]{2,1,0:T(8,128)S(1)}, u32[]{:S(2)}, u32[]{:S(2)}) %collective-permute-start.2) | collective-permute-done | bytes 196640 | tf_op jit(solution)/shard_map/while/body/eval_jaxpr/ppermute | solution.py:42
  25.2 4.2 %collective-permute-done.3 = f32[4,96,128]{2,1,0:T(8,128)S(1)} collective-permute-done((f32[4,96,128]{2,1,0:T(8,128)S(1)}, f32[4,96,128]{2,1,0:T(8,128)S(1)}, u32[]{:S(2)}, u32[]{:S(2)}) %collective-permute-start.3) | collective-permute-done | bytes 196640 | tf_op jit(solution)/shard_map/while/body/eval_jaxpr/ppermute | solution.py:42
  30.6 1.0 collective-permute-start.7
  32.0 2.7 %eval_jaxpr.24 = (bf16[32,96,256]{2,1,0:T(8,128)(2,1)S(1)}, f32[32,96,128]{2,1,0:T(8,128)S(1)}) custom-call(s32[1,1,176]{2,1,0:T(1,128)S(1)} %copy-done, s32[1,1,176]{2,1,0:T(1,128)S(1)} %copy-done.1, s32[3]{0:T(128)S(1)} %get-tuple-element.704.refs_2_, f32[1,1,176,128,128]{4,3,2,1,0:T(8,128)} %get-tuple-element.705.refs_3_, ...), custom_call_target="tpu_custom_call" | custom-call | flops 3321888768 | bytes 5767168 | tf_op jit(solution)/shard_map/while/body/eval_jaxpr/pallas_call | solution.py:256
  34.7 1.9 collective-permute-done.6.refs_5_
  36.6 1.4 collective-permute-done.7.refs_10_
  38.0 2.7 %collective-permute-start.9 = (f32[4,96,128]{2,1,0:T(8,128)S(1)}, f32[4,96,128]{2,1,0:T(8,128)S(1)}, u32[]{:S(2)}, u32[]{:S(2)}) collective-permute-start(f32[4,96,128]{2,1,0:T(8,128)S(1)} %collective-permute-done.6.refs_5_), channel_id=1, source_target_pairs={{0,14},{1,15},{2,0},{3,1},{4,2},{5,3},{6,4},{7,5},{8,6},{9,7},{10,... | collective-permute-start | bytes 589832 | tf_op jit(solution)/shard_map/while/body/eval_jaxpr/ppermute | solution.py:42
  40.7 2.8 %eval_jaxpr.25 = (f32[4,96,128]{2,1,0:T(8,128)S(1)}, f32[4,96,128]{2,1,0:T(8,128)S(1)}, f32[4,96,128]{2,1,0:T(8,128)S(1)}, f32[4,96,128]{2,1,0:T(8,128)S(1)}, f3...) custom-call(s32[1,1,176]{2,1,0:T(1,128)S(1)} %copy-done, ...), custom_call_target="tpu_custom_call" | custom-call | flops 3321888768 | bytes 5767168 | tf_op jit(solution)/shard_map/while/body/eval_jaxpr/pallas_call | solution.py:256
  43.5 1.0 collective-permute-done.10.refs_9_
  44.6 2.7 %collective-permute-start.11 = (f32[6,96,128]{2,1,0:T(8,128)S(1)}, f32[6,96,128]{2,1,0:T(8,128)S(1)}, u32[]{:S(2)}, u32[]{:S(2)}) collective-permute-start(f32[6,96,128]{2,1,0:T(8,128)S(1)} %pad_maximum_fusion.8), channel_id=1, source_target_pairs={{0,14},{1,15},{2,0},{3,1},{4,2},{5,3},{6,4},{7,5},{8,6},{9,7},{10,... | collective-permute-start | bytes 884744 | tf_op jit(solution)/shard_map/while/body/eval_jaxpr/ppermute | solution.py:42
  47.4 4.0 %collective-permute-done.12.refs_8_ = f32[6,96,128]{2,1,0:T(8,128)S(1)} collective-permute-done((f32[6,96,128]{2,1,0:T(8,128)S(1)}, f32[6,96,128]{2,1,0:T(8,128)S(1)}, u32[]{:S(2)}, u32[]{:S(2)}) %collective-permute-start.12) | collective-permute-done | bytes 294944 | tf_op jit(solution)/shard_map/while/body/eval_jaxpr/ppermute | solution.py:42
  51.5 3.0 %collective-permute-start.14 = (f32[6,96,128]{2,1,0:T(8,128)S(1)}, f32[6,96,128]{2,1,0:T(8,128)S(1)}, u32[]{:S(2)}, u32[]{:S(2)}) collective-permute-start(f32[6,96,128]{2,1,0:T(8,128)S(1)} %pad_maximum_fusion.11), channel_id=1, source_target_pairs={{0,2},{1,3},{2,4},{3,5},{4,6},{5,7},{6,8},{7,9},{8,10},{9,11},{10,... | collective-permute-start | bytes 884744 | tf_op jit(solution)/shard_map/while/body/eval_jaxpr/ppermute | solution.py:42
  54.6 2.9 %eval_jaxpr.26.refs_6_ = f32[32,96,128]{2,1,0:T(8,128)S(1)} custom-call(s32[1,1,176]{2,1,0:T(1,128)S(1)} %copy-done, s32[1,1,176]{2,1,0:T(1,128)S(1)} %copy-done.1, s32[3]{0:T(128)S(1)} %get-tuple-element.704.refs_2_, f32[1,1,176,128,128]{4,3,2,1,0:T(8,128)} %get-tuple-element.705.refs_3_, f32[4,96,128]{2,1,0:T(8,128)S(1)} %constant_dynamic-update-slice_fusion.19.refs_4_, ...), custom_call_target="tpu_custom_call" | custom-call | flops 6643777536 | bytes 11534336 | tf_op jit(solution)/shard_map/while/body/eval_jaxpr/pallas_call | solution.py:256
  57.5 1.7 collective-permute-done.14.refs_4_
  59.2 1.4 collective-permute-done.13.refs_5_
  60.6 1.8 collective-permute-start.16
  62.4 2.6 %collective-permute-start.15 = (f32[4,96,128]{2,1,0:T(8,128)S(1)}, f32[4,96,128]{2,1,0:T(8,128)S(1)}, u32[]{:S(2)}, u32[]{:S(2)}) collective-permute-start(f32[4,96,128]{2,1,0:T(8,128)S(1)} %slice_add_fusion.24), channel_id=1, source_target_pairs={{0,2},{1,3},{2,4},{3,5},{4,6},{5,7},{6,8},{7,9},{8,10},{9,11},{10,... | collective-permute-start | bytes 589832 | tf_op jit(solution)/shard_map/while/body/eval_jaxpr/ppermute | solution.py:42
  65.0 3.7 %eval_jaxpr.27 = (f32[4,96,128]{2,1,0:T(8,128)S(1)}, f32[4,96,128]{2,1,0:T(8,128)S(1)}, f32[4,96,128]{2,1,0:T(8,128)S(1)}, f32[4,96,128]{2,1,0:T(8,128)S(1)}, f32[16,96,128]{2,1,0:T(8,128)S(1)}) custom-call(s32[1,1,176]{2,1,0:T(1,128)S(1)} %copy-done, s32[1,1,176]{2,1,0:T(1,128)S(1)} %copy-done.1, s32[3]{0:T(128)S(1)} %get-tuple-element.704.refs_2_, ...), custom_call_target="tpu_custom_call" | custom-call | flops 830472192 | bytes 1441792 | tf_op jit(solution)/shard_map/while/body/eval_jaxpr/pallas_call | solution.py:256
  68.8 9.6 %collective-permute-start.17 = (f32[16,96,128]{2,1,0:T(8,128)S(1)}, f32[16,96,128]{2,1,0:T(8,128)S(1)}, u32[]{:S(2)}, u32[]{:S(2)}) collective-permute-start(f32[16,96,128]{2,1,0:T(8,128)S(1)} %get-tuple-element.650), channel_id=1, source_target_pairs={{0,16},{16,0},{32,48},{48,32},{64,80},{80,64},{96,112},{112,96},{1... | collective-permute-start | bytes 2359304 | tf_op jit(solution)/shard_map/while/body/eval_jaxpr/ppermute | solution.py:42
  78.5 2.7 %collective-permute-start.22 = (f32[4,96,128]{2,1,0:T(8,128)S(1)}, f32[4,96,128]{2,1,0:T(8,128)S(1)}, u32[]{:S(2)}, u32[]{:S(2)}) collective-permute-start(f32[4,96,128]{2,1,0:T(8,128)S(1)} %add.330), channel_id=1, source_target_pairs={{0,14},{1,15},{2,0},{3,1},{4,2},{5,3},{6,4},{7,5},{8,6},{9,7},{10,... | collective-permute-start | bytes 589832 | tf_op jit(solution)/shard_map/while/body/eval_jaxpr/ppermute | solution.py:42
  81.3 4.0 %collective-permute-start.18 = (f32[4,96,128]{2,1,0:T(8,128)S(1)}, f32[4,96,128]{2,1,0:T(8,128)S(1)}, u32[]{:S(2)}, u32[]{:S(2)}) collective-permute-start(f32[4,96,128]{2,1,0:T(8,128)S(1)} %get-tuple-element.653), channel_id=1, source_target_pairs={{0,96},{16,112},{32,0},{48,16},{64,32},{80,48},{96,64},{112,80},{1... | collective-permute-start | bytes 589832 | tf_op jit(solution)/shard_map/while/body/eval_jaxpr/ppermute | solution.py:42
  86.3 3.5 %collective-permute-done.24 = f32[2,96,128]{2,1,0:T(8,128)S(1)} collective-permute-done((f32[2,96,128]{2,1,0:T(8,128)S(1)}, f32[2,96,128]{2,1,0:T(8,128)S(1)}, u32[]{:S(2)}, u32[]{:S(2)}) %collective-permute-start.24) | collective-permute-done | bytes 98336 | tf_op jit(solution)/shard_map/while/body/eval_jaxpr/ppermute | solution.py:42
  89.7 6.5 %collective-permute-start.25 = (f32[2,96,128]{2,1,0:T(8,128)S(1)}, f32[2,96,128]{2,1,0:T(8,128)S(1)}, u32[]{:S(2)}, u32[]{:S(2)}) collective-permute-start(f32[2,96,128]{2,1,0:T(8,128)S(1)} %add.332), channel_id=1, source_target_pairs={{0,0},{1,16},{2,32},{3,48},{4,64},{5,80},{6,96},{7,112},{8,128},{9... | collective-permute-start | bytes 294920 | tf_op jit(solution)/shard_map/while/body/eval_jaxpr/ppermute | solution.py:46
  96.3 0.9 collective-permute-done.20
  97.3 1.3 collective-permute-start.21
  98.6 12.5 %collective-permute-done.21 = f32[2,96,128]{2,1,0:T(8,128)S(1)} collective-permute-done((f32[2,96,128]{2,1,0:T(8,128)S(1)}, f32[2,96,128]{2,1,0:T(8,128)S(1)}, u32[]{:S(2)}, u32[]{:S(2)}) %collective-permute-start.21) | collective-permute-done | bytes 98336 | tf_op jit(solution)/shard_map/while/body/eval_jaxpr/ppermute | solution.py:42
  111.4 6.6 %collective-permute-start.4 = (f32[2,96,128]{2,1,0:T(8,128)S(1)}, f32[2,96,128]{2,1,0:T(8,128)S(1)}, u32[]{:S(2)}, u32[]{:S(2)}) collective-permute-start(f32[2,96,128]{2,1,0:T(8,128)S(1)} %get-tuple-element.684), channel_id=1, source_target_pairs={{0,0},{1,16},{2,32},{3,48},{4,64},{5,80},{6,96},{7,112},{8,128},{9... | collective-permute-start | bytes 294920 | tf_op jit(solution)/shard_map/while/body/eval_jaxpr/ppermute | solution.py:46
  118.1 1.7 collective-permute-start.1
  120.5 4.5 %collective-permute-done.4 = f32[2,96,128]{2,1,0:T(8,128)S(1)} collective-permute-done((f32[2,96,128]{2,1,0:T(8,128)S(1)}, f32[2,96,128]{2,1,0:T(8,128)S(1)}, u32[]{:S(2)}, u32[]{:S(2)}) %collective-permute-start.4) | collective-permute-done | bytes 98336 | tf_op jit(solution)/shard_map/while/body/eval_jaxpr/ppermute | solution.py:46
  125.1 3.5 %collective-permute-done.5 = f32[2,96,128]{2,1,0:T(8,128)S(1)} collective-permute-done((f32[2,96,128]{2,1,0:T(8,128)S(1)}, f32[2,96,128]{2,1,0:T(8,128)S(1)}, u32[]{:S(2)}, u32[]{:S(2)}) %collective-permute-start.5) | collective-permute-done | bytes 98336 | tf_op jit(solution)/shard_map/while/body/eval_jaxpr/ppermute | solution.py:42
  128.7 7.5 %collective-permute-start.8 = (f32[16,96,128]{2,1,0:T(8,128)S(1)}, f32[16,96,128]{2,1,0:T(8,128)S(1)}, u32[]{:S(2)}, u32[]{:S(2)}) collective-permute-start(f32[16,96,128]{2,1,0:T(8,128)S(1)} %constant_dynamic-update-slice_fusion.22.refs_4_), channel_id=1, source_target_pairs={{0,16},{16,0},{32,48},{48,32},{64,80},{80,64},{96,112},{112,96},{1... | collective-permute-start | bytes 2359304 | tf_op jit(solution)/shard_map/while/body/eval_jaxpr/ppermute | solution.py:42
  136.3 1.5 collective-permute-start.7
  138.1 2.7 %eval_jaxpr.24 = (bf16[32,96,256]{2,1,0:T(8,128)(2,1)S(1)}, f32[32,96,128]{2,1,0:T(8,128)S(1)}) custom-call(s32[1,1,176]{2,1,0:T(1,128)S(1)} %copy-done, s32[1,1,176]{2,1,0:T(1,128)S(1)} %copy-done.1, s32[3]{0:T(128)S(1)} %get-tuple-element.704.refs_2_, f32[1,1,176,128,128]{4,3,2,1,0:T(8,128)} %get-tuple-element.705.refs_3_, ...), custom_call_target="tpu_custom_call" | custom-call | flops 3321888768 | bytes 5767168 | tf_op jit(solution)/shard_map/while/body/eval_jaxpr/pallas_call | solution.py:256
  140.8 1.9 collective-permute-done.6.refs_5_
  142.8 1.3 collective-permute-done.7.refs_10_
  144.1 1.1 collective-permute-start.10
  145.2 1.6 collective-permute-start.9
  146.7 2.8 %eval_jaxpr.25 = (f32[4,96,128]{2,1,0:T(8,128)S(1)}, f32[4,96,128]{2,1,0:T(8,128)S(1)}, f32[4,96,128]{2,1,0:T(8,128)S(1)}, f32[4,96,128]{2,1,0:T(8,128)S(1)}, f3...) custom-call(s32[1,1,176]{2,1,0:T(1,128)S(1)} %copy-done, ...), custom_call_target="tpu_custom_call" | custom-call | flops 3321888768 | bytes 5767168 | tf_op jit(solution)/shard_map/while/body/eval_jaxpr/pallas_call | solution.py:256
  149.5 1.3 collective-permute-done.10.refs_9_
  151.7 2.0 collective-permute-start.11
  153.7 4.0 %collective-permute-done.12.refs_8_ = f32[6,96,128]{2,1,0:T(8,128)S(1)} collective-permute-done((f32[6,96,128]{2,1,0:T(8,128)S(1)}, f32[6,96,128]{2,1,0:T(8,128)S(1)}, u32[]{:S(2)}, u32[]{:S(2)}) %collective-permute-start.12) | collective-permute-done | bytes 294944 | tf_op jit(solution)/shard_map/while/body/eval_jaxpr/ppermute | solution.py:42
  157.8 2.5 %collective-permute-start.14 = (f32[6,96,128]{2,1,0:T(8,128)S(1)}, f32[6,96,128]{2,1,0:T(8,128)S(1)}, u32[]{:S(2)}, u32[]{:S(2)}) collective-permute-start(f32[6,96,128]{2,1,0:T(8,128)S(1)} %pad_maximum_fusion.11), channel_id=1, source_target_pairs={{0,2},{1,3},{2,4},{3,5},{4,6},{5,7},{6,8},{7,9},{8,10},{9,11},{10,... | collective-permute-start | bytes 884744 | tf_op jit(solution)/shard_map/while/body/eval_jaxpr/ppermute | solution.py:42
  160.8 2.9 %eval_jaxpr.26.refs_6_ = f32[32,96,128]{2,1,0:T(8,128)S(1)} custom-call(s32[1,1,176]{2,1,0:T(1,128)S(1)} %copy-done, s32[1,1,176]{2,1,0:T(1,128)S(1)} %copy-done.1, s32[3]{0:T(128)S(1)} %get-tuple-element.704.refs_2_, f32[1,1,176,128,128]{4,3,2,1,0:T(8,128)} %get-tuple-element.705.refs_3_, f32[4,96,128]{2,1,0:T(8,128)S(1)} %constant_dynamic-update-slice_fusion.19.refs_4_, ...), custom_call_target="tpu_custom_call" | custom-call | flops 6643777536 | bytes 11534336 | tf_op jit(solution)/shard_map/while/body/eval_jaxpr/pallas_call | solution.py:256
  163.7 1.4 collective-permute-done.14.refs_4_
  165.0 1.5 collective-permute-done.13.refs_5_
  166.5 1.6 collective-permute-start.16
  168.2 3.3 %collective-permute-start.15 = (f32[4,96,128]{2,1,0:T(8,128)S(1)}, f32[4,96,128]{2,1,0:T(8,128)S(1)}, u32[]{:S(2)}, u32[]{:S(2)}) collective-permute-start(f32[4,96,128]{2,1,0:T(8,128)S(1)} %slice_add_fusion.24), channel_id=1, source_target_pairs={{0,2},{1,3},{2,4},{3,5},{4,6},{5,7},{6,8},{7,9},{8,10},{9,11},{10,... | collective-permute-start | bytes 589832 | tf_op jit(solution)/shard_map/while/body/eval_jaxpr/ppermute | solution.py:42
  171.5 3.7 %eval_jaxpr.27 = (f32[4,96,128]{2,1,0:T(8,128)S(1)}, f32[4,96,128]{2,1,0:T(8,128)S(1)}, f32[4,96,128]{2,1,0:T(8,128)S(1)}, f32[4,96,128]{2,1,0:T(8,128)S(1)}, f32[16,96,128]{2,1,0:T(8,128)S(1)}) custom-call(s32[1,1,176]{2,1,0:T(1,128)S(1)} %copy-done, s32[1,1,176]{2,1,0:T(1,128)S(1)} %copy-done.1, s32[3]{0:T(128)S(1)} %get-tuple-element.704.refs_2_, ...), custom_call_target="tpu_custom_call" | custom-call | flops 830472192 | bytes 1441792 | tf_op jit(solution)/shard_map/while/body/eval_jaxpr/pallas_call | solution.py:256
  175.2 8.3 %collective-permute-start.17 = (f32[16,96,128]{2,1,0:T(8,128)S(1)}, f32[16,96,128]{2,1,0:T(8,128)S(1)}, u32[]{:S(2)}, u32[]{:S(2)}) collective-permute-start(f32[16,96,128]{2,1,0:T(8,128)S(1)} %get-tuple-element.650), channel_id=1, source_target_pairs={{0,16},{16,0},{32,48},{48,32},{64,80},{80,64},{96,112},{112,96},{1... | collective-permute-start | bytes 2359304 | tf_op jit(solution)/shard_map/while/body/eval_jaxpr/ppermute | solution.py:42
  183.6 2.7 %collective-permute-start.22 = (f32[4,96,128]{2,1,0:T(8,128)S(1)}, f32[4,96,128]{2,1,0:T(8,128)S(1)}, u32[]{:S(2)}, u32[]{:S(2)}) collective-permute-start(f32[4,96,128]{2,1,0:T(8,128)S(1)} %add.330), channel_id=1, source_target_pairs={{0,14},{1,15},{2,0},{3,1},{4,2},{5,3},{6,4},{7,5},{8,6},{9,7},{10,... | collective-permute-start | bytes 589832 | tf_op jit(solution)/shard_map/while/body/eval_jaxpr/ppermute | solution.py:42
  186.5 1.8 collective-permute-start.18
  188.9 2.4 %collective-permute-done.23 = f32[4,96,128]{2,1,0:T(8,128)S(1)} collective-permute-done((f32[4,96,128]{2,1,0:T(8,128)S(1)}, f32[4,96,128]{2,1,0:T(8,128)S(1)}, u32[]{:S(2)}, u32[]{:S(2)}) %collective-permute-start.23) | collective-permute-done | bytes 196640 | tf_op jit(solution)/shard_map/while/body/eval_jaxpr/ppermute | solution.py:42
  191.3 0.9 collective-permute-start.24
  192.2 3.0 %collective-permute-done.24 = f32[2,96,128]{2,1,0:T(8,128)S(1)} collective-permute-done((f32[2,96,128]{2,1,0:T(8,128)S(1)}, f32[2,96,128]{2,1,0:T(8,128)S(1)}, u32[]{:S(2)}, u32[]{:S(2)}) %collective-permute-start.24) | collective-permute-done | bytes 98336 | tf_op jit(solution)/shard_map/while/body/eval_jaxpr/ppermute | solution.py:42
  195.2 6.5 %collective-permute-start.25 = (f32[2,96,128]{2,1,0:T(8,128)S(1)}, f32[2,96,128]{2,1,0:T(8,128)S(1)}, u32[]{:S(2)}, u32[]{:S(2)}) collective-permute-start(f32[2,96,128]{2,1,0:T(8,128)S(1)} %add.332), channel_id=1, source_target_pairs={{0,0},{1,16},{2,32},{3,48},{4,64},{5,80},{6,96},{7,112},{8,128},{9... | collective-permute-start | bytes 294920 | tf_op jit(solution)/shard_map/while/body/eval_jaxpr/ppermute | solution.py:46
  201.9 13.8 %collective-permute-done.21 = f32[2,96,128]{2,1,0:T(8,128)S(1)} collective-permute-done((f32[2,96,128]{2,1,0:T(8,128)S(1)}, f32[2,96,128]{2,1,0:T(8,128)S(1)}, u32[]{:S(2)}, u32[]{:S(2)}) %collective-permute-start.21) | collective-permute-done | bytes 98336 | tf_op jit(solution)/shard_map/while/body/eval_jaxpr/ppermute | solution.py:42
  (118 shorter events, 8.4 us)
Async XLA Ops:
  3.1 28.9 %copy-start = (s32[1,1,176]{2,1,0:T(1,128)S(1)}, s32[1,1,176]{2,1,0:T(1,128)}, u32[]{:S(2)}) copy-start(s32[1,1,176]{2,1,0:T(1,128)} %get-tuple-element.702.refs_0_) | copy-start | bytes 2116 | tf_op jit(solution)/shard_map/while
  3.1 28.9 %copy-start.1 = (s32[1,1,176]{2,1,0:T(1,128)S(1)}, s32[1,1,176]{2,1,0:T(1,128)}, u32[]{:S(2)}) copy-start(s32[1,1,176]{2,1,0:T(1,128)} %get-tuple-element.703.refs_1_) | copy-start | bytes 2116 | tf_op jit(solution)/shard_map/while
  3.1 11.6 %collective-permute-start = (f32[2,96,128]{2,1,0:T(8,128)S(1)}, f32[2,96,128]{2,1,0:T(8,128)S(1)}, u32[]{:S(2)}, u32[]{:S(2)}) collective-permute-start(f32[2,96,128]{2,1,0:T(8,128)S(1)} %copy.29), channel_id=1, source_target_pairs={{0,128},{16,144},{32,160},{48,176},{64,192},{80,208},{96,224},{112... | collective-permute-start | bytes 294920 | tf_op jit(solution)/shard_map/while/body/eval_jaxpr/ppermute | solution.py:42
  4.3 14.3 %collective-permute-start.4 = (f32[2,96,128]{2,1,0:T(8,128)S(1)}, f32[2,96,128]{2,1,0:T(8,128)S(1)}, u32[]{:S(2)}, u32[]{:S(2)}) collective-permute-start(f32[2,96,128]{2,1,0:T(8,128)S(1)} %get-tuple-element.684), channel_id=1, source_target_pairs={{0,0},{1,16},{2,32},{3,48},{4,64},{5,80},{6,96},{7,112},{8,128},{9... | collective-permute-start | bytes 294920 | tf_op jit(solution)/shard_map/while/body/eval_jaxpr/ppermute | solution.py:46
  14.8 8.2 %collective-permute-start.1 = (f32[4,96,128]{2,1,0:T(8,128)S(1)}, f32[4,96,128]{2,1,0:T(8,128)S(1)}, u32[]{:S(2)}, u32[]{:S(2)}) collective-permute-start(f32[4,96,128]{2,1,0:T(8,128)S(1)} %get-tuple-element.601), channel_id=1, source_target_pairs={{0,96},{16,112},{32,0},{48,16},{64,32},{80,48},{96,64},{112,80},{1... | collective-permute-start | bytes 589832 | tf_op jit(solution)/shard_map/while/body/eval_jaxpr/ppermute | solution.py:42
  15.9 9.3 %collective-permute-start.2 = (f32[4,96,128]{2,1,0:T(8,128)S(1)}, f32[4,96,128]{2,1,0:T(8,128)S(1)}, u32[]{:S(2)}, u32[]{:S(2)}) collective-permute-start(f32[4,96,128]{2,1,0:T(8,128)S(1)} %get-tuple-element.601), channel_id=1, source_target_pairs={{0,64},{16,80},{32,96},{48,112},{64,0},{80,16},{96,32},{112,48},{1... | collective-permute-start | bytes 589832 | tf_op jit(solution)/shard_map/while/body/eval_jaxpr/ppermute | solution.py:42
  17.4 12.0 %collective-permute-start.3 = (f32[4,96,128]{2,1,0:T(8,128)S(1)}, f32[4,96,128]{2,1,0:T(8,128)S(1)}, u32[]{:S(2)}, u32[]{:S(2)}) collective-permute-start(f32[4,96,128]{2,1,0:T(8,128)S(1)} %get-tuple-element.601), channel_id=1, source_target_pairs={{0,32},{16,48},{32,64},{48,80},{64,96},{80,112},{96,0},{112,16},{1... | collective-permute-start | bytes 589832 | tf_op jit(solution)/shard_map/while/body/eval_jaxpr/ppermute | solution.py:42
  18.7 4.2 %collective-permute-start.5 = (f32[2,96,128]{2,1,0:T(8,128)S(1)}, f32[2,96,128]{2,1,0:T(8,128)S(1)}, u32[]{:S(2)}, u32[]{:S(2)}) collective-permute-start(f32[2,96,128]{2,1,0:T(8,128)S(1)} %multiply_add_fusion.2), channel_id=1, source_target_pairs={{0,1},{1,0},{2,3},{3,2},{4,5},{5,4},{6,7},{7,6},{8,9},{9,8},{10,11... | collective-permute-start | bytes 294920 | tf_op jit(solution)/shard_map/while/body/eval_jaxpr/ppermute | solution.py:42
  29.5 2.6 %collective-permute-start.8 = (f32[16,96,128]{2,1,0:T(8,128)S(1)}, f32[16,96,128]{2,1,0:T(8,128)S(1)}, u32[]{:S(2)}, u32[]{:S(2)}) collective-permute-start(f32[16,96,128]{2,1,0:T(8,128)S(1)} %constant_dynamic-update-slice_fusion.22.refs_4_), channel_id=1, source_target_pairs={{0,16},{16,0},{32,48},{48,32},{64,80},{80,64},{96,112},{112,96},{1... | collective-permute-start | bytes 2359304 | tf_op jit(solution)/shard_map/while/body/eval_jaxpr/ppermute | solution.py:42
  30.1 6.5 %collective-permute-start.6 = (f32[4,96,128]{2,1,0:T(8,128)S(1)}, f32[4,96,128]{2,1,0:T(8,128)S(1)}, u32[]{:S(2)}, u32[]{:S(2)}) collective-permute-start(f32[4,96,128]{2,1,0:T(8,128)S(1)} %constant_dynamic-update-slice_fusion.19.refs_4_), channel_id=1, source_target_pairs={{0,14},{1,15},{2,0},{3,1},{4,2},{5,3},{6,4},{7,5},{8,6},{9,7},{10,... | collective-permute-start | bytes 589832 | tf_op jit(solution)/shard_map/while/body/eval_jaxpr/ppermute | solution.py:42
  30.6 7.4 %collective-permute-start.7 = (f32[4,96,128]{2,1,0:T(8,128)S(1)}, f32[4,96,128]{2,1,0:T(8,128)S(1)}, u32[]{:S(2)}, u32[]{:S(2)}) collective-permute-start(f32[4,96,128]{2,1,0:T(8,128)S(1)} %constant_dynamic-update-slice_fusion.19.refs_4_), channel_id=1, source_target_pairs={{0,2},{1,3},{2,4},{3,5},{4,6},{5,7},{6,8},{7,9},{8,10},{9,11},{10,... | collective-permute-start | bytes 589832 | tf_op jit(solution)/shard_map/while/body/eval_jaxpr/ppermute | solution.py:42
  38.0 6.5 %collective-permute-start.10 = (f32[4,96,128]{2,1,0:T(8,128)S(1)}, f32[4,96,128]{2,1,0:T(8,128)S(1)}, u32[]{:S(2)}, u32[]{:S(2)}) collective-permute-start(f32[4,96,128]{2,1,0:T(8,128)S(1)} %collective-permute-done.7.refs_10_), channel_id=1, source_target_pairs={{0,2},{1,3},{2,4},{3,5},{4,6},{5,7},{6,8},{7,9},{8,10},{9,11},{10,... | collective-permute-start | bytes 589832 | tf_op jit(solution)/shard_map/while/body/eval_jaxpr/ppermute | solution.py:42
  38.0 6.5 %collective-permute-start.9 = (f32[4,96,128]{2,1,0:T(8,128)S(1)}, f32[4,96,128]{2,1,0:T(8,128)S(1)}, u32[]{:S(2)}, u32[]{:S(2)}) collective-permute-start(f32[4,96,128]{2,1,0:T(8,128)S(1)} %collective-permute-done.6.refs_5_), channel_id=1, source_target_pairs={{0,14},{1,15},{2,0},{3,1},{4,2},{5,3},{6,4},{7,5},{8,6},{9,7},{10,... | collective-permute-start | bytes 589832 | tf_op jit(solution)/shard_map/while/body/eval_jaxpr/ppermute | solution.py:42
  44.5 6.9 %collective-permute-start.12 = (f32[6,96,128]{2,1,0:T(8,128)S(1)}, f32[6,96,128]{2,1,0:T(8,128)S(1)}, u32[]{:S(2)}, u32[]{:S(2)}) collective-permute-start(f32[6,96,128]{2,1,0:T(8,128)S(1)} %pad_maximum_fusion.9), channel_id=1, source_target_pairs={{0,2},{1,3},{2,4},{3,5},{4,6},{5,7},{6,8},{7,9},{8,10},{9,11},{10,... | collective-permute-start | bytes 884744 | tf_op jit(solution)/shard_map/while/body/eval_jaxpr/ppermute | solution.py:42
  44.6 6.7 %collective-permute-start.11 = (f32[6,96,128]{2,1,0:T(8,128)S(1)}, f32[6,96,128]{2,1,0:T(8,128)S(1)}, u32[]{:S(2)}, u32[]{:S(2)}) collective-permute-start(f32[6,96,128]{2,1,0:T(8,128)S(1)} %pad_maximum_fusion.8), channel_id=1, source_target_pairs={{0,14},{1,15},{2,0},{3,1},{4,2},{5,3},{6,4},{7,5},{8,6},{9,7},{10,... | collective-permute-start | bytes 884744 | tf_op jit(solution)/shard_map/while/body/eval_jaxpr/ppermute | solution.py:42
  51.5 7.8 %collective-permute-start.14 = (f32[6,96,128]{2,1,0:T(8,128)S(1)}, f32[6,96,128]{2,1,0:T(8,128)S(1)}, u32[]{:S(2)}, u32[]{:S(2)}) collective-permute-start(f32[6,96,128]{2,1,0:T(8,128)S(1)} %pad_maximum_fusion.11), channel_id=1, source_target_pairs={{0,2},{1,3},{2,4},{3,5},{4,6},{5,7},{6,8},{7,9},{8,10},{9,11},{10,... | collective-permute-start | bytes 884744 | tf_op jit(solution)/shard_map/while/body/eval_jaxpr/ppermute | solution.py:42
  54.5 6.1 %collective-permute-start.13 = (f32[6,96,128]{2,1,0:T(8,128)S(1)}, f32[6,96,128]{2,1,0:T(8,128)S(1)}, u32[]{:S(2)}, u32[]{:S(2)}) collective-permute-start(f32[6,96,128]{2,1,0:T(8,128)S(1)} %pad_maximum_fusion.10), channel_id=1, source_target_pairs={{0,14},{1,15},{2,0},{3,1},{4,2},{5,3},{6,4},{7,5},{8,6},{9,7},{10,... | collective-permute-start | bytes 884744 | tf_op jit(solution)/shard_map/while/body/eval_jaxpr/ppermute | solution.py:42
  60.6 8.1 %collective-permute-start.16 = (f32[4,96,128]{2,1,0:T(8,128)S(1)}, f32[4,96,128]{2,1,0:T(8,128)S(1)}, u32[]{:S(2)}, u32[]{:S(2)}) collective-permute-start(f32[4,96,128]{2,1,0:T(8,128)S(1)} %slice_add_fusion.25), channel_id=1, source_target_pairs={{0,14},{1,15},{2,0},{3,1},{4,2},{5,3},{6,4},{7,5},{8,6},{9,7},{10,... | collective-permute-start | bytes 589832 | tf_op jit(solution)/shard_map/while/body/eval_jaxpr/ppermute | solution.py:42
  62.4 6.3 %collective-permute-start.15 = (f32[4,96,128]{2,1,0:T(8,128)S(1)}, f32[4,96,128]{2,1,0:T(8,128)S(1)}, u32[]{:S(2)}, u32[]{:S(2)}) collective-permute-start(f32[4,96,128]{2,1,0:T(8,128)S(1)} %slice_add_fusion.24), channel_id=1, source_target_pairs={{0,2},{1,3},{2,4},{3,5},{4,6},{5,7},{6,8},{7,9},{8,10},{9,11},{10,... | collective-permute-start | bytes 589832 | tf_op jit(solution)/shard_map/while/body/eval_jaxpr/ppermute | solution.py:42
  68.8 12.5 %collective-permute-start.17 = (f32[16,96,128]{2,1,0:T(8,128)S(1)}, f32[16,96,128]{2,1,0:T(8,128)S(1)}, u32[]{:S(2)}, u32[]{:S(2)}) collective-permute-start(f32[16,96,128]{2,1,0:T(8,128)S(1)} %get-tuple-element.650), channel_id=1, source_target_pairs={{0,16},{16,0},{32,48},{48,32},{64,80},{80,64},{96,112},{112,96},{1... | collective-permute-start | bytes 2359304 | tf_op jit(solution)/shard_map/while/body/eval_jaxpr/ppermute | solution.py:42
  78.4 7.7 %collective-permute-start.23 = (f32[4,96,128]{2,1,0:T(8,128)S(1)}, f32[4,96,128]{2,1,0:T(8,128)S(1)}, u32[]{:S(2)}, u32[]{:S(2)}) collective-permute-start(f32[4,96,128]{2,1,0:T(8,128)S(1)} %add.331), channel_id=1, source_target_pairs={{0,2},{1,3},{2,4},{3,5},{4,6},{5,7},{6,8},{7,9},{8,10},{9,11},{10,... | collective-permute-start | bytes 589832 | tf_op jit(solution)/shard_map/while/body/eval_jaxpr/ppermute | solution.py:42
  78.5 7.6 %collective-permute-start.22 = (f32[4,96,128]{2,1,0:T(8,128)S(1)}, f32[4,96,128]{2,1,0:T(8,128)S(1)}, u32[]{:S(2)}, u32[]{:S(2)}) collective-permute-start(f32[4,96,128]{2,1,0:T(8,128)S(1)} %add.330), channel_id=1, source_target_pairs={{0,14},{1,15},{2,0},{3,1},{4,2},{5,3},{6,4},{7,5},{8,6},{9,7},{10,... | collective-permute-start | bytes 589832 | tf_op jit(solution)/shard_map/while/body/eval_jaxpr/ppermute | solution.py:42
  81.3 15.0 %collective-permute-start.18 = (f32[4,96,128]{2,1,0:T(8,128)S(1)}, f32[4,96,128]{2,1,0:T(8,128)S(1)}, u32[]{:S(2)}, u32[]{:S(2)}) collective-permute-start(f32[4,96,128]{2,1,0:T(8,128)S(1)} %get-tuple-element.653), channel_id=1, source_target_pairs={{0,96},{16,112},{32,0},{48,16},{64,32},{80,48},{96,64},{112,80},{1... | collective-permute-start | bytes 589832 | tf_op jit(solution)/shard_map/while/body/eval_jaxpr/ppermute | solution.py:42
  85.3 11.0 %collective-permute-start.19 = (f32[4,96,128]{2,1,0:T(8,128)S(1)}, f32[4,96,128]{2,1,0:T(8,128)S(1)}, u32[]{:S(2)}, u32[]{:S(2)}) collective-permute-start(f32[4,96,128]{2,1,0:T(8,128)S(1)} %get-tuple-element.654), channel_id=1, source_target_pairs={{0,64},{16,80},{32,96},{48,112},{64,0},{80,16},{96,32},{112,48},{1... | collective-permute-start | bytes 589832 | tf_op jit(solution)/shard_map/while/body/eval_jaxpr/ppermute | solution.py:42
  85.3 12.0 %collective-permute-start.20 = (f32[4,96,128]{2,1,0:T(8,128)S(1)}, f32[4,96,128]{2,1,0:T(8,128)S(1)}, u32[]{:S(2)}, u32[]{:S(2)}) collective-permute-start(f32[4,96,128]{2,1,0:T(8,128)S(1)} %get-tuple-element.655), channel_id=1, source_target_pairs={{0,32},{16,48},{32,64},{48,80},{64,96},{80,112},{96,0},{112,16},{1... | collective-permute-start | bytes 589832 | tf_op jit(solution)/shard_map/while/body/eval_jaxpr/ppermute | solution.py:42
  86.2 3.6 %collective-permute-start.24 = (f32[2,96,128]{2,1,0:T(8,128)S(1)}, f32[2,96,128]{2,1,0:T(8,128)S(1)}, u32[]{:S(2)}, u32[]{:S(2)}) collective-permute-start(f32[2,96,128]{2,1,0:T(8,128)S(1)} %get-tuple-element.665), channel_id=1, source_target_pairs={{0,1},{1,0},{2,3},{3,2},{4,5},{5,4},{6,7},{7,6},{8,9},{9,8},{10,11... | collective-permute-start | bytes 294920 | tf_op jit(solution)/shard_map/while/body/eval_jaxpr/ppermute | solution.py:42
  89.7 21.4 %collective-permute-start.25 = (f32[2,96,128]{2,1,0:T(8,128)S(1)}, f32[2,96,128]{2,1,0:T(8,128)S(1)}, u32[]{:S(2)}, u32[]{:S(2)}) collective-permute-start(f32[2,96,128]{2,1,0:T(8,128)S(1)} %add.332), channel_id=1, source_target_pairs={{0,0},{1,16},{2,32},{3,48},{4,64},{5,80},{6,96},{7,112},{8,128},{9... | collective-permute-start | bytes 294920 | tf_op jit(solution)/shard_map/while/body/eval_jaxpr/ppermute | solution.py:46
  97.3 13.9 %collective-permute-start.21 = (f32[2,96,128]{2,1,0:T(8,128)S(1)}, f32[2,96,128]{2,1,0:T(8,128)S(1)}, u32[]{:S(2)}, u32[]{:S(2)}) collective-permute-start(f32[2,96,128]{2,1,0:T(8,128)S(1)} %slice_add_fusion.27), channel_id=1, source_target_pairs={{0,128},{16,144},{32,160},{48,176},{64,192},{80,208},{96,224},{112... | collective-permute-start | bytes 294920 | tf_op jit(solution)/shard_map/while/body/eval_jaxpr/ppermute | solution.py:42
  111.3 26.9 %copy-start = (s32[1,1,176]{2,1,0:T(1,128)S(1)}, s32[1,1,176]{2,1,0:T(1,128)}, u32[]{:S(2)}) copy-start(s32[1,1,176]{2,1,0:T(1,128)} %get-tuple-element.702.refs_0_) | copy-start | bytes 2116 | tf_op jit(solution)/shard_map/while
  111.3 26.9 %copy-start.1 = (s32[1,1,176]{2,1,0:T(1,128)S(1)}, s32[1,1,176]{2,1,0:T(1,128)}, u32[]{:S(2)}) copy-start(s32[1,1,176]{2,1,0:T(1,128)} %get-tuple-element.703.refs_1_) | copy-start | bytes 2116 | tf_op jit(solution)/shard_map/while
  111.3 6.8 %collective-permute-start = (f32[2,96,128]{2,1,0:T(8,128)S(1)}, f32[2,96,128]{2,1,0:T(8,128)S(1)}, u32[]{:S(2)}, u32[]{:S(2)}) collective-permute-start(f32[2,96,128]{2,1,0:T(8,128)S(1)} %copy.29), channel_id=1, source_target_pairs={{0,128},{16,144},{32,160},{48,176},{64,192},{80,208},{96,224},{112... | collective-permute-start | bytes 294920 | tf_op jit(solution)/shard_map/while/body/eval_jaxpr/ppermute | solution.py:42
  111.4 13.6 %collective-permute-start.4 = (f32[2,96,128]{2,1,0:T(8,128)S(1)}, f32[2,96,128]{2,1,0:T(8,128)S(1)}, u32[]{:S(2)}, u32[]{:S(2)}) collective-permute-start(f32[2,96,128]{2,1,0:T(8,128)S(1)} %get-tuple-element.684), channel_id=1, source_target_pairs={{0,0},{1,16},{2,32},{3,48},{4,64},{5,80},{6,96},{7,112},{8,128},{9... | collective-permute-start | bytes 294920 | tf_op jit(solution)/shard_map/while/body/eval_jaxpr/ppermute | solution.py:46
  118.1 10.4 %collective-permute-start.1 = (f32[4,96,128]{2,1,0:T(8,128)S(1)}, f32[4,96,128]{2,1,0:T(8,128)S(1)}, u32[]{:S(2)}, u32[]{:S(2)}) collective-permute-start(f32[4,96,128]{2,1,0:T(8,128)S(1)} %get-tuple-element.601), channel_id=1, source_target_pairs={{0,96},{16,112},{32,0},{48,16},{64,32},{80,48},{96,64},{112,80},{1... | collective-permute-start | bytes 589832 | tf_op jit(solution)/shard_map/while/body/eval_jaxpr/ppermute | solution.py:42
  119.9 8.7 %collective-permute-start.2 = (f32[4,96,128]{2,1,0:T(8,128)S(1)}, f32[4,96,128]{2,1,0:T(8,128)S(1)}, u32[]{:S(2)}, u32[]{:S(2)}) collective-permute-start(f32[4,96,128]{2,1,0:T(8,128)S(1)} %get-tuple-element.601), channel_id=1, source_target_pairs={{0,64},{16,80},{32,96},{48,112},{64,0},{80,16},{96,32},{112,48},{1... | collective-permute-start | bytes 589832 | tf_op jit(solution)/shard_map/while/body/eval_jaxpr/ppermute | solution.py:42
  119.9 8.7 %collective-permute-start.3 = (f32[4,96,128]{2,1,0:T(8,128)S(1)}, f32[4,96,128]{2,1,0:T(8,128)S(1)}, u32[]{:S(2)}, u32[]{:S(2)}) collective-permute-start(f32[4,96,128]{2,1,0:T(8,128)S(1)} %get-tuple-element.601), channel_id=1, source_target_pairs={{0,32},{16,48},{32,64},{48,80},{64,96},{80,112},{96,0},{112,16},{1... | collective-permute-start | bytes 589832 | tf_op jit(solution)/shard_map/while/body/eval_jaxpr/ppermute | solution.py:42
  125.0 3.6 %collective-permute-start.5 = (f32[2,96,128]{2,1,0:T(8,128)S(1)}, f32[2,96,128]{2,1,0:T(8,128)S(1)}, u32[]{:S(2)}, u32[]{:S(2)}) collective-permute-start(f32[2,96,128]{2,1,0:T(8,128)S(1)} %multiply_add_fusion.2), channel_id=1, source_target_pairs={{0,1},{1,0},{2,3},{3,2},{4,5},{5,4},{6,7},{7,6},{8,9},{9,8},{10,11... | collective-permute-start | bytes 294920 | tf_op jit(solution)/shard_map/while/body/eval_jaxpr/ppermute | solution.py:42
  128.7 9.5 %collective-permute-start.8 = (f32[16,96,128]{2,1,0:T(8,128)S(1)}, f32[16,96,128]{2,1,0:T(8,128)S(1)}, u32[]{:S(2)}, u32[]{:S(2)}) collective-permute-start(f32[16,96,128]{2,1,0:T(8,128)S(1)} %constant_dynamic-update-slice_fusion.22.refs_4_), channel_id=1, source_target_pairs={{0,16},{16,0},{32,48},{48,32},{64,80},{80,64},{96,112},{112,96},{1... | collective-permute-start | bytes 2359304 | tf_op jit(solution)/shard_map/while/body/eval_jaxpr/ppermute | solution.py:42
  136.2 6.5 %collective-permute-start.6 = (f32[4,96,128]{2,1,0:T(8,128)S(1)}, f32[4,96,128]{2,1,0:T(8,128)S(1)}, u32[]{:S(2)}, u32[]{:S(2)}) collective-permute-start(f32[4,96,128]{2,1,0:T(8,128)S(1)} %constant_dynamic-update-slice_fusion.19.refs_4_), channel_id=1, source_target_pairs={{0,14},{1,15},{2,0},{3,1},{4,2},{5,3},{6,4},{7,5},{8,6},{9,7},{10,... | collective-permute-start | bytes 589832 | tf_op jit(solution)/shard_map/while/body/eval_jaxpr/ppermute | solution.py:42
  136.3 7.7 %collective-permute-start.7 = (f32[4,96,128]{2,1,0:T(8,128)S(1)}, f32[4,96,128]{2,1,0:T(8,128)S(1)}, u32[]{:S(2)}, u32[]{:S(2)}) collective-permute-start(f32[4,96,128]{2,1,0:T(8,128)S(1)} %constant_dynamic-update-slice_fusion.19.refs_4_), channel_id=1, source_target_pairs={{0,2},{1,3},{2,4},{3,5},{4,6},{5,7},{6,8},{7,9},{8,10},{9,11},{10,... | collective-permute-start | bytes 589832 | tf_op jit(solution)/shard_map/while/body/eval_jaxpr/ppermute | solution.py:42
  144.1 6.8 %collective-permute-start.10 = (f32[4,96,128]{2,1,0:T(8,128)S(1)}, f32[4,96,128]{2,1,0:T(8,128)S(1)}, u32[]{:S(2)}, u32[]{:S(2)}) collective-permute-start(f32[4,96,128]{2,1,0:T(8,128)S(1)} %collective-permute-done.7.refs_10_), channel_id=1, source_target_pairs={{0,2},{1,3},{2,4},{3,5},{4,6},{5,7},{6,8},{7,9},{8,10},{9,11},{10,... | collective-permute-start | bytes 589832 | tf_op jit(solution)/shard_map/while/body/eval_jaxpr/ppermute | solution.py:42
  145.2 5.7 %collective-permute-start.9 = (f32[4,96,128]{2,1,0:T(8,128)S(1)}, f32[4,96,128]{2,1,0:T(8,128)S(1)}, u32[]{:S(2)}, u32[]{:S(2)}) collective-permute-start(f32[4,96,128]{2,1,0:T(8,128)S(1)} %collective-permute-done.6.refs_5_), channel_id=1, source_target_pairs={{0,14},{1,15},{2,0},{3,1},{4,2},{5,3},{6,4},{7,5},{8,6},{9,7},{10,... | collective-permute-start | bytes 589832 | tf_op jit(solution)/shard_map/while/body/eval_jaxpr/ppermute | solution.py:42
  150.9 6.9 %collective-permute-start.12 = (f32[6,96,128]{2,1,0:T(8,128)S(1)}, f32[6,96,128]{2,1,0:T(8,128)S(1)}, u32[]{:S(2)}, u32[]{:S(2)}) collective-permute-start(f32[6,96,128]{2,1,0:T(8,128)S(1)} %pad_maximum_fusion.9), channel_id=1, source_target_pairs={{0,2},{1,3},{2,4},{3,5},{4,6},{5,7},{6,8},{7,9},{8,10},{9,11},{10,... | collective-permute-start | bytes 884744 | tf_op jit(solution)/shard_map/while/body/eval_jaxpr/ppermute | solution.py:42
  151.7 6.0 %collective-permute-start.11 = (f32[6,96,128]{2,1,0:T(8,128)S(1)}, f32[6,96,128]{2,1,0:T(8,128)S(1)}, u32[]{:S(2)}, u32[]{:S(2)}) collective-permute-start(f32[6,96,128]{2,1,0:T(8,128)S(1)} %pad_maximum_fusion.8), channel_id=1, source_target_pairs={{0,14},{1,15},{2,0},{3,1},{4,2},{5,3},{6,4},{7,5},{8,6},{9,7},{10,... | collective-permute-start | bytes 884744 | tf_op jit(solution)/shard_map/while/body/eval_jaxpr/ppermute | solution.py:42
  157.8 7.2 %collective-permute-start.14 = (f32[6,96,128]{2,1,0:T(8,128)S(1)}, f32[6,96,128]{2,1,0:T(8,128)S(1)}, u32[]{:S(2)}, u32[]{:S(2)}) collective-permute-start(f32[6,96,128]{2,1,0:T(8,128)S(1)} %pad_maximum_fusion.11), channel_id=1, source_target_pairs={{0,2},{1,3},{2,4},{3,5},{4,6},{5,7},{6,8},{7,9},{8,10},{9,11},{10,... | collective-permute-start | bytes 884744 | tf_op jit(solution)/shard_map/while/body/eval_jaxpr/ppermute | solution.py:42
  160.3 6.2 %collective-permute-start.13 = (f32[6,96,128]{2,1,0:T(8,128)S(1)}, f32[6,96,128]{2,1,0:T(8,128)S(1)}, u32[]{:S(2)}, u32[]{:S(2)}) collective-permute-start(f32[6,96,128]{2,1,0:T(8,128)S(1)} %pad_maximum_fusion.10), channel_id=1, source_target_pairs={{0,14},{1,15},{2,0},{3,1},{4,2},{5,3},{6,4},{7,5},{8,6},{9,7},{10,... | collective-permute-start | bytes 884744 | tf_op jit(solution)/shard_map/while/body/eval_jaxpr/ppermute | solution.py:42
  166.5 8.7 %collective-permute-start.16 = (f32[4,96,128]{2,1,0:T(8,128)S(1)}, f32[4,96,128]{2,1,0:T(8,128)S(1)}, u32[]{:S(2)}, u32[]{:S(2)}) collective-permute-start(f32[4,96,128]{2,1,0:T(8,128)S(1)} %slice_add_fusion.25), channel_id=1, source_target_pairs={{0,14},{1,15},{2,0},{3,1},{4,2},{5,3},{6,4},{7,5},{8,6},{9,7},{10,... | collective-permute-start | bytes 589832 | tf_op jit(solution)/shard_map/while/body/eval_jaxpr/ppermute | solution.py:42
  168.2 7.0 %collective-permute-start.15 = (f32[4,96,128]{2,1,0:T(8,128)S(1)}, f32[4,96,128]{2,1,0:T(8,128)S(1)}, u32[]{:S(2)}, u32[]{:S(2)}) collective-permute-start(f32[4,96,128]{2,1,0:T(8,128)S(1)} %slice_add_fusion.24), channel_id=1, source_target_pairs={{0,2},{1,3},{2,4},{3,5},{4,6},{5,7},{6,8},{7,9},{8,10},{9,11},{10,... | collective-permute-start | bytes 589832 | tf_op jit(solution)/shard_map/while/body/eval_jaxpr/ppermute | solution.py:42
  175.2 11.2 %collective-permute-start.17 = (f32[16,96,128]{2,1,0:T(8,128)S(1)}, f32[16,96,128]{2,1,0:T(8,128)S(1)}, u32[]{:S(2)}, u32[]{:S(2)}) collective-permute-start(f32[16,96,128]{2,1,0:T(8,128)S(1)} %get-tuple-element.650), channel_id=1, source_target_pairs={{0,16},{16,0},{32,48},{48,32},{64,80},{80,64},{96,112},{112,96},{1... | collective-permute-start | bytes 2359304 | tf_op jit(solution)/shard_map/while/body/eval_jaxpr/ppermute | solution.py:42
  183.5 7.7 %collective-permute-start.23 = (f32[4,96,128]{2,1,0:T(8,128)S(1)}, f32[4,96,128]{2,1,0:T(8,128)S(1)}, u32[]{:S(2)}, u32[]{:S(2)}) collective-permute-start(f32[4,96,128]{2,1,0:T(8,128)S(1)} %add.331), channel_id=1, source_target_pairs={{0,2},{1,3},{2,4},{3,5},{4,6},{5,7},{6,8},{7,9},{8,10},{9,11},{10,... | collective-permute-start | bytes 589832 | tf_op jit(solution)/shard_map/while/body/eval_jaxpr/ppermute | solution.py:42
  183.6 7.6 %collective-permute-start.22 = (f32[4,96,128]{2,1,0:T(8,128)S(1)}, f32[4,96,128]{2,1,0:T(8,128)S(1)}, u32[]{:S(2)}, u32[]{:S(2)}) collective-permute-start(f32[4,96,128]{2,1,0:T(8,128)S(1)} %add.330), channel_id=1, source_target_pairs={{0,14},{1,15},{2,0},{3,1},{4,2},{5,3},{6,4},{7,5},{8,6},{9,7},{10,... | collective-permute-start | bytes 589832 | tf_op jit(solution)/shard_map/while/body/eval_jaxpr/ppermute | solution.py:42
  186.5 15.2 %collective-permute-start.18 = (f32[4,96,128]{2,1,0:T(8,128)S(1)}, f32[4,96,128]{2,1,0:T(8,128)S(1)}, u32[]{:S(2)}, u32[]{:S(2)}) collective-permute-start(f32[4,96,128]{2,1,0:T(8,128)S(1)} %get-tuple-element.653), channel_id=1, source_target_pairs={{0,96},{16,112},{32,0},{48,16},{64,32},{80,48},{96,64},{112,80},{1... | collective-permute-start | bytes 589832 | tf_op jit(solution)/shard_map/while/body/eval_jaxpr/ppermute | solution.py:42
  188.2 13.5 %collective-permute-start.19 = (f32[4,96,128]{2,1,0:T(8,128)S(1)}, f32[4,96,128]{2,1,0:T(8,128)S(1)}, u32[]{:S(2)}, u32[]{:S(2)}) collective-permute-start(f32[4,96,128]{2,1,0:T(8,128)S(1)} %get-tuple-element.654), channel_id=1, source_target_pairs={{0,64},{16,80},{32,96},{48,112},{64,0},{80,16},{96,32},{112,48},{1... | collective-permute-start | bytes 589832 | tf_op jit(solution)/shard_map/while/body/eval_jaxpr/ppermute | solution.py:42
  188.2 13.5 %collective-permute-start.20 = (f32[4,96,128]{2,1,0:T(8,128)S(1)}, f32[4,96,128]{2,1,0:T(8,128)S(1)}, u32[]{:S(2)}, u32[]{:S(2)}) collective-permute-start(f32[4,96,128]{2,1,0:T(8,128)S(1)} %get-tuple-element.655), channel_id=1, source_target_pairs={{0,32},{16,48},{32,64},{48,80},{64,96},{80,112},{96,0},{112,16},{1... | collective-permute-start | bytes 589832 | tf_op jit(solution)/shard_map/while/body/eval_jaxpr/ppermute | solution.py:42
  191.3 3.8 %collective-permute-start.24 = (f32[2,96,128]{2,1,0:T(8,128)S(1)}, f32[2,96,128]{2,1,0:T(8,128)S(1)}, u32[]{:S(2)}, u32[]{:S(2)}) collective-permute-start(f32[2,96,128]{2,1,0:T(8,128)S(1)} %get-tuple-element.665), channel_id=1, source_target_pairs={{0,1},{1,0},{2,3},{3,2},{4,5},{5,4},{6,7},{7,6},{8,9},{9,8},{10,11... | collective-permute-start | bytes 294920 | tf_op jit(solution)/shard_map/while/body/eval_jaxpr/ppermute | solution.py:42
  195.2 20.5 %collective-permute-start.25 = (f32[2,96,128]{2,1,0:T(8,128)S(1)}, f32[2,96,128]{2,1,0:T(8,128)S(1)}, u32[]{:S(2)}, u32[]{:S(2)}) collective-permute-start(f32[2,96,128]{2,1,0:T(8,128)S(1)} %add.332), channel_id=1, source_target_pairs={{0,0},{1,16},{2,32},{3,48},{4,64},{5,80},{6,96},{7,112},{8,128},{9... | collective-permute-start | bytes 294920 | tf_op jit(solution)/shard_map/while/body/eval_jaxpr/ppermute | solution.py:46
  201.7 13.9 %collective-permute-start.21 = (f32[2,96,128]{2,1,0:T(8,128)S(1)}, f32[2,96,128]{2,1,0:T(8,128)S(1)}, u32[]{:S(2)}, u32[]{:S(2)}) collective-permute-start(f32[2,96,128]{2,1,0:T(8,128)S(1)} %slice_add_fusion.27), channel_id=1, source_target_pairs={{0,128},{16,144},{32,160},{48,176},{64,192},{80,208},{96,224},{112... | collective-permute-start | bytes 294920 | tf_op jit(solution)/shard_map/while/body/eval_jaxpr/ppermute | solution.py:42
